TPU v7x, 128 devices: a whole 4x4x4 slice. The times are simulated.
128 devices in a mesh: node: 32 (over x, y, core), local: 4 (over z).
Axes of the slice: x: 4, y: 4, z: 4, core: 2. Of those that a mesh axis runs over, the one named last changes fastest.
Arguments:
- tokens: bfloat16 [16384, 2048], P(('node', 'local')), may hold values from -6 to 6
- route: int32 [16384, 4], P(('node', 'local')), may hold values from 0 to 63, all different within a row; in each aligned block of 128 rows (0 to 127, 128 to 255, ...) at most 9 rows name the same one
- combine_weights: float32 [16384, 4], P(('node', 'local')), may hold values from 0.05 to 1
- w_gate: bfloat16 [64, 2048, 1408], P('node', None, 'local'), may hold values from -0.125 to 0.125
- w_up: bfloat16 [64, 2048, 1408], P('node', None, 'local'), may hold values from -0.125 to 0.125
- w_down: bfloat16 [64, 1408, 2048], P('node', 'local'), may hold values from -0.15625 to 0.15625
- grad_out: bfloat16 [16384, 2048], P(('node', 'local')), may hold values from -6 to 6
Outputs:
- combined: bfloat16 [16384, 2048], P(('node', 'local'))
- d_tokens: bfloat16 [16384, 2048], P(('node', 'local'))
- d_weights: float32 [16384, 4], P(('node', 'local'))
Inputs may be any that keep to these rules, and one draw needn't show every extreme that they name: `route`: the 4 experts of one token differ; within the 128 tokens of one device no expert is named more than 9 times, and some device names some expert exactly 9 times.
All inputs are finite; a program needn't handle non-finite values.
Results may differ from a plain program's by a relative error of at most 0.012.
Values may be sent and summed in bfloat16 or wider, within the bound.
No kernel may reach another device: no remote copies, remote signals or barrier semaphores. Data moves between devices by JAX's collectives and lax.ppermute only.
A program may use at most 192 MiB of HBM per device.

v0:
```python
import functools

import jax
import jax.numpy as jnp
from jax import lax
from jax.experimental import pallas as pl
from jax.experimental.pallas import tpu as pltpu
from jax.sharding import PartitionSpec as P

EXPERTS = 64
TOP = 4
CAP = 9
BF = jnp.bfloat16
F32 = jnp.float32

IN_ROWS = 56
OUT0_ROWS = 40
OUT1_ROWS = 24


def slots_of(route_t):
    toks = route_t.shape[1]
    expert_ids = jnp.arange(EXPERTS, dtype=jnp.int32)[:, None]
    hits = [(route_t[k][None, :] == expert_ids) for k in range(TOP)]
    named = sum(h.astype(BF) for h in hits)
    before = (
        jnp.arange(toks, dtype=jnp.int32)[:, None] < jnp.arange(toks, dtype=jnp.int32)[None, :]
    ).astype(BF)
    earlier = jnp.dot(named, before, preferred_element_type=F32)
    slots = [jnp.sum(jnp.where(h, earlier, 0.0), axis=0) for h in hits]
    return jnp.stack(slots).astype(jnp.int32)


def one_hot_rows(row_t, rows):
    ids = jnp.arange(rows, dtype=jnp.int32)[:, None]
    total = 0
    for k in range(TOP):
        total = total + jnp.where(row_t[k][None, :] == ids, 1.0, 0.0)
    return total.astype(BF)


def expert_kernel(
    nodes, main, extra, in_rows, out_rows, x_at, g_at, rest_at, x_rest, g_rest, blocks, n_pieces, *refs
):
    arrived, pieces, home = refs[0], refs[1 : 1 + n_pieces], refs[1 + n_pieces]
    xs, gs, rest, wg, wu, wd, outs, backs, out_rest, sems = refs[2 + n_pieces :]
    spread = nodes * 8
    count = nodes * main
    part = pieces[0].shape[1]

    def fetch(first, size, dst, sem):
        def step(n, carry):
            src = arrived.at[pl.ds(pl.multiple_of(n * in_rows + first, 8), size)]
            to = dst.at[pl.ds(pl.multiple_of(n * size, 8), size)]
            pltpu.make_async_copy(src, to, sem).start()
            return carry

        lax.fori_loop(0, nodes, step, 0)

    def landed(dst, sem):
        pltpu.make_async_copy(dst, dst, sem).wait()

    fetch(x_at, main, xs, sems.at[0])
    fetch(rest_at, 8, rest, sems.at[1])
    for j, w in enumerate((wg, wu, wd)):
        for i, p in enumerate(pieces):
            pltpu.make_async_copy(p.at[j], w.at[pl.ds(i * part, part)], sems.at[3 + j]).start()
        if j == 1:
            fetch(g_at, main, gs, sems.at[2])

    small = nodes * extra

    def picked(offset, out_major):
        shape = (small, spread) if not out_major else (spread, small)
        compact = lax.broadcasted_iota(jnp.int32, shape, 1 if out_major else 0)
        wide = lax.broadcasted_iota(jnp.int32, shape, 0 if out_major else 1)
        want = (compact // extra) * 8 + offset + compact % extra
        return (want == wide).astype(F32).astype(BF)

    landed(rest, sems.at[1])
    landed(xs.at[pl.ds(0, count)], sems.at[0])
    xs[pl.ds(count, small)] = jnp.dot(picked(x_rest, False), rest[...], preferred_element_type=F32).astype(BF)
    gs[pl.ds(count, small)] = jnp.dot(picked(g_rest, False), rest[...], preferred_element_type=F32).astype(BF)
    landed(wg, sems.at[3])
    landed(wu, sems.at[4])
    landed(gs.at[pl.ds(0, count)], sems.at[2])
    landed(wd, sems.at[5])

    size = (count + small) // blocks

    def by_hidden(rows, w):
        return lax.dot_general(rows, w, (((1,), (1,)), ((), ())), preferred_element_type=F32)

    def block(b, carry):
        at = pl.ds(pl.multiple_of(b * size, 16), size)
        x = xs[at]
        gate = by_hidden(x, wg[...])
        upper = by_hidden(x, wu[...])
        d_hidden = by_hidden(gs[at], wd[...])
        s = jax.nn.sigmoid(gate)
        act = gate * s
        hidden = (act * upper).astype(BF)
        d_gate = (d_hidden * upper * s * (1.0 + gate * (1.0 - s))).astype(BF)
        d_up = (d_hidden * act).astype(BF)
        outs[at] = jnp.dot(hidden, wd[...], preferred_element_type=F32).astype(BF)
        backs[at] = (
            jnp.dot(d_gate, wg[...], preferred_element_type=F32)
            + jnp.dot(d_up, wu[...], preferred_element_type=F32)
        ).astype(BF)
        return carry

    lax.fori_loop(0, blocks, block, 0)
    out_rest[...] = (
        jnp.dot(picked(0, True), outs[pl.ds(count, small)], preferred_element_type=F32)
        + jnp.dot(picked(extra, True), backs[pl.ds(count, small)], preferred_element_type=F32)
    ).astype(BF)

    def put(src, size, first, sem):
        def step(n, carry):
            frm = src.at[pl.ds(pl.multiple_of(n * size, 8), size)]
            to = home.at[pl.ds(pl.multiple_of(n * out_rows + first, 8), size)]
            pltpu.make_async_copy(frm, to, sem).start()
            return carry

        lax.fori_loop(0, nodes, step, 0)

    put(outs, main, 0, sems.at[0])
    put(backs, main, main, sems.at[1])
    put(out_rest, 8, 2 * main, sems.at[2])
    landed(outs.at[pl.ds(0, count)], sems.at[0])
    landed(backs.at[pl.ds(0, count)], sems.at[1])
    landed(out_rest, sems.at[2])


def expert(arrived, pieces, nodes, main, extra, in_rows, x_at, g_at, rest_at, x_rest, g_rest, blocks):
    width = arrived.shape[1]
    rows = nodes * (main + extra)
    hidden = len(pieces) * pieces[0].shape[1]
    out_rows = 2 * main + 8
    body = functools.partial(
        expert_kernel, nodes, main, extra, in_rows, out_rows, x_at, g_at, rest_at, x_rest, g_rest, blocks, len(pieces)
    )
    any_spec = pl.BlockSpec(memory_space=pl.ANY)
    return pl.pallas_call(
        body,
        out_shape=jax.ShapeDtypeStruct((nodes * out_rows, width), BF),
        in_specs=[any_spec] * (1 + len(pieces)),
        out_specs=any_spec,
        scratch_shapes=[
            pltpu.VMEM((rows, width), BF),
            pltpu.VMEM((rows, width), BF),
            pltpu.VMEM((nodes * 8, width), BF),
            pltpu.VMEM((hidden, width), BF),
            pltpu.VMEM((hidden, width), BF),
            pltpu.VMEM((hidden, width), BF),
            pltpu.VMEM((rows, width), BF),
            pltpu.VMEM((rows, width), BF),
            pltpu.VMEM((nodes * 8, width), BF),
            pltpu.SemaphoreType.DMA((6,)),
        ],
        compiler_params=pltpu.CompilerParams(vmem_limit_bytes=60 * 1024 * 1024),
        cost_estimate=pl.CostEstimate(
            flops=12 * rows * hidden * width,
            transcendentals=rows * hidden,
            bytes_accessed=2 * width * (4 * rows + 3 * hidden),
        ),
    )(arrived, *pieces)


def mixed(rows_ref, places, first, values, ids):
    total = 0.0
    for k in range(TOP):
        total = total + jnp.where(places[:, first + k : first + k + 1] == ids, values[:, k : k + 1], 0.0)
    return jnp.dot(total.astype(BF), rows_ref[...], preferred_element_type=F32)


def weight_grads(rows_ref, grads, places, first, ids):
    table = lax.dot_general(grads, rows_ref[...], (((1,), (1,)), ((), ())), preferred_element_type=F32)
    return jnp.concatenate(
        [
            jnp.sum(jnp.where(places[:, first + k : first + k + 1] == ids, table, 0.0), axis=1, keepdims=True)
            for k in range(TOP)
        ],
        axis=1,
    )


def combine_pair_kernel(home, places_ref, values_ref, grads, grads_other, back, own, dw_other, dw_own):
    toks = grads.shape[0]
    ids = lax.broadcasted_iota(jnp.int32, (toks, home.shape[0]), 1)
    places = places_ref[...]
    values, values_other = values_ref[:, :TOP], values_ref[:, TOP:]
    back[:toks] = mixed(home, places, 2 * TOP, values_other, ids).astype(BF)
    back[toks:] = mixed(home, places, 3 * TOP, values_other, ids).astype(BF)
    dw_other[...] = weight_grads(home, grads_other[...], places, 2 * TOP, ids)
    own[:toks] = mixed(home, places, 0, values, ids)
    own[toks:] = mixed(home, places, TOP, values, ids)
    dw_own[...] = weight_grads(home, grads[...], places, 0, ids)


def combine_full_kernel(home, places_ref, values_ref, grads, own, returned, dw_own, dw_back, combined, d_tokens, d_weights):
    toks = grads.shape[0]
    ids = lax.broadcasted_iota(jnp.int32, (toks, home.shape[0]), 1)
    places = places_ref[...]
    values = values_ref[:, :TOP]
    combined[...] = (
        mixed(home, places, 0, values, ids) + own[:toks] + returned[:toks].astype(F32)
    ).astype(BF)
    d_tokens[...] = (
        mixed(home, places, TOP, values, ids) + own[toks:] + returned[toks:].astype(F32)
    ).astype(BF)
    d_weights[...] = weight_grads(home, grads[...], places, 0, ids) + dw_own[...] + dw_back[...]


def combine_pair(home, places, values, grads, other):
    toks, width = grads.shape
    whole = pl.BlockSpec(memory_space=pltpu.VMEM)
    return pl.pallas_call(
        combine_pair_kernel,
        name="combine_pair",
        grid=(1,),
        out_shape=(
            jax.ShapeDtypeStruct((2 * toks, width), BF),
            jax.ShapeDtypeStruct((2 * toks, width), F32),
            jax.ShapeDtypeStruct((toks, TOP), F32),
            jax.ShapeDtypeStruct((toks, TOP), F32),
        ),
        in_specs=[whole] * 4 + [pl.BlockSpec((toks, width), lambda i: (1, 0))],
        out_specs=(whole,) * 4,
        cost_estimate=pl.CostEstimate(
            flops=12 * toks * home.shape[0] * width, transcendentals=0, bytes_accessed=12 * 1024 * 1024
        ),
    )(home, places, values, grads, other)


def combine_full(home, places, values, grads, own, returned, dw_own, dw_back):
    toks, width = grads.shape
    return pl.pallas_call(
        combine_full_kernel,
        name="combine_full",
        out_shape=(
            jax.ShapeDtypeStruct((toks, width), BF),
            jax.ShapeDtypeStruct((toks, width), BF),
            jax.ShapeDtypeStruct((toks, TOP), F32),
        ),
        cost_estimate=pl.CostEstimate(
            flops=6 * toks * home.shape[0] * width, transcendentals=0, bytes_accessed=8 * 1024 * 1024
        ),
    )(home, places, values, grads, own, returned, dw_own, dw_back)


def shards(tokens, route, combine_weights, w_gate, w_up, w_down, grad_out):
    nodes = lax.axis_size("node")
    planes = lax.axis_size("local")
    up = [(i, (i + 1) % planes) for i in range(planes)]
    down = [(i, (i - 1) % planes) for i in range(planes)]
    across = [(i, (i + 2) % planes) for i in range(planes)]

    def send(value, pairs):
        return lax.ppermute(value, "local", pairs)

    def exchange(rows):
        return lax.all_to_all(rows, "node", split_axis=0, concat_axis=0, tiled=True)

    own = jnp.concatenate([tokens, grad_out], axis=0)
    other = send(own, across)
    route_t = route.T
    weight_t = combine_weights.T
    small = send(jnp.concatenate([weight_t, route_t.astype(F32)], axis=0), across)
    weight_other = small[:TOP]
    route_other = small[TOP:].astype(jnp.int32)

    gate_t = jnp.swapaxes(w_gate, 1, 2)
    up_t = jnp.swapaxes(w_up, 1, 2)
    half = gate_t.shape[1] // 2

    def piece(expert, part):
        cut = slice(part * half, (part + 1) * half)
        return jnp.stack([gate_t[expert, cut], up_t[expert, cut], w_down[expert, cut]])

    p0a, p0b, p1a, p1b = piece(0, 0), piece(0, 1), piece(1, 0), piece(1, 1)
    w0 = [p0a, p0b, send(p0a, down), send(p0b, up)]
    below_a, above_b = send(p1a, up), send(p1b, down)
    below_b, above_a = send(p1b, up), send(p1a, down)
    far_a, far_b = send(below_a, up), send(above_b, down)
    w1 = [p1a, p1b, below_a, below_b, above_a, above_b, far_a, far_b]

    slot_own, slot_other = slots_of(route_t), slots_of(route_other)

    def places(route_rows, index, odd, chunk, main, first, rest):
        row = jnp.where(index < main, first + index, rest + index - main)
        return jnp.where(route_rows % 2 == odd, (route_rows // 2) * chunk + row, -1)

    def pair_places(route_rows, index, chunk, first, rest):
        return places(route_rows, index, 0, chunk, 16, first, rest)

    def full_places(chunk, first, rest):
        return places(route_t, slot_own, 1, chunk, 8, first, rest)

    send_rows = jnp.dot(
        jnp.concatenate(
            [
                one_hot_rows(
                    jnp.maximum(
                        pair_places(route_t, slot_own, IN_ROWS, 0, 48),
                        full_places(IN_ROWS, 32, 52),
                    ),
                    nodes * IN_ROWS,
                ),
                one_hot_rows(
                    jnp.maximum(
                        pair_places(route_t, slot_own, IN_ROWS, 16, 50),
                        full_places(IN_ROWS, 40, 53),
                    ),
                    nodes * IN_ROWS,
                ),
                one_hot_rows(
                    pair_places(route_other, slot_other + CAP, IN_ROWS, 0, 48), nodes * IN_ROWS
                ),
                one_hot_rows(
                    pair_places(route_other, slot_other + CAP, IN_ROWS, 16, 50), nodes * IN_ROWS
                ),
            ],
            axis=1,
        ),
        jnp.concatenate([own, other], axis=0),
        preferred_element_type=F32,
    ).astype(BF)

    arrived = exchange(send_rows)
    rows0 = expert(arrived, w0, nodes, 16, 2, IN_ROWS, 0, 16, 48, 0, 2, 1)
    home0 = exchange(rows0)
    rows1 = expert(arrived, w1, nodes, 8, 1, IN_ROWS, 32, 40, 48, 4, 5, 1)
    home1 = exchange(rows1)

    places0 = jnp.concatenate(
        [
            pair_places(route_t, slot_own, OUT0_ROWS, 0, 32),
            pair_places(route_t, slot_own, OUT0_ROWS, 16, 34),
            pair_places(route_other, slot_other + CAP, OUT0_ROWS, 0, 32),
            pair_places(route_other, slot_other + CAP, OUT0_ROWS, 16, 34),
        ],
        axis=0,
    ).T
    places1 = jnp.concatenate(
        [full_places(OUT1_ROWS, 0, 16), full_places(OUT1_ROWS, 8, 17)], axis=0
    ).T
    values = jnp.concatenate([weight_t, weight_other], axis=0).T
    back, kept, dw_other, dw_own = combine_pair(home0, places0, values, grad_out, other)
    returned = send(back, across)
    dw_back = send(dw_other, across)
    return combine_full(home1, places1, values, grad_out, kept, returned, dw_own, dw_back)


def solution(mesh):
    tokens_spec = P(("node", "local"), None)

    return jax.shard_map(
        shards,
        mesh=mesh,
        in_specs=(
            tokens_spec,
            tokens_spec,
            tokens_spec,
            P("node", None, "local"),
            P("node", None, "local"),
            P("node", "local", None),
            tokens_spec,
        ),
        out_specs=(tokens_spec, tokens_spec, tokens_spec),
        check_vma=False,
    )
```

profile of v0, /device:TPU:2, one launch (start us, length us, event | category | flops | bytes accessed | tf_op | source)
XLA Modules:
  0.0 358.6 jit_solution(8232758828507571041)
XLA Ops:
  0.6 0.0 copy-start.10
  0.6 0.7 bitcast_convert_fusion
  1.4 0.7 pad_maximum_fusion.6
  2.1 4.0 %collective-permute-start = (f32[8,128]{1,0:T(8,128)S(1)}, f32[8,128]{1,0:T(8,128)S(1)}, u32[]{:S(2)}, u32[]{:S(2)}) collective-permute-start(f32[8,128]{1,0:T(8,128)S(1)} %pad_maximum_fusion.6), channel_id=1, source_target_pairs={{0,2},{1,3},{2,0},{3,1},{4,6},{5,7},{6,4},{7,5},{8,10},{9,11},{10,... | collective-permute-start | bytes 12296 | tf_op jit(solution)/shard_map/ppermute | solution.py:260
  6.0 1.3 pad_maximum_fusion.4
  7.3 0.2 collective-permute-start.1
  7.5 0.8 slice_bitcast_fusion.23
  8.3 0.2 select_reduce_fusion.7
  8.6 0.7 add_convert_fusion.2
  9.3 0.0 collective-permute-done
  9.4 0.2 select_reduce_fusion.3
  9.6 0.4 add_convert_fusion.1
  10.0 0.4 add_convert_fusion
  10.4 23.1 %collective-permute-done.1.grads_other = bf16[256,2048]{1,0:T(8,128)(2,1)S(1)} collective-permute-done((bf16[256,2048]{1,0:T(8,128)(2,1)S(1)}, bf16[256,2048]{1,0:T(8,128)(2,1)S(1)}, u32[]{:S(2)}, u32[]{:S(2)}) %collective-permute-start.1) | collective-permute-done | bytes 1048608 | tf_op jit(solution)/shard_map/ppermute | solution.py:260
  33.5 6.1 %convolution_convert_fusion = bf16[1792,2048]{1,0:T(8,128)(2,1)} fusion(bf16[256,2048]{1,0:T(8,128)(2,1)S(1)} %collective-permute-done.1.grads_other, bf16[128,2048]{1,0:T(8,128)(2,1)S(1)} %copy-done.7, bf16[128,2048]{1,0:T(8,128)(2,1)S(1)} %copy-done.8, bf16[1792,128]{1,0:T(8,128)(2,1)S(1)} %add_convert_fusion, bf16[1792,128]{1,0:T(8,128)(2,1)S(1)} %add_convert_fusion.1, ...), kind=kOutput, calls=%fused_computation | convolution fusion | flops 3775397888 | bytes 11272192 | tf_op jit(solution)/shard_map/dot_general | solution.py:300
  39.6 7.9 %all-to-all-start = ((bf16[32,56,2048]{2,1,0:T(8,128)(2,1)}), bf16[32,56,2048]{2,1,0:T(8,128)(2,1)}, u32[]{:S(2)}, u32[]{:S(2)}) async-start(bf16[32,56,2048]{2,1,0:T(8,128)(2,1)} %bitcast.94), calls=%async_computation | async-start | bytes 14680064 | tf_op jit(solution)/shard_map/all_to_all | solution.py:263
  47.6 0.0 copy-start.2
  47.6 0.0 copy-start.3
  47.6 0.4 fusion.66
  48.0 1.4 copy-done.2
  49.4 0.9 copy-done.3
  50.3 1.0 fusion.64
  51.3 0.2 pad_maximum_fusion.2.refs_1_
  51.5 0.8 collective-permute-start.8
  52.3 0.2 pad_maximum_fusion.3.refs_2_
  52.5 0.3 copy-done.5
  52.8 1.1 collective-permute-start.9
  53.9 0.2 pad_maximum_fusion.refs_1_
  54.2 1.1 collective-permute-start.2
  55.3 1.7 pad_maximum_fusion.1.refs_2_
  56.9 2.7 collective-permute-start.5
  59.6 41.9 %collective-permute-done.8.refs_3_ = bf16[3,176,2048]{2,1,0:T(8,128)(2,1)S(1)} collective-permute-done((bf16[3,176,2048]{2,1,0:T(8,128)(2,1)S(1)}, bf16[3,176,2048]{2,1,0:T(8,128)(2,1)S(1)}, u32[]{:S(2)}, u32[]{:S(2)}) %collective-permute-start.8) | collective-permute-done | bytes 2162720 | tf_op jit(solution)/shard_map/ppermute | solution.py:260
  101.5 1.3 copy-done.12
  102.8 1.2 collective-permute-done.9.refs_4_
  104.1 33.8 %all-to-all-done = bf16[32,56,2048]{2,1,0:T(8,128)(2,1)} async-done(((bf16[32,56,2048]{2,1,0:T(8,128)(2,1)}), bf16[32,56,2048]{2,1,0:T(8,128)(2,1)}, u32[]{:S(2)}, u32[]{:S(2)}) %all-to-all-start) | async-done | bytes 7340064 | tf_op jit(solution)/shard_map/all_to_all | solution.py:263
  137.9 19.7 %shard_map.95 = bf16[1280,2048]{1,0:T(8,128)(2,1)} custom-call(bf16[1792,2048]{1,0:T(8,128)(2,1)} %bitcast.35.refs_0_, bf16[3,176,2048]{2,1,0:T(8,128)(2,1)} %copy-done.5, bf16[3,176,2048]{2,1,0:T(8,128)(2,1)} %copy-done.6, bf16[3,176,2048]{2,1,0:T(8,128)(2,1)} %copy-done.12, bf16[3,176,2048]{2,1,0:T(8,128)(2,1)} %collective-permute-done.9.refs_4_), custom_call_target="tpu_custom_call" | custom-call | flops 9965666304 | bytes 18087936 | tf_op jit(solution)/shard_map/pallas_call | solution.py:144
  157.6 24.4 %all-to-all-start.2 = ((bf16[32,40,2048]{2,1,0:T(8,128)(2,1)}), bf16[32,40,2048]{2,1,0:T(8,128)(2,1)}, u32[]{:S(2)}, u32[]{:S(2)}) async-start(bf16[32,40,2048]{2,1,0:T(8,128)(2,1)} %bitcast.95), calls=%async_computation.2 | async-start | bytes 10485760 | tf_op jit(solution)/shard_map/all_to_all | solution.py:263
  182.0 1.1 collective-permute-start.3
  183.1 2.2 collective-permute-start.4
  185.3 0.0 collective-permute-done.2.refs_3_
  185.3 0.0 collective-permute-start.6
  185.3 0.0 collective-permute-done.5.refs_6_
  185.3 3.4 collective-permute-start.7
  188.7 44.7 %collective-permute-done.3.refs_4_ = bf16[3,176,2048]{2,1,0:T(8,128)(2,1)S(1)} collective-permute-done((bf16[3,176,2048]{2,1,0:T(8,128)(2,1)}, bf16[3,176,2048]{2,1,0:T(8,128)(2,1)S(1)}, u32[]{:S(2)}, u32[]{:S(2)}) %collective-permute-start.3) | collective-permute-done | bytes 2162720 | tf_op jit(solution)/shard_map/ppermute | solution.py:260
  233.4 0.0 collective-permute-done.4.refs_5_
  233.4 1.3 copy-done.13
  234.7 44.2 %collective-permute-done.6.refs_7_ = bf16[3,176,2048]{2,1,0:T(8,128)(2,1)S(1)} collective-permute-done((bf16[3,176,2048]{2,1,0:T(8,128)(2,1)}, bf16[3,176,2048]{2,1,0:T(8,128)(2,1)S(1)}, u32[]{:S(2)}, u32[]{:S(2)}) %collective-permute-start.6) | collective-permute-done | bytes 2162720 | tf_op jit(solution)/shard_map/ppermute | solution.py:260
  278.9 1.3 copy-done.15
  280.3 0.0 collective-permute-done.7.refs_8_
  280.3 20.8 %shard_map.94 = bf16[768,2048]{1,0:T(8,128)(2,1)} custom-call(bf16[1792,2048]{1,0:T(8,128)(2,1)} %bitcast.35.refs_0_, bf16[3,176,2048]{2,1,0:T(8,128)(2,1)} %copy-done.4, bf16[3,176,2048]{2,1,0:T(8,128)(2,1)} %pad_maximum_fusion.1.refs_2_, bf16[3,176,2048]{2,1,0:T(8,128)(2,1)} %collective-permute-done.2.refs_3_, bf16[3,176,2048]{2,1,0:T(8,128)(2,1)} %copy-done.13, ...), custom_call_target="tpu_custom_call" | custom-call | flops 9965666304 | bytes 22020096 | tf_op jit(solution)/shard_map/pallas_call | solution.py:144
  301.1 0.0 all-to-all-done.2
  301.1 0.0 copy-start.11
  301.1 7.7 %all-to-all-start.1 = ((bf16[32,24,2048]{2,1,0:T(8,128)(2,1)}), bf16[32,24,2048]{2,1,0:T(8,128)(2,1)S(1)}, u32[]{:S(2)}, u32[]{:S(2)}) async-start(bf16[32,24,2048]{2,1,0:T(8,128)(2,1)} %bitcast.96), calls=%async_computation.1 | async-start | bytes 6291456 | tf_op jit(solution)/shard_map/all_to_all | solution.py:263
  308.9 0.7 copy.34
  309.6 0.7 copy.33
  310.4 11.2 %combine_pair.1 = (bf16[256,2048]{1,0:T(8,128)(2,1)}, f32[256,2048]{1,0:T(8,128)}, f32[128,4]{1,0:T(8,128)}, f32[128,4]{1,0:T(8,128)}) custom-call(bf16[1280,2048]{1,0:T(8,128)(2,1)} %bitcast.43.home, s32[128,16]{1,0:T(8,128)} %bitcast.102, f32[128,8]{1,0:T(8,128)} %bitcast.99, bf16[128,2048]{1,0:T(8,128)(2,1)} %grads.3, bf16[256,2048]{1,0:T(8,128)(2,1)} %copy-done.16), custom_call_target="tpu_custom_call" | custom-call | flops 4026531840 | bytes 12582912 | tf_op jit(solution)/shard_map/combine_pair/pallas_call | solution.py:218
  321.6 0.1 collective-permute-start.10
  321.7 3.4 collective-permute-start.11
  325.1 0.7 copy.32
  325.9 19.9 %all-to-all-done.1 = bf16[32,24,2048]{2,1,0:T(8,128)(2,1)S(1)} async-done(((bf16[32,24,2048]{2,1,0:T(8,128)(2,1)}), bf16[32,24,2048]{2,1,0:T(8,128)(2,1)S(1)}, u32[]{:S(2)}, u32[]{:S(2)}) %all-to-all-start.1) | async-done | bytes 3145760 | tf_op jit(solution)/shard_map/all_to_all | solution.py:263
  345.8 4.1 %collective-permute-done.11.dw_back = f32[128,4]{1,0:T(8,128)S(1)} collective-permute-done((f32[128,4]{1,0:T(8,128)}, f32[128,4]{1,0:T(8,128)S(1)}, u32[]{:S(2)}, u32[]{:S(2)}) %collective-permute-start.11) | collective-permute-done | bytes 2080 | tf_op jit(solution)/shard_map/ppermute | solution.py:260
  349.9 0.6 copy-done.9
  350.5 6.3 %combine_full.1 = (bf16[128,2048]{1,0:T(8,128)(2,1)}, bf16[128,2048]{1,0:T(8,128)(2,1)}, f32[128,4]{1,0:T(8,128)}) custom-call(bf16[768,2048]{1,0:T(8,128)(2,1)} %bitcast.93, s32[128,8]{1,0:T(8,128)} %bitcast.101, f32[128,8]{1,0:T(8,128)} %bitcast.100, bf16[128,2048]{1,0:T(8,128)(2,1)} %grads.3, f32[256,2048]{1,0:T(8,128)} %get-tuple-element.7.own, ...), custom_call_target="tpu_custom_call" | custom-call | flops 1207959552 | bytes 8388608 | tf_op jit(solution)/shard_map/combine_full/pallas_call | solution.py:238
  356.9 1.5 copy.35
  (37 shorter events, 0.2 us)
Async XLA Ops:
  0.6 7.9 %copy-start.10 = (s32[128,4]{0,1:T(4,128)S(1)}, s32[128,4]{0,1:T(4,128)}, u32[]{:S(2)}) copy-start(s32[128,4]{0,1:T(4,128)} %param.8) | copy-start | bytes 6148
  2.1 31.4 %copy-start.7 = (bf16[128,2048]{1,0:T(8,128)(2,1)S(1)}, bf16[128,2048]{1,0:T(8,128)(2,1)}, u32[]{:S(2)}) copy-start(bf16[128,2048]{1,0:T(8,128)(2,1)} %grads.3) | copy-start | bytes 1572868
  2.1 31.4 %copy-start.8 = (bf16[128,2048]{1,0:T(8,128)(2,1)S(1)}, bf16[128,2048]{1,0:T(8,128)(2,1)}, u32[]{:S(2)}) copy-start(bf16[128,2048]{1,0:T(8,128)(2,1)} %param.7) | copy-start | bytes 1572868
  2.1 7.3 %collective-permute-start = (f32[8,128]{1,0:T(8,128)S(1)}, f32[8,128]{1,0:T(8,128)S(1)}, u32[]{:S(2)}, u32[]{:S(2)}) collective-permute-start(f32[8,128]{1,0:T(8,128)S(1)} %pad_maximum_fusion.6), channel_id=1, source_target_pairs={{0,2},{1,3},{2,0},{3,1},{4,6},{5,7},{6,4},{7,5},{8,10},{9,11},{10,... | collective-permute-start | bytes 12296 | tf_op jit(solution)/shard_map/ppermute | solution.py:260
  7.3 26.2 %collective-permute-start.1 = (bf16[256,2048]{1,0:T(8,128)(2,1)S(1)}, bf16[256,2048]{1,0:T(8,128)(2,1)S(1)}, u32[]{:S(2)}, u32[]{:S(2)}) collective-permute-start(bf16[256,2048]{1,0:T(8,128)(2,1)S(1)} %pad_maximum_fusion.4), channel_id=1, source_target_pairs={{0,2},{1,3},{2,0},{3,1},{4,6},{5,7},{6,4},{7,5},{8,10},{9,11},{10,... | collective-permute-start | bytes 3145736 | tf_op jit(solution)/shard_map/ppermute | solution.py:260
  33.5 6.1 %copy-start.16 = (bf16[256,2048]{1,0:T(8,128)(2,1)}, bf16[256,2048]{1,0:T(8,128)(2,1)S(1)}, u32[]{:S(2)}) copy-start(bf16[256,2048]{1,0:T(8,128)(2,1)S(1)} %collective-permute-done.1.grads_other) | copy-start | bytes 3145732
  39.6 7.9 %copy-start.1 = (bf16[2,352,2048]{2,1,0:T(8,128)(2,1)S(1)}, bf16[2,352,2048]{2,1,0:T(8,128)(2,1)}, u32[]{:S(2)}) copy-start(bf16[2,352,2048]{2,1,0:T(8,128)(2,1)} %param.12) | copy-start | bytes 8650756
  39.6 98.3 %all-to-all-start = ((bf16[32,56,2048]{2,1,0:T(8,128)(2,1)}), bf16[32,56,2048]{2,1,0:T(8,128)(2,1)}, u32[]{:S(2)}, u32[]{:S(2)}) async-start(bf16[32,56,2048]{2,1,0:T(8,128)(2,1)} %bitcast.94), calls=%async_computation | async-start | bytes 14680064 | tf_op jit(solution)/shard_map/all_to_all | solution.py:263
  47.6 1.8 copy-start.2
  47.6 2.7 copy-start.3
  51.5 1.3 copy-start.5
  51.5 50.0 %collective-permute-start.8 = (bf16[3,176,2048]{2,1,0:T(8,128)(2,1)S(1)}, bf16[3,176,2048]{2,1,0:T(8,128)(2,1)S(1)}, u32[]{:S(2)}, u32[]{:S(2)}) collective-permute-start(bf16[3,176,2048]{2,1,0:T(8,128)(2,1)S(1)} %pad_maximum_fusion.2.refs_1_), channel_id=1, source_target_pairs={{0,3},{1,0},{2,1},{3,2},{4,7},{5,4},{6,5},{7,6},{8,11},{9,8},{10,9... | collective-permute-start | bytes 6488072 | tf_op jit(solution)/shard_map/ppermute | solution.py:260
  52.8 1.3 copy-start.6
  52.8 51.2 %collective-permute-start.9 = (bf16[3,176,2048]{2,1,0:T(8,128)(2,1)S(1)}, bf16[3,176,2048]{2,1,0:T(8,128)(2,1)}, u32[]{:S(2)}, u32[]{:S(2)}) collective-permute-start(bf16[3,176,2048]{2,1,0:T(8,128)(2,1)S(1)} %pad_maximum_fusion.3.refs_2_), channel_id=1, source_target_pairs={{0,1},{1,2},{2,3},{3,0},{4,5},{5,6},{6,7},{7,4},{8,9},{9,10},{10,1... | collective-permute-start | bytes 6488072 | tf_op jit(solution)/shard_map/ppermute | solution.py:260
  54.2 128.9 %copy-start.4 = (bf16[3,176,2048]{2,1,0:T(8,128)(2,1)}, bf16[3,176,2048]{2,1,0:T(8,128)(2,1)S(1)}, u32[]{:S(2)}) copy-start(bf16[3,176,2048]{2,1,0:T(8,128)(2,1)S(1)} %pad_maximum_fusion.refs_1_) | copy-start | bytes 6488068
  54.2 131.1 %collective-permute-start.2 = (bf16[3,176,2048]{2,1,0:T(8,128)(2,1)S(1)}, bf16[3,176,2048]{2,1,0:T(8,128)(2,1)}, u32[]{:S(2)}, u32[]{:S(2)}) collective-permute-start(bf16[3,176,2048]{2,1,0:T(8,128)(2,1)S(1)} %pad_maximum_fusion.refs_1_), channel_id=1, source_target_pairs={{0,1},{1,2},{2,3},{3,0},{4,5},{5,6},{6,7},{7,4},{8,9},{9,10},{10,1... | collective-permute-start | bytes 6488072 | tf_op jit(solution)/shard_map/ppermute | solution.py:260
  56.9 128.4 %collective-permute-start.5 = (bf16[3,176,2048]{2,1,0:T(8,128)(2,1)}, bf16[3,176,2048]{2,1,0:T(8,128)(2,1)}, u32[]{:S(2)}, u32[]{:S(2)}) collective-permute-start(bf16[3,176,2048]{2,1,0:T(8,128)(2,1)} %pad_maximum_fusion.1.refs_2_), channel_id=1, source_target_pairs={{0,3},{1,0},{2,1},{3,2},{4,7},{5,4},{6,5},{7,6},{8,11},{9,8},{10,9... | collective-permute-start | bytes 6488072 | tf_op jit(solution)/shard_map/ppermute | solution.py:260
  101.5 1.4 copy-start.12
  157.6 143.5 %all-to-all-start.2 = ((bf16[32,40,2048]{2,1,0:T(8,128)(2,1)}), bf16[32,40,2048]{2,1,0:T(8,128)(2,1)}, u32[]{:S(2)}, u32[]{:S(2)}) async-start(bf16[32,40,2048]{2,1,0:T(8,128)(2,1)} %bitcast.95), calls=%async_computation.2 | async-start | bytes 10485760 | tf_op jit(solution)/shard_map/all_to_all | solution.py:263
  182.0 51.4 %collective-permute-start.3 = (bf16[3,176,2048]{2,1,0:T(8,128)(2,1)}, bf16[3,176,2048]{2,1,0:T(8,128)(2,1)S(1)}, u32[]{:S(2)}, u32[]{:S(2)}) collective-permute-start(bf16[3,176,2048]{2,1,0:T(8,128)(2,1)} %pad_maximum_fusion.1.refs_2_), channel_id=1, source_target_pairs={{0,1},{1,2},{2,3},{3,0},{4,5},{5,6},{6,7},{7,4},{8,9},{9,10},{10,1... | collective-permute-start | bytes 6488072 | tf_op jit(solution)/shard_map/ppermute | solution.py:260
  183.1 50.3 %collective-permute-start.4 = (bf16[3,176,2048]{2,1,0:T(8,128)(2,1)S(1)}, bf16[3,176,2048]{2,1,0:T(8,128)(2,1)S(1)}, u32[]{:S(2)}, u32[]{:S(2)}) collective-permute-start(bf16[3,176,2048]{2,1,0:T(8,128)(2,1)S(1)} %pad_maximum_fusion.refs_1_), channel_id=1, source_target_pairs={{0,3},{1,0},{2,1},{3,2},{4,7},{5,4},{6,5},{7,6},{8,11},{9,8},{10,9... | collective-permute-start | bytes 6488072 | tf_op jit(solution)/shard_map/ppermute | solution.py:260
  185.3 93.6 %collective-permute-start.6 = (bf16[3,176,2048]{2,1,0:T(8,128)(2,1)}, bf16[3,176,2048]{2,1,0:T(8,128)(2,1)S(1)}, u32[]{:S(2)}, u32[]{:S(2)}) collective-permute-start(bf16[3,176,2048]{2,1,0:T(8,128)(2,1)} %collective-permute-done.2.refs_3_), channel_id=1, source_target_pairs={{0,1},{1,2},{2,3},{3,0},{4,5},{5,6},{6,7},{7,4},{8,9},{9,10},{10,1... | collective-permute-start | bytes 6488072 | tf_op jit(solution)/shard_map/ppermute | solution.py:260
  185.3 94.9 %collective-permute-start.7 = (bf16[3,176,2048]{2,1,0:T(8,128)(2,1)}, bf16[3,176,2048]{2,1,0:T(8,128)(2,1)}, u32[]{:S(2)}, u32[]{:S(2)}) collective-permute-start(bf16[3,176,2048]{2,1,0:T(8,128)(2,1)} %collective-permute-done.5.refs_6_), channel_id=1, source_target_pairs={{0,3},{1,0},{2,1},{3,2},{4,7},{5,4},{6,5},{7,6},{8,11},{9,8},{10,9... | collective-permute-start | bytes 6488072 | tf_op jit(solution)/shard_map/ppermute | solution.py:260
  233.4 1.3 copy-start.13
  234.7 44.2 %copy-start.14 = (bf16[3,176,2048]{2,1,0:T(8,128)(2,1)}, bf16[3,176,2048]{2,1,0:T(8,128)(2,1)S(1)}, u32[]{:S(2)}) copy-start(bf16[3,176,2048]{2,1,0:T(8,128)(2,1)S(1)} %collective-permute-done.4.refs_5_) | copy-start | bytes 6488068
  278.9 1.4 copy-start.15
  301.1 8.5 %copy-start.11 = (f32[128,4]{0,1:T(4,128)S(1)}, f32[128,4]{0,1:T(4,128)}, u32[]{:S(2)}) copy-start(f32[128,4]{0,1:T(4,128)} %param.9) | copy-start | bytes 6148
  301.1 44.7 %all-to-all-start.1 = ((bf16[32,24,2048]{2,1,0:T(8,128)(2,1)}), bf16[32,24,2048]{2,1,0:T(8,128)(2,1)S(1)}, u32[]{:S(2)}, u32[]{:S(2)}) async-start(bf16[32,24,2048]{2,1,0:T(8,128)(2,1)} %bitcast.96), calls=%async_computation.1 | async-start | bytes 6291456 | tf_op jit(solution)/shard_map/all_to_all | solution.py:263
  321.6 28.3 %collective-permute-start.10 = (bf16[256,2048]{1,0:T(8,128)(2,1)}, bf16[256,2048]{1,0:T(8,128)(2,1)}, u32[]{:S(2)}, u32[]{:S(2)}) collective-permute-start(bf16[256,2048]{1,0:T(8,128)(2,1)} %get-tuple-element.8), channel_id=1, source_target_pairs={{0,2},{1,3},{2,0},{3,1},{4,6},{5,7},{6,4},{7,5},{8,10},{9,11},{10,... | collective-permute-start | bytes 3145736 | tf_op jit(solution)/shard_map/ppermute | solution.py:260
  321.7 28.2 %collective-permute-start.11 = (f32[128,4]{1,0:T(8,128)}, f32[128,4]{1,0:T(8,128)S(1)}, u32[]{:S(2)}, u32[]{:S(2)}) collective-permute-start(f32[128,4]{1,0:T(8,128)} %get-tuple-element.10), channel_id=1, source_target_pairs={{0,2},{1,3},{2,0},{3,1},{4,6},{5,7},{6,4},{7,5},{8,10},{9,11},{10,... | collective-permute-start | bytes 6152 | tf_op jit(solution)/shard_map/ppermute | solution.py:260
  345.8 4.1 %copy-start = (bf16[32,24,2048]{2,1,0:T(8,128)(2,1)}, bf16[32,24,2048]{2,1,0:T(8,128)(2,1)S(1)}, u32[]{:S(2)}) copy-start(bf16[32,24,2048]{2,1,0:T(8,128)(2,1)S(1)} %all-to-all-done.1) | copy-start | bytes 9437188
  349.9 0.6 copy-start.9
where the time goes:
time: 365 us; the launch traced here: 359 us
  waiting for transfers between devices  213 us (58%)
  starting transfers between devices  60 us (16%)
  Pallas kernels  58.1 us (16%)
  local copies, waits for them, and re-layouts  13.2 us (4%)
  other arithmetic  6.72 us (2%)
  matrix products  6.43 us (2%)
    ppermute x12, waiting for transfers between devices, send(): return lax.ppermute(value, 'local', pairs)  159 us
    all_to_all x3, waiting for transfers between devices, exchange(): return lax.all_to_all(rows, 'node', split_axis=0, concat_axis=0, tiled=True)  53.8 us
    pallas_call x2, Pallas kernels, expert(): pl.pallas_call(body, out_shape=jax.ShapeDtypeStruct((nodes * out_rows, wi...  40.5 us
    all_to_all x3, starting transfers between devices, exchange(): return lax.all_to_all(rows, 'node', split_axis=0, concat_axis=0, tiled=True)  40 us
    ppermute x12, starting transfers between devices, send(): return lax.ppermute(value, 'local', pairs)  20 us
    pallas_call x1, Pallas kernels, combine_pair(): pl.pallas_call(combine_pair_kernel, name='combine_pair', grid=(1,), out_s...  11.2 us
  transfers between devices with their start and end apart: 15, of which 8 were waited for; matrix products, arithmetic and copies ran while one was open for 3% of the time, Pallas kernels for 14%

commit v1 on v0

v1 whole, which is shorter than its diff:
```python
import functools

import jax
import jax.numpy as jnp
from jax import lax
from jax.experimental import pallas as pl
from jax.experimental.pallas import tpu as pltpu
from jax.sharding import PartitionSpec as P

EXPERTS = 64
TOP = 4
BF = jnp.bfloat16
F32 = jnp.float32

OWN_ROWS = 32
OTHER_ROWS = 24
OUT0_ROWS = 40
OUT1_ROWS = 24


def slots_of(route_t):
    toks = route_t.shape[1]
    expert_ids = jnp.arange(EXPERTS, dtype=jnp.int32)[:, None]
    hits = [(route_t[k][None, :] == expert_ids) for k in range(TOP)]
    named = sum(h.astype(BF) for h in hits)
    before = (
        jnp.arange(toks, dtype=jnp.int32)[:, None] < jnp.arange(toks, dtype=jnp.int32)[None, :]
    ).astype(BF)
    earlier = jnp.dot(named, before, preferred_element_type=F32)
    slots = [jnp.sum(jnp.where(h, earlier, 0.0), axis=0) for h in hits]
    return jnp.stack(slots).astype(jnp.int32)


def one_hot_rows(row_t, rows):
    ids = jnp.arange(rows, dtype=jnp.int32)[:, None]
    total = 0
    for k in range(TOP):
        total = total + jnp.where(row_t[k][None, :] == ids, 1.0, 0.0)
    return total.astype(BF)


def landed(dst, sem):
    pltpu.make_async_copy(dst, dst, sem).wait()


def fetch_rows(nodes, src, stride, first, dst, at, sem):
    def step(n, carry):
        frm = src.at[pl.ds(pl.multiple_of(n * stride + first, 8), 8)]
        to = dst.at[pl.ds(pl.multiple_of(at + n * 8, 8), 8)]
        pltpu.make_async_copy(frm, to, sem).start()
        return carry

    lax.fori_loop(0, nodes, step, 0)


def put_rows(nodes, src, at, dst, stride, first, sem):
    def step(n, carry):
        frm = src.at[pl.ds(pl.multiple_of(at + n * 8, 8), 8)]
        to = dst.at[pl.ds(pl.multiple_of(n * stride + first, 8), 8)]
        pltpu.make_async_copy(frm, to, sem).start()
        return carry

    lax.fori_loop(0, nodes, step, 0)


def fetch_weights(pieces, weights, sems, first):
    part = pieces[0].shape[1]
    for j, w in enumerate(weights):
        for i, p in enumerate(pieces):
            pltpu.make_async_copy(p.at[j], w.at[pl.ds(i * part, part)], sems.at[first + j]).start()


def picked(nodes, extra, offset, out_major):
    shape = (nodes * 8, nodes * extra) if out_major else (nodes * extra, nodes * 8)
    compact = lax.broadcasted_iota(jnp.int32, shape, 1 if out_major else 0)
    wide = lax.broadcasted_iota(jnp.int32, shape, 0 if out_major else 1)
    want = (compact // extra) * 8 + offset + compact % extra
    return (want == wide).astype(F32).astype(BF)


def by_hidden(rows, w):
    return lax.dot_general(rows, w, (((1,), (1,)), ((), ())), preferred_element_type=F32)


def by_row(rows, w):
    return jnp.dot(rows, w, preferred_element_type=F32)


def inner(x, g, wg, wu, wd):
    gate = by_hidden(x, wg)
    upper = by_hidden(x, wu)
    d_hidden = by_hidden(g, wd)
    s = jax.nn.sigmoid(gate)
    act = gate * s
    hidden = (act * upper).astype(BF)
    d_gate = (d_hidden * upper * s * (1.0 + gate * (1.0 - s))).astype(BF)
    d_up = (d_hidden * act).astype(BF)
    return hidden, d_gate, d_up


def expert_pair_kernel(nodes, n_pieces, *refs):
    arrived, arrived_other, pieces, home = refs[0], refs[1], refs[2 : 2 + n_pieces], refs[2 + n_pieces]
    xs, gs, rest, wg, wu, wd, outs, backs, out_rest, sems = refs[3 + n_pieces :]
    main, small = nodes * 16, nodes * 2
    fetch_rows(nodes, arrived, OWN_ROWS, 0, xs, 0, sems.at[0])
    fetch_rows(nodes, arrived_other, OTHER_ROWS, 0, xs, nodes * 8, sems.at[0])
    fetch_rows(nodes, arrived_other, OTHER_ROWS, 16, rest, 0, sems.at[1])
    fetch_weights(pieces, (wg, wu, wd), sems, 3)
    fetch_rows(nodes, arrived, OWN_ROWS, 8, gs, 0, sems.at[2])
    fetch_rows(nodes, arrived_other, OTHER_ROWS, 8, gs, nodes * 8, sems.at[2])
    landed(rest, sems.at[1])
    xs[pl.ds(main, small)] = by_row(picked(nodes, 2, 0, False), rest[...]).astype(BF)
    gs[pl.ds(main, small)] = by_row(picked(nodes, 2, 2, False), rest[...]).astype(BF)
    landed(xs.at[pl.ds(0, main)], sems.at[0])
    landed(wg, sems.at[3])
    landed(wu, sems.at[4])
    landed(gs.at[pl.ds(0, main)], sems.at[2])
    landed(wd, sems.at[5])
    size = (main + small) // 2

    def block(b, carry):
        at = pl.ds(pl.multiple_of(b * size, 16), size)
        hidden, d_gate, d_up = inner(xs[at], gs[at], wg[...], wu[...], wd[...])
        outs[at] = by_row(hidden, wd[...]).astype(BF)
        backs[at] = (by_row(d_gate, wg[...]) + by_row(d_up, wu[...])).astype(BF)
        return carry

    lax.fori_loop(0, 2, block, 0)
    put_rows(nodes, outs, 0, home, OUT0_ROWS, 0, sems.at[0])
    put_rows(nodes, outs, nodes * 8, home, OUT0_ROWS, 8, sems.at[0])
    put_rows(nodes, backs, 0, home, OUT0_ROWS, 16, sems.at[1])
    put_rows(nodes, backs, nodes * 8, home, OUT0_ROWS, 24, sems.at[1])
    out_rest[...] = (
        by_row(picked(nodes, 2, 0, True), outs[pl.ds(main, small)])
        + by_row(picked(nodes, 2, 2, True), backs[pl.ds(main, small)])
    ).astype(BF)
    put_rows(nodes, out_rest, 0, home, OUT0_ROWS, 32, sems.at[2])
    landed(outs.at[pl.ds(0, main)], sems.at[0])
    landed(backs.at[pl.ds(0, main)], sems.at[1])
    landed(out_rest, sems.at[2])


def expert_near_kernel(nodes, n_pieces, *refs):
    arrived, arrived_other, pieces = refs[0], refs[1], refs[2 : 2 + n_pieces]
    out_part, back_part, xs, gs = refs[2 + n_pieces : 6 + n_pieces]
    rest, wg, wu, wd, sems = refs[6 + n_pieces :]
    main, small = nodes * 8, nodes
    fetch_rows(nodes, arrived, OWN_ROWS, 16, xs, 0, sems.at[0])
    fetch_rows(nodes, arrived, OWN_ROWS, 24, gs, 0, sems.at[2])
    fetch_rows(nodes, arrived_other, OTHER_ROWS, 16, rest, 0, sems.at[1])
    fetch_weights(pieces, (wg, wu, wd), sems, 3)
    landed(rest, sems.at[1])
    landed(xs.at[pl.ds(0, main)], sems.at[0])
    landed(gs.at[pl.ds(0, main)], sems.at[2])
    xs[pl.ds(main, small)] = by_row(picked(nodes, 1, 4, False), rest[...]).astype(BF)
    gs[pl.ds(main, small)] = by_row(picked(nodes, 1, 5, False), rest[...]).astype(BF)
    landed(wg, sems.at[3])
    landed(wu, sems.at[4])
    landed(wd, sems.at[5])
    hidden, d_gate, d_up = inner(xs[...], gs[...], wg[...], wu[...], wd[...])
    out_part[...] = by_row(hidden, wd[...])
    back_part[...] = by_row(d_gate, wg[...]) + by_row(d_up, wu[...])


def expert_far_kernel(nodes, n_pieces, *refs):
    xs, gs, out_part, back_part = refs[:4]
    pieces, home = refs[4 : 4 + n_pieces], refs[4 + n_pieces]
    wg, wu, wd, outs, backs, out_rest, sems = refs[5 + n_pieces :]
    main, small = nodes * 8, nodes
    fetch_weights(pieces, (wg, wu, wd), sems, 3)
    for j, w in enumerate((wg, wu, wd)):
        landed(w, sems.at[3 + j])
    hidden, d_gate, d_up = inner(xs[...], gs[...], wg[...], wu[...], wd[...])
    outs[...] = (by_row(hidden, wd[...]) + out_part[...]).astype(BF)
    put_rows(nodes, outs, 0, home, OUT1_ROWS, 0, sems.at[0])
    backs[...] = (by_row(d_gate, wg[...]) + by_row(d_up, wu[...]) + back_part[...]).astype(BF)
    put_rows(nodes, backs, 0, home, OUT1_ROWS, 8, sems.at[1])
    out_rest[...] = (
        by_row(picked(nodes, 1, 0, True), outs[pl.ds(main, small)])
        + by_row(picked(nodes, 1, 1, True), backs[pl.ds(main, small)])
    ).astype(BF)
    put_rows(nodes, out_rest, 0, home, OUT1_ROWS, 16, sems.at[2])
    landed(outs.at[pl.ds(0, main)], sems.at[0])
    landed(backs.at[pl.ds(0, main)], sems.at[1])
    landed(out_rest, sems.at[2])


ANY = pl.BlockSpec(memory_space=pl.ANY)
WHOLE = pl.BlockSpec(memory_space=pltpu.VMEM)
PARAMS = pltpu.CompilerParams(vmem_limit_bytes=60 * 1024 * 1024)


def expert_cost(rows, hidden, width):
    return pl.CostEstimate(
        flops=12 * rows * hidden * width,
        transcendentals=rows * hidden,
        bytes_accessed=2 * width * (4 * rows + 3 * hidden),
    )


def expert_pair(arrived, arrived_other, pieces, nodes):
    width = arrived.shape[1]
    rows, hidden = nodes * 18, len(pieces) * pieces[0].shape[1]
    scratch = [(rows, width), (rows, width), (nodes * 8, width)] + [(hidden, width)] * 3
    scratch += [(rows, width), (rows, width), (nodes * 8, width)]
    return pl.pallas_call(
        functools.partial(expert_pair_kernel, nodes, len(pieces)),
        name="expert_pair",
        out_shape=jax.ShapeDtypeStruct((nodes * OUT0_ROWS, width), BF),
        in_specs=[ANY] * (2 + len(pieces)),
        out_specs=ANY,
        scratch_shapes=[pltpu.VMEM(s, BF) for s in scratch] + [pltpu.SemaphoreType.DMA((6,))],
        compiler_params=PARAMS,
        cost_estimate=expert_cost(rows, hidden, width),
    )(arrived, arrived_other, *pieces)


def expert_near(arrived, arrived_other, pieces, nodes):
    width = arrived.shape[1]
    rows, hidden = nodes * 9, len(pieces) * pieces[0].shape[1]
    scratch = [(nodes * 8, width)] + [(hidden, width)] * 3
    return pl.pallas_call(
        functools.partial(expert_near_kernel, nodes, len(pieces)),
        name="expert_near",
        out_shape=tuple(jax.ShapeDtypeStruct((rows, width), t) for t in (F32, F32, BF, BF)),
        in_specs=[ANY] * (2 + len(pieces)),
        out_specs=(WHOLE,) * 4,
        scratch_shapes=[pltpu.VMEM(s, BF) for s in scratch] + [pltpu.SemaphoreType.DMA((6,))],
        compiler_params=PARAMS,
        cost_estimate=expert_cost(rows, hidden, width),
    )(arrived, arrived_other, *pieces)


def expert_far(near, pieces, nodes):
    out_part, back_part, xs, gs = near
    rows, width = xs.shape
    hidden = len(pieces) * pieces[0].shape[1]
    scratch = [(hidden, width)] * 3 + [(rows, width), (rows, width), (nodes * 8, width)]
    return pl.pallas_call(
        functools.partial(expert_far_kernel, nodes, len(pieces)),
        name="expert_far",
        out_shape=jax.ShapeDtypeStruct((nodes * OUT1_ROWS, width), BF),
        in_specs=[WHOLE] * 4 + [ANY] * len(pieces),
        out_specs=ANY,
        scratch_shapes=[pltpu.VMEM(s, BF) for s in scratch] + [pltpu.SemaphoreType.DMA((6,))],
        compiler_params=PARAMS,
        cost_estimate=expert_cost(rows, hidden, width),
    )(xs, gs, out_part, back_part, *pieces)


def mixed(rows_ref, places, first, values, ids):
    total = 0.0
    for k in range(TOP):
        total = total + jnp.where(places[:, first + k : first + k + 1] == ids, values[:, k : k + 1], 0.0)
    return jnp.dot(total.astype(BF), rows_ref[...], preferred_element_type=F32)


def weight_grads(rows_ref, grads, places, first, ids):
    table = lax.dot_general(grads, rows_ref[...], (((1,), (1,)), ((), ())), preferred_element_type=F32)
    return jnp.concatenate(
        [
            jnp.sum(jnp.where(places[:, first + k : first + k + 1] == ids, table, 0.0), axis=1, keepdims=True)
            for k in range(TOP)
        ],
        axis=1,
    )


def combine_pair_kernel(home, places_ref, values_ref, grads, grads_other, back, own, dw_other, dw_own):
    toks = grads.shape[0]
    ids = lax.broadcasted_iota(jnp.int32, (toks, home.shape[0]), 1)
    places = places_ref[...]
    values, values_other = values_ref[:, :TOP], values_ref[:, TOP:]
    back[:toks] = mixed(home, places, 2 * TOP, values_other, ids).astype(BF)
    back[toks:] = mixed(home, places, 3 * TOP, values_other, ids).astype(BF)
    dw_other[...] = weight_grads(home, grads_other[...], places, 2 * TOP, ids)
    own[:toks] = mixed(home, places, 0, values, ids)
    own[toks:] = mixed(home, places, TOP, values, ids)
    dw_own[...] = weight_grads(home, grads[...], places, 0, ids)


def combine_full_kernel(home, places_ref, values_ref, grads, own, returned, dw_own, dw_back, combined, d_tokens, d_weights):
    toks = grads.shape[0]
    ids = lax.broadcasted_iota(jnp.int32, (toks, home.shape[0]), 1)
    places = places_ref[...]
    values = values_ref[:, :TOP]
    combined[...] = (
        mixed(home, places, 0, values, ids) + own[:toks] + returned[:toks].astype(F32)
    ).astype(BF)
    d_tokens[...] = (
        mixed(home, places, TOP, values, ids) + own[toks:] + returned[toks:].astype(F32)
    ).astype(BF)
    d_weights[...] = weight_grads(home, grads[...], places, 0, ids) + dw_own[...] + dw_back[...]


def combine_pair(home, places, values, grads, other):
    toks, width = grads.shape
    whole = pl.BlockSpec(memory_space=pltpu.VMEM)
    return pl.pallas_call(
        combine_pair_kernel,
        name="combine_pair",
        grid=(1,),
        out_shape=(
            jax.ShapeDtypeStruct((2 * toks, width), BF),
            jax.ShapeDtypeStruct((2 * toks, width), F32),
            jax.ShapeDtypeStruct((toks, TOP), F32),
            jax.ShapeDtypeStruct((toks, TOP), F32),
        ),
        in_specs=[whole] * 4 + [pl.BlockSpec((toks, width), lambda i: (1, 0))],
        out_specs=(whole,) * 4,
        cost_estimate=pl.CostEstimate(
            flops=12 * toks * home.shape[0] * width, transcendentals=0, bytes_accessed=12 * 1024 * 1024
        ),
    )(home, places, values, grads, other)


def combine_full(home, places, values, grads, own, returned, dw_own, dw_back):
    toks, width = grads.shape
    return pl.pallas_call(
        combine_full_kernel,
        name="combine_full",
        out_shape=(
            jax.ShapeDtypeStruct((toks, width), BF),
            jax.ShapeDtypeStruct((toks, width), BF),
            jax.ShapeDtypeStruct((toks, TOP), F32),
        ),
        cost_estimate=pl.CostEstimate(
            flops=6 * toks * home.shape[0] * width, transcendentals=0, bytes_accessed=8 * 1024 * 1024
        ),
    )(home, places, values, grads, own, returned, dw_own, dw_back)


def shards(tokens, route, combine_weights, w_gate, w_up, w_down, grad_out):
    nodes = lax.axis_size("node")
    planes = lax.axis_size("local")
    up = [(i, (i + 1) % planes) for i in range(planes)]
    down = [(i, (i - 1) % planes) for i in range(planes)]
    across = [(i, (i + 2) % planes) for i in range(planes)]

    def send(value, pairs):
        return lax.ppermute(value, "local", pairs)

    def exchange(rows):
        return lax.all_to_all(rows, "node", split_axis=0, concat_axis=0, tiled=True)

    own = jnp.concatenate([tokens, grad_out], axis=0)
    other = send(own, across)
    route_t = route.T
    weight_t = combine_weights.T
    small = send(jnp.concatenate([weight_t, route_t.astype(F32)], axis=0), across)
    weight_other = small[:TOP]
    route_other = small[TOP:].astype(jnp.int32)

    gate_t = jnp.swapaxes(w_gate, 1, 2)
    up_t = jnp.swapaxes(w_up, 1, 2)
    half = gate_t.shape[1] // 2

    def piece(expert, part):
        cut = slice(part * half, (part + 1) * half)
        return jnp.stack([gate_t[expert, cut], up_t[expert, cut], w_down[expert, cut]])

    p0a, p0b, p1a, p1b = piece(0, 0), piece(0, 1), piece(1, 0), piece(1, 1)
    w0 = [p0a, p0b, send(p0a, down), send(p0b, up)]
    below_a, above_b = send(p1a, up), send(p1b, down)
    below_b, above_a = send(p1b, up), send(p1a, down)
    far_a, far_b = send(below_a, up), send(above_b, down)
    w1 = [p1a, p1b, below_a, below_b, above_a, above_b, far_a, far_b]

    slot_own, slot_other = slots_of(route_t), slots_of(route_other)

    def places(route_rows, row, keep):
        chunk, index = row
        return jnp.where(keep, (route_rows // 2) * chunk + index, -1)

    own_even, other_even = route_t % 2 == 0, route_other % 2 == 0
    own_main, other_main = slot_own < 8, slot_other < 8

    def own_place(first_even, first_odd):
        index = jnp.where(own_even, first_even, first_odd) + slot_own
        return places(route_t, (OWN_ROWS, index), own_main)

    def rest_place(even, odd):
        return places(route_t, (OTHER_ROWS, jnp.where(own_even, even, odd)), ~own_main)

    def other_place(main, rest, chunk):
        index = jnp.where(other_main, main + slot_other, rest)
        return places(route_other, (chunk, index), other_even)

    own_rows = jnp.dot(
        jnp.concatenate(
            [
                one_hot_rows(own_place(0, 16), nodes * OWN_ROWS),
                one_hot_rows(own_place(8, 24), nodes * OWN_ROWS),
            ],
            axis=1,
        ),
        own,
        preferred_element_type=F32,
    ).astype(BF)
    arrived = exchange(own_rows)
    other_rows = jnp.dot(
        jnp.concatenate(
            [
                one_hot_rows(rest_place(16, 20), nodes * OTHER_ROWS),
                one_hot_rows(rest_place(18, 21), nodes * OTHER_ROWS),
                one_hot_rows(other_place(0, 17, OTHER_ROWS), nodes * OTHER_ROWS),
                one_hot_rows(other_place(8, 19, OTHER_ROWS), nodes * OTHER_ROWS),
            ],
            axis=1,
        ),
        jnp.concatenate([own, other], axis=0),
        preferred_element_type=F32,
    ).astype(BF)
    arrived_other = exchange(other_rows)

    rows0 = expert_pair(arrived, arrived_other, w0, nodes)
    home0 = exchange(rows0)
    near = expert_near(arrived, arrived_other, w1[:6], nodes)
    rows1 = expert_far(near, w1[6:], nodes)
    home1 = exchange(rows1)

    def home_place(main, rest):
        index = jnp.where(own_main, main + slot_own, rest)
        return places(route_t, (OUT0_ROWS, index), own_even)

    def full_place(main, rest):
        index = jnp.where(own_main, main + slot_own, rest)
        return places(route_t, (OUT1_ROWS, index), ~own_even)

    places0 = jnp.concatenate(
        [
            home_place(0, 32),
            home_place(16, 34),
            other_place(8, 33, OUT0_ROWS),
            other_place(24, 35, OUT0_ROWS),
        ],
        axis=0,
    ).T
    places1 = jnp.concatenate([full_place(0, 16), full_place(8, 17)], axis=0).T
    values = jnp.concatenate([weight_t, weight_other], axis=0).T
    back, kept, dw_other, dw_own = combine_pair(home0, places0, values, grad_out, other)
    returned = send(back, across)
    dw_back = send(dw_other, across)
    return combine_full(home1, places1, values, grad_out, kept, returned, dw_own, dw_back)


def solution(mesh):
    tokens_spec = P(("node", "local"), None)

    return jax.shard_map(
        shards,
        mesh=mesh,
        in_specs=(
            tokens_spec,
            tokens_spec,
            tokens_spec,
            P("node", None, "local"),
            P("node", None, "local"),
            P("node", "local", None),
            tokens_spec,
        ),
        out_specs=(tokens_spec, tokens_spec, tokens_spec),
        check_vma=False,
    )
```

time: 365 us -> 383 us (1.049)
  waiting for transfers between devices: 213 us -> 225 us
  local copies, waits for them, and re-layouts: 13.2 us -> 22.7 us
  starting transfers between devices: 60 us -> 52 us
  Pallas kernels: 58.1 us -> 65.6 us
    ppermute x12, waiting for transfers between devices: 159 us -> 188 us  [send(): return lax.ppermute(value, 'local', pairs)]
    all_to_all x3 -> x4, waiting for transfers between devices: 53.8 us -> 37.2 us  [exchange(): return lax.all_to_all(rows, 'node', split_axis=0, concat_axis=0, tiled=True)]
    all_to_all x3 -> x4, starting transfers between devices: 40 us -> 32.4 us  [exchange(): return lax.all_to_all(rows, 'node', split_axis=0, concat_axis=0, tiled=True)]
    pallas_call x2 -> x3, Pallas kernels: 40.5 us -> 48 us  [the longest x1 19.3 us: expert_pair(): pl.pallas_call(functools.partial(expert_pair_kernel, nodes, len(pieces)),...]
    unnamed x34 -> x55, local copies, waits for them, and re-layouts: 7.29 us -> 9.22 us
  transfers between devices with their start and end apart: 15 -> 16, of which waited for: 8 -> 11; matrix products, arithmetic and copies ran while one was open for 3% -> 4% of each run, Pallas kernels for 14% -> 11%
where the time goes in v1:
time: 383 us; the launch traced here: 376 us
  waiting for transfers between devices  225 us (59%)
  Pallas kernels  65.6 us (17%)
  starting transfers between devices  52 us (14%)
  local copies, waits for them, and re-layouts  22.7 us (6%)
  matrix products  7.06 us (2%)
    ppermute x12, waiting for transfers between devices, send(): return lax.ppermute(value, 'local', pairs)  188 us
    all_to_all x4, waiting for transfers between devices, exchange(): return lax.all_to_all(rows, 'node', split_axis=0, concat_axis=0, tiled=True)  37.2 us
    all_to_all x4, starting transfers between devices, exchange(): return lax.all_to_all(rows, 'node', split_axis=0, concat_axis=0, tiled=True)  32.4 us
    ppermute x12, starting transfers between devices, send(): return lax.ppermute(value, 'local', pairs)  19.5 us
    pallas_call x1, Pallas kernels, expert_pair(): pl.pallas_call(functools.partial(expert_pair_kernel, nodes, len(pieces)),...  19.3 us
    pallas_call x1, Pallas kernels, expert_near(): pl.pallas_call(functools.partial(expert_near_kernel, nodes, len(pieces)),...  17.1 us
    pallas_call x1, Pallas kernels, expert_far(): pl.pallas_call(functools.partial(expert_far_kernel, nodes, len(pieces)),...  11.6 us
    pallas_call x1, Pallas kernels, combine_pair(): pl.pallas_call(combine_pair_kernel, name='combine_pair', grid=(1,), out_s...  11.2 us
  transfers between devices with their start and end apart: 16, of which 11 were waited for; matrix products, arithmetic and copies ran while one was open for 4% of the time, Pallas kernels for 11%

profile of v1, /device:TPU:2, one launch (start us, length us, event | category | flops | bytes accessed | tf_op | source)
XLA Modules:
  0.0 376.4 jit_solution(4680974052846953070)
XLA Ops:
  0.6 0.8 slice_bitcast_fusion.31
  1.5 1.1 constant_dynamic-update-slice_fusion.1
  2.6 0.2 select_reduce_fusion.7
  2.7 0.7 add_select_fusion.7
  3.5 1.1 constant_dynamic-update-slice_fusion
  4.6 0.2 add_convert_fusion
  4.8 0.2 add_convert_fusion.1
  5.0 3.2 convolution_convert_fusion
  8.3 8.0 %all-to-all-start = ((bf16[32,32,2048]{2,1,0:T(8,128)(2,1)}), bf16[32,32,2048]{2,1,0:T(8,128)(2,1)}, u32[]{:S(2)}, u32[]{:S(2)}) async-start(bf16[32,32,2048]{2,1,0:T(8,128)(2,1)} %bitcast.93), calls=%async_computation | async-start | bytes 8388608 | tf_op jit(solution)/shard_map/all_to_all | solution.py:344
  16.3 4.0 %collective-permute-start.1 = (bf16[256,2048]{1,0:T(8,128)(2,1)}, bf16[256,2048]{1,0:T(8,128)(2,1)S(1)}, u32[]{:S(2)}, u32[]{:S(2)}) collective-permute-start(bf16[256,2048]{1,0:T(8,128)(2,1)} %copy-done.13), channel_id=1, source_target_pairs={{0,2},{1,3},{2,0},{3,1},{4,6},{5,7},{6,4},{7,5},{8,10},{9,11},{10,... | collective-permute-start | bytes 3145736 | tf_op jit(solution)/shard_map/ppermute | solution.py:341
  20.2 0.1 collective-permute-start
  20.4 0.2 add_convert_fusion.5
  20.6 4.6 %fusion.54 = (bf16[1,176,2048]{2,1,0:T(8,128)(2,1)}, bf16[1,176,2048]{2,1,0:T(8,128)(2,1)}, bf16[1,176,2048]{2,1,0:T(8,128)(2,1)}, bf16[1,176,2048]{2,1,0:T(8,12...) fusion(bf16[2,352,2048]{2,1,0:T(8,128)(2,1)S(1)} %bitcast.100, ...), kind=kLoop, calls=%fused_computation.168 | loop fusion | bytes 11534336 | tf_op jit(solution)/shard_map/slice | solution.py:360
  25.2 0.2 add_convert_fusion.4
  25.4 18.6 %collective-permute-done = f32[8,128]{1,0:T(8,128)S(1)} collective-permute-done((f32[8,128]{1,0:T(8,128)S(1)}, f32[8,128]{1,0:T(8,128)S(1)}, u32[]{:S(2)}, u32[]{:S(2)}) %collective-permute-start) | collective-permute-done | bytes 4128 | tf_op jit(solution)/shard_map/ppermute | solution.py:341
  44.0 0.2 select_reduce_fusion.3
  44.2 0.2 add_convert_fusion.2
  44.4 0.2 add_convert_fusion.3
  44.6 1.0 copy-done.26
  45.5 3.5 convolution_convert_fusion.1
  49.0 17.2 %all-to-all-done = bf16[32,32,2048]{2,1,0:T(8,128)(2,1)} async-done(((bf16[32,32,2048]{2,1,0:T(8,128)(2,1)}), bf16[32,32,2048]{2,1,0:T(8,128)(2,1)}, u32[]{:S(2)}, u32[]{:S(2)}) %all-to-all-start) | async-done | bytes 4194336 | tf_op jit(solution)/shard_map/all_to_all | solution.py:344
  66.2 9.2 %all-to-all-start.1 = ((bf16[32,24,2048]{2,1,0:T(8,128)(2,1)}), bf16[32,24,2048]{2,1,0:T(8,128)(2,1)S(1)}, u32[]{:S(2)}, u32[]{:S(2)}) async-start(bf16[32,24,2048]{2,1,0:T(8,128)(2,1)} %bitcast.99), calls=%async_computation.1 | async-start | bytes 6291456 | tf_op jit(solution)/shard_map/all_to_all | solution.py:344
  75.4 3.3 fusion.56
  78.7 0.2 pad_maximum_fusion.2.refs_2_
  79.0 4.1 %collective-permute-start.8 = (bf16[3,176,2048]{2,1,0:T(8,128)(2,1)S(1)}, bf16[3,176,2048]{2,1,0:T(8,128)(2,1)S(1)}, u32[]{:S(2)}, u32[]{:S(2)}) collective-permute-start(bf16[3,176,2048]{2,1,0:T(8,128)(2,1)S(1)} %pad_maximum_fusion.2.refs_2_), channel_id=1, source_target_pairs={{0,3},{1,0},{2,1},{3,2},{4,7},{5,4},{6,5},{7,6},{8,11},{9,8},{10,9... | collective-permute-start | bytes 6488072 | tf_op jit(solution)/shard_map/ppermute | solution.py:341
  83.1 0.2 pad_maximum_fusion.3.refs_3_
  83.4 0.5 collective-permute-start.9
  83.9 45.8 %collective-permute-done.8.refs_4_ = bf16[3,176,2048]{2,1,0:T(8,128)(2,1)S(1)} collective-permute-done((bf16[3,176,2048]{2,1,0:T(8,128)(2,1)S(1)}, bf16[3,176,2048]{2,1,0:T(8,128)(2,1)S(1)}, u32[]{:S(2)}, u32[]{:S(2)}) %collective-permute-start.8) | collective-permute-done | bytes 2162720 | tf_op jit(solution)/shard_map/ppermute | solution.py:341
  129.7 1.4 copy-done.25
  131.1 2.9 collective-permute-done.9.refs_5_
  134.0 1.6 copy-done.1
  135.6 19.3 %expert_pair.1 = bf16[1280,2048]{1,0:T(8,128)(2,1)} custom-call(bf16[1024,2048]{1,0:T(8,128)(2,1)} %bitcast.18.refs_0_, bf16[768,2048]{1,0:T(8,128)(2,1)} %bitcast.97, bf16[3,176,2048]{2,1,0:T(8,128)(2,1)} %copy-done.17, bf16[3,176,2048]{2,1,0:T(8,128)(2,1)} %copy-done.18, bf16[3,176,2048]{2,1,0:T(8,128)(2,1)} %copy-done.25, ...), custom_call_target="tpu_custom_call" | custom-call | flops 9965666304 | bytes 18087936 | tf_op jit(solution)/shard_map/expert_pair/pallas_call | solution.py:206
  155.0 7.6 %all-to-all-start.3 = ((bf16[32,40,2048]{2,1,0:T(8,128)(2,1)}), bf16[32,40,2048]{2,1,0:T(8,128)(2,1)}, u32[]{:S(2)}, u32[]{:S(2)}) async-start(bf16[32,40,2048]{2,1,0:T(8,128)(2,1)} %bitcast.96), calls=%async_computation.3 | async-start | bytes 10485760 | tf_op jit(solution)/shard_map/all_to_all | solution.py:344
  162.6 0.2 pad_maximum_fusion.refs_2_
  162.9 0.1 collective-permute-start.2
  163.0 0.7 copy-done.3
  163.7 0.6 copy-done.4
  164.3 0.6 copy-done.11
  164.9 0.2 pad_maximum_fusion.1.refs_3_
  165.2 1.3 collective-permute-start.5
  166.5 0.8 collective-permute-start.3
  167.3 2.5 collective-permute-start.4
  169.8 44.4 %collective-permute-done.2.refs_4_ = bf16[3,176,2048]{2,1,0:T(8,128)(2,1)} collective-permute-done((bf16[3,176,2048]{2,1,0:T(8,128)(2,1)S(1)}, bf16[3,176,2048]{2,1,0:T(8,128)(2,1)}, u32[]{:S(2)}, u32[]{:S(2)}) %collective-permute-start.2) | collective-permute-done | bytes 2162720 | tf_op jit(solution)/shard_map/ppermute | solution.py:341
  214.2 1.1 collective-permute-done.5.refs_7_
  215.3 2.6 collective-permute-start.7
  217.9 42.5 %collective-permute-done.3.refs_5_ = bf16[3,176,2048]{2,1,0:T(8,128)(2,1)S(1)} collective-permute-done((bf16[3,176,2048]{2,1,0:T(8,128)(2,1)S(1)}, bf16[3,176,2048]{2,1,0:T(8,128)(2,1)S(1)}, u32[]{:S(2)}, u32[]{:S(2)}) %collective-permute-start.3) | collective-permute-done | bytes 2162720 | tf_op jit(solution)/shard_map/ppermute | solution.py:341
  260.4 1.4 copy-done.24
  261.8 17.1 %expert_near.1 = (f32[288,2048]{1,0:T(8,128)}, f32[288,2048]{1,0:T(8,128)}, bf16[288,2048]{1,0:T(8,128)(2,1)}, bf16[288,2048]{1,0:T(8,128)(2,1)}) custom-call(bf16[1024,2048]{1,0:T(8,128)(2,1)} %bitcast.18.refs_0_, bf16[768,2048]{1,0:T(8,128)(2,1)} %bitcast.98, bf16[3,176,2048]{2,1,0:T(8,128)(2,1)} %copy-done.15, bf16[3,176,2048]{2,1,0:T(8,128)(2,1)} %copy-done.16, ...), custom_call_target="tpu_custom_call" | custom-call | flops 7474249728 | bytes 17694720 | tf_op jit(solution)/shard_map/expert_near/pallas_call | solution.py:222
  278.9 27.0 %collective-permute-done.6.refs_4_ = bf16[3,176,2048]{2,1,0:T(8,128)(2,1)S(1)} collective-permute-done((bf16[3,176,2048]{2,1,0:T(8,128)(2,1)}, bf16[3,176,2048]{2,1,0:T(8,128)(2,1)S(1)}, u32[]{:S(2)}, u32[]{:S(2)}) %collective-permute-start.6) | collective-permute-done | bytes 2162720 | tf_op jit(solution)/shard_map/ppermute | solution.py:341
  305.9 1.2 collective-permute-done.7.refs_5_
  307.1 0.2 copy-done.14
  307.3 11.6 %expert_far.1 = bf16[768,2048]{1,0:T(8,128)(2,1)} custom-call(bf16[288,2048]{1,0:T(8,128)(2,1)} %get-tuple-element.11.refs_0_, bf16[288,2048]{1,0:T(8,128)(2,1)} %get-tuple-element.12.refs_1_, f32[288,2048]{1,0:T(8,128)} %get-tuple-element.13.refs_2_, f32[288,2048]{1,0:T(8,128)} %get-tuple-element.14.refs_3_, bf16[3,176,2048]{2,1,0:T(8,128)(2,1)} %copy-done.14, ...), custom_call_target="tpu_custom_call" | custom-call | flops 2491416576 | bytes 9043968 | tf_op jit(solution)/shard_map/expert_far/pallas_call | solution.py:239
  318.9 7.7 %all-to-all-start.2 = ((bf16[32,24,2048]{2,1,0:T(8,128)(2,1)}), bf16[32,24,2048]{2,1,0:T(8,128)(2,1)S(1)}, u32[]{:S(2)}, u32[]{:S(2)}) async-start(bf16[32,24,2048]{2,1,0:T(8,128)(2,1)} %bitcast.95), calls=%async_computation.2 | async-start | bytes 6291456 | tf_op jit(solution)/shard_map/all_to_all | solution.py:344
  326.7 0.7 copy.34
  327.4 0.7 copy.33
  328.1 11.2 %combine_pair.1 = (bf16[256,2048]{1,0:T(8,128)(2,1)}, f32[256,2048]{1,0:T(8,128)}, f32[128,4]{1,0:T(8,128)}, f32[128,4]{1,0:T(8,128)}) custom-call(bf16[1280,2048]{1,0:T(8,128)(2,1)} %bitcast.53.home, s32[128,16]{1,0:T(8,128)} %bitcast.105, f32[128,8]{1,0:T(8,128)} %bitcast.102, bf16[128,2048]{1,0:T(8,128)(2,1)} %grads.3, bf16[256,2048]{1,0:T(8,128)(2,1)} %copy-done.26), custom_call_target="tpu_custom_call" | custom-call | flops 4026531840 | bytes 12582912 | tf_op jit(solution)/shard_map/combine_pair/pallas_call | solution.py:299
  339.4 0.6 collective-permute-start.10
  339.9 3.0 collective-permute-start.11
  342.9 0.7 copy.32
  343.6 19.9 %all-to-all-done.2 = bf16[32,24,2048]{2,1,0:T(8,128)(2,1)S(1)} async-done(((bf16[32,24,2048]{2,1,0:T(8,128)(2,1)}), bf16[32,24,2048]{2,1,0:T(8,128)(2,1)S(1)}, u32[]{:S(2)}, u32[]{:S(2)}) %all-to-all-start.2) | async-done | bytes 3145760 | tf_op jit(solution)/shard_map/all_to_all | solution.py:344
  363.6 4.1 %collective-permute-done.11.dw_back = f32[128,4]{1,0:T(8,128)S(1)} collective-permute-done((f32[128,4]{1,0:T(8,128)}, f32[128,4]{1,0:T(8,128)S(1)}, u32[]{:S(2)}, u32[]{:S(2)}) %collective-permute-start.11) | collective-permute-done | bytes 2080 | tf_op jit(solution)/shard_map/ppermute | solution.py:341
  367.7 0.6 copy-done.21
  368.3 6.4 %combine_full.1 = (bf16[128,2048]{1,0:T(8,128)(2,1)}, bf16[128,2048]{1,0:T(8,128)(2,1)}, f32[128,4]{1,0:T(8,128)}) custom-call(bf16[768,2048]{1,0:T(8,128)(2,1)} %bitcast.94, s32[128,8]{1,0:T(8,128)} %bitcast.104, f32[128,8]{1,0:T(8,128)} %bitcast.103, bf16[128,2048]{1,0:T(8,128)(2,1)} %grads.3, f32[256,2048]{1,0:T(8,128)} %get-tuple-element.15.own, ...), custom_call_target="tpu_custom_call" | custom-call | flops 1207959552 | bytes 8388608 | tf_op jit(solution)/shard_map/combine_full/pallas_call | solution.py:319
  374.7 1.5 copy.35
  (66 shorter events, 0.3 us)
Async XLA Ops:
  4.6 3.7 copy-start.13
  8.3 11.9 %copy-start.22 = (s32[128,4]{0,1:T(4,128)S(1)}, s32[128,4]{0,1:T(4,128)}, u32[]{:S(2)}) copy-start(s32[128,4]{0,1:T(4,128)} %param.8) | copy-start | bytes 6148
  8.3 11.9 %copy-start.23 = (f32[128,4]{0,1:T(4,128)S(1)}, f32[128,4]{0,1:T(4,128)}, u32[]{:S(2)}) copy-start(f32[128,4]{0,1:T(4,128)} %param.9) | copy-start | bytes 6148
  8.3 12.3 %copy-start.2 = (bf16[2,2048,352]{1,2,0:T(8,128)(2,1)S(1)}, bf16[2,2048,352]{1,2,0:T(8,128)(2,1)}, u32[]{:S(2)}) copy-start(bf16[2,2048,352]{1,2,0:T(8,128)(2,1)} %param.10) | copy-start | bytes 8650756
  8.3 57.9 %all-to-all-start = ((bf16[32,32,2048]{2,1,0:T(8,128)(2,1)}), bf16[32,32,2048]{2,1,0:T(8,128)(2,1)}, u32[]{:S(2)}, u32[]{:S(2)}) async-start(bf16[32,32,2048]{2,1,0:T(8,128)(2,1)} %bitcast.93), calls=%async_computation | async-start | bytes 8388608 | tf_op jit(solution)/shard_map/all_to_all | solution.py:344
  16.3 28.3 %collective-permute-start.1 = (bf16[256,2048]{1,0:T(8,128)(2,1)}, bf16[256,2048]{1,0:T(8,128)(2,1)S(1)}, u32[]{:S(2)}, u32[]{:S(2)}) collective-permute-start(bf16[256,2048]{1,0:T(8,128)(2,1)} %copy-done.13), channel_id=1, source_target_pairs={{0,2},{1,3},{2,0},{3,1},{4,6},{5,7},{6,4},{7,5},{8,10},{9,11},{10,... | collective-permute-start | bytes 3145736 | tf_op jit(solution)/shard_map/ppermute | solution.py:341
  20.2 23.7 %collective-permute-start = (f32[8,128]{1,0:T(8,128)S(1)}, f32[8,128]{1,0:T(8,128)S(1)}, u32[]{:S(2)}, u32[]{:S(2)}) collective-permute-start(f32[8,128]{1,0:T(8,128)S(1)} %pad_maximum_fusion.5), channel_id=1, source_target_pairs={{0,2},{1,3},{2,0},{3,1},{4,6},{5,7},{6,4},{7,5},{8,10},{9,11},{10,... | collective-permute-start | bytes 12296 | tf_op jit(solution)/shard_map/ppermute | solution.py:341
  20.6 25.0 %copy-start.19 = (bf16[128,2048]{1,0:T(8,128)(2,1)S(1)}, bf16[128,2048]{1,0:T(8,128)(2,1)}, u32[]{:S(2)}) copy-start(bf16[128,2048]{1,0:T(8,128)(2,1)} %grads.3) | copy-start | bytes 1572868
  20.6 25.0 %copy-start.20 = (bf16[128,2048]{1,0:T(8,128)(2,1)S(1)}, bf16[128,2048]{1,0:T(8,128)(2,1)}, u32[]{:S(2)}) copy-start(bf16[128,2048]{1,0:T(8,128)(2,1)} %param.7) | copy-start | bytes 1572868
  44.6 1.0 copy-start.26
  66.2 67.8 %all-to-all-start.1 = ((bf16[32,24,2048]{2,1,0:T(8,128)(2,1)}), bf16[32,24,2048]{2,1,0:T(8,128)(2,1)S(1)}, u32[]{:S(2)}, u32[]{:S(2)}) async-start(bf16[32,24,2048]{2,1,0:T(8,128)(2,1)} %bitcast.99), calls=%async_computation.1 | async-start | bytes 6291456 | tf_op jit(solution)/shard_map/all_to_all | solution.py:344
  75.4 3.3 copy-start.9
  75.4 3.3 copy-start.10
  78.7 4.4 %copy-start.7 = (bf16[1,176,2048]{2,1,0:T(8,128)(2,1)S(1)}, bf16[1,176,2048]{2,1,0:T(8,128)(2,1)}, u32[]{:S(2)}) copy-start(bf16[1,176,2048]{2,1,0:T(8,128)(2,1)} %get-tuple-element.41) | copy-start | bytes 2162692
  78.7 4.4 %copy-start.8 = (bf16[1,176,2048]{2,1,0:T(8,128)(2,1)S(1)}, bf16[1,176,2048]{2,1,0:T(8,128)(2,1)}, u32[]{:S(2)}) copy-start(bf16[1,176,2048]{2,1,0:T(8,128)(2,1)} %get-tuple-element.108) | copy-start | bytes 2162692
  79.0 4.4 %copy-start.17 = (bf16[3,176,2048]{2,1,0:T(8,128)(2,1)}, bf16[3,176,2048]{2,1,0:T(8,128)(2,1)S(1)}, u32[]{:S(2)}) copy-start(bf16[3,176,2048]{2,1,0:T(8,128)(2,1)S(1)} %pad_maximum_fusion.2.refs_2_) | copy-start | bytes 6488068
  79.0 50.7 %collective-permute-start.8 = (bf16[3,176,2048]{2,1,0:T(8,128)(2,1)S(1)}, bf16[3,176,2048]{2,1,0:T(8,128)(2,1)S(1)}, u32[]{:S(2)}, u32[]{:S(2)}) collective-permute-start(bf16[3,176,2048]{2,1,0:T(8,128)(2,1)S(1)} %pad_maximum_fusion.2.refs_2_), channel_id=1, source_target_pairs={{0,3},{1,0},{2,1},{3,2},{4,7},{5,4},{6,5},{7,6},{8,11},{9,8},{10,9... | collective-permute-start | bytes 6488072 | tf_op jit(solution)/shard_map/ppermute | solution.py:341
  83.4 46.3 %copy-start.18 = (bf16[3,176,2048]{2,1,0:T(8,128)(2,1)}, bf16[3,176,2048]{2,1,0:T(8,128)(2,1)S(1)}, u32[]{:S(2)}) copy-start(bf16[3,176,2048]{2,1,0:T(8,128)(2,1)S(1)} %pad_maximum_fusion.3.refs_3_) | copy-start | bytes 6488068
  83.4 50.6 %collective-permute-start.9 = (bf16[3,176,2048]{2,1,0:T(8,128)(2,1)S(1)}, bf16[3,176,2048]{2,1,0:T(8,128)(2,1)}, u32[]{:S(2)}, u32[]{:S(2)}) collective-permute-start(bf16[3,176,2048]{2,1,0:T(8,128)(2,1)S(1)} %pad_maximum_fusion.3.refs_3_), channel_id=1, source_target_pairs={{0,1},{1,2},{2,3},{3,0},{4,5},{5,6},{6,7},{7,4},{8,9},{9,10},{10,1... | collective-permute-start | bytes 6488072 | tf_op jit(solution)/shard_map/ppermute | solution.py:341
  129.7 1.4 copy-start.25
  134.0 1.6 copy-start.1
  155.0 7.6 %copy-start.5 = (bf16[1,176,2048]{2,1,0:T(8,128)(2,1)S(1)}, bf16[1,176,2048]{2,1,0:T(8,128)(2,1)}, u32[]{:S(2)}) copy-start(bf16[1,176,2048]{2,1,0:T(8,128)(2,1)} %get-tuple-element.44) | copy-start | bytes 2162692
  155.0 7.6 %copy-start.6 = (bf16[1,176,2048]{2,1,0:T(8,128)(2,1)S(1)}, bf16[1,176,2048]{2,1,0:T(8,128)(2,1)}, u32[]{:S(2)}) copy-start(bf16[1,176,2048]{2,1,0:T(8,128)(2,1)} %get-tuple-element.105) | copy-start | bytes 2162692
  155.0 7.6 %copy-start.12 = (bf16[1,176,2048]{2,1,0:T(8,128)(2,1)S(1)}, bf16[1,176,2048]{2,1,0:T(8,128)(2,1)}, u32[]{:S(2)}) copy-start(bf16[1,176,2048]{2,1,0:T(8,128)(2,1)} %get-tuple-element.51) | copy-start | bytes 2162692
  155.0 163.9 %all-to-all-start.3 = ((bf16[32,40,2048]{2,1,0:T(8,128)(2,1)}), bf16[32,40,2048]{2,1,0:T(8,128)(2,1)}, u32[]{:S(2)}, u32[]{:S(2)}) async-start(bf16[32,40,2048]{2,1,0:T(8,128)(2,1)} %bitcast.96), calls=%async_computation.3 | async-start | bytes 10485760 | tf_op jit(solution)/shard_map/all_to_all | solution.py:344
  162.6 1.1 copy-start.3
  162.6 1.7 copy-start.4
  162.6 2.3 copy-start.11
  162.9 4.4 %copy-start.15 = (bf16[3,176,2048]{2,1,0:T(8,128)(2,1)}, bf16[3,176,2048]{2,1,0:T(8,128)(2,1)S(1)}, u32[]{:S(2)}) copy-start(bf16[3,176,2048]{2,1,0:T(8,128)(2,1)S(1)} %pad_maximum_fusion.refs_2_) | copy-start | bytes 6488068
  162.9 51.3 %collective-permute-start.2 = (bf16[3,176,2048]{2,1,0:T(8,128)(2,1)S(1)}, bf16[3,176,2048]{2,1,0:T(8,128)(2,1)}, u32[]{:S(2)}, u32[]{:S(2)}) collective-permute-start(bf16[3,176,2048]{2,1,0:T(8,128)(2,1)S(1)} %pad_maximum_fusion.refs_2_), channel_id=1, source_target_pairs={{0,1},{1,2},{2,3},{3,0},{4,5},{5,6},{6,7},{7,4},{8,9},{9,10},{10,1... | collective-permute-start | bytes 6488072 | tf_op jit(solution)/shard_map/ppermute | solution.py:341
  165.2 49.0 %copy-start.16 = (bf16[3,176,2048]{2,1,0:T(8,128)(2,1)}, bf16[3,176,2048]{2,1,0:T(8,128)(2,1)S(1)}, u32[]{:S(2)}) copy-start(bf16[3,176,2048]{2,1,0:T(8,128)(2,1)S(1)} %pad_maximum_fusion.1.refs_3_) | copy-start | bytes 6488068
  165.2 50.1 %collective-permute-start.5 = (bf16[3,176,2048]{2,1,0:T(8,128)(2,1)S(1)}, bf16[3,176,2048]{2,1,0:T(8,128)(2,1)}, u32[]{:S(2)}, u32[]{:S(2)}) collective-permute-start(bf16[3,176,2048]{2,1,0:T(8,128)(2,1)S(1)} %pad_maximum_fusion.1.refs_3_), channel_id=1, source_target_pairs={{0,3},{1,0},{2,1},{3,2},{4,7},{5,4},{6,5},{7,6},{8,11},{9,8},{10,9... | collective-permute-start | bytes 6488072 | tf_op jit(solution)/shard_map/ppermute | solution.py:341
  166.5 93.9 %collective-permute-start.3 = (bf16[3,176,2048]{2,1,0:T(8,128)(2,1)S(1)}, bf16[3,176,2048]{2,1,0:T(8,128)(2,1)S(1)}, u32[]{:S(2)}, u32[]{:S(2)}) collective-permute-start(bf16[3,176,2048]{2,1,0:T(8,128)(2,1)S(1)} %pad_maximum_fusion.1.refs_3_), channel_id=1, source_target_pairs={{0,1},{1,2},{2,3},{3,0},{4,5},{5,6},{6,7},{7,4},{8,9},{9,10},{10,1... | collective-permute-start | bytes 6488072 | tf_op jit(solution)/shard_map/ppermute | solution.py:341
  167.3 94.5 %collective-permute-start.4 = (bf16[3,176,2048]{2,1,0:T(8,128)(2,1)S(1)}, bf16[3,176,2048]{2,1,0:T(8,128)(2,1)}, u32[]{:S(2)}, u32[]{:S(2)}) collective-permute-start(bf16[3,176,2048]{2,1,0:T(8,128)(2,1)S(1)} %pad_maximum_fusion.refs_2_), channel_id=1, source_target_pairs={{0,3},{1,0},{2,1},{3,2},{4,7},{5,4},{6,5},{7,6},{8,11},{9,8},{10,9... | collective-permute-start | bytes 6488072 | tf_op jit(solution)/shard_map/ppermute | solution.py:341
  214.2 91.7 %collective-permute-start.6 = (bf16[3,176,2048]{2,1,0:T(8,128)(2,1)}, bf16[3,176,2048]{2,1,0:T(8,128)(2,1)S(1)}, u32[]{:S(2)}, u32[]{:S(2)}) collective-permute-start(bf16[3,176,2048]{2,1,0:T(8,128)(2,1)} %collective-permute-done.2.refs_4_), channel_id=1, source_target_pairs={{0,1},{1,2},{2,3},{3,0},{4,5},{5,6},{6,7},{7,4},{8,9},{9,10},{10,1... | collective-permute-start | bytes 6488072 | tf_op jit(solution)/shard_map/ppermute | solution.py:341
  215.3 91.8 %collective-permute-start.7 = (bf16[3,176,2048]{2,1,0:T(8,128)(2,1)}, bf16[3,176,2048]{2,1,0:T(8,128)(2,1)}, u32[]{:S(2)}, u32[]{:S(2)}) collective-permute-start(bf16[3,176,2048]{2,1,0:T(8,128)(2,1)} %collective-permute-done.5.refs_7_), channel_id=1, source_target_pairs={{0,3},{1,0},{2,1},{3,2},{4,7},{5,4},{6,5},{7,6},{8,11},{9,8},{10,9... | collective-permute-start | bytes 6488072 | tf_op jit(solution)/shard_map/ppermute | solution.py:341
  260.4 1.4 copy-start.24
  305.9 1.3 copy-start.14
  318.9 44.7 %all-to-all-start.2 = ((bf16[32,24,2048]{2,1,0:T(8,128)(2,1)}), bf16[32,24,2048]{2,1,0:T(8,128)(2,1)S(1)}, u32[]{:S(2)}, u32[]{:S(2)}) async-start(bf16[32,24,2048]{2,1,0:T(8,128)(2,1)} %bitcast.95), calls=%async_computation.2 | async-start | bytes 6291456 | tf_op jit(solution)/shard_map/all_to_all | solution.py:344
  339.4 28.3 %collective-permute-start.10 = (bf16[256,2048]{1,0:T(8,128)(2,1)}, bf16[256,2048]{1,0:T(8,128)(2,1)}, u32[]{:S(2)}, u32[]{:S(2)}) collective-permute-start(bf16[256,2048]{1,0:T(8,128)(2,1)} %get-tuple-element.16), channel_id=1, source_target_pairs={{0,2},{1,3},{2,0},{3,1},{4,6},{5,7},{6,4},{7,5},{8,10},{9,11},{10,... | collective-permute-start | bytes 3145736 | tf_op jit(solution)/shard_map/ppermute | solution.py:341
  339.9 27.7 %collective-permute-start.11 = (f32[128,4]{1,0:T(8,128)}, f32[128,4]{1,0:T(8,128)S(1)}, u32[]{:S(2)}, u32[]{:S(2)}) collective-permute-start(f32[128,4]{1,0:T(8,128)} %get-tuple-element.18), channel_id=1, source_target_pairs={{0,2},{1,3},{2,0},{3,1},{4,6},{5,7},{6,4},{7,5},{8,10},{9,11},{10,... | collective-permute-start | bytes 6152 | tf_op jit(solution)/shard_map/ppermute | solution.py:341
  363.6 4.1 %copy-start = (bf16[32,24,2048]{2,1,0:T(8,128)(2,1)}, bf16[32,24,2048]{2,1,0:T(8,128)(2,1)S(1)}, u32[]{:S(2)}) copy-start(bf16[32,24,2048]{2,1,0:T(8,128)(2,1)S(1)} %all-to-all-done.2) | copy-start | bytes 9437188
  367.7 0.6 copy-start.21

commit v2 on v1

--- a/solution.py
+++ b/solution.py
@@ -20,23 +20,79 @@
 
 def slots_of(route_t):
     toks = route_t.shape[1]
-    expert_ids = jnp.arange(EXPERTS, dtype=jnp.int32)[:, None]
-    hits = [(route_t[k][None, :] == expert_ids) for k in range(TOP)]
-    named = sum(h.astype(BF) for h in hits)
-    before = (
-        jnp.arange(toks, dtype=jnp.int32)[:, None] < jnp.arange(toks, dtype=jnp.int32)[None, :]
-    ).astype(BF)
+    expert_ids = lax.broadcasted_iota(jnp.int32, (EXPERTS, toks), 0)
+    hits = [(route_t[k : k + 1] == expert_ids) for k in range(TOP)]
+    named = sum(jnp.where(h, 1.0, 0.0) for h in hits).astype(BF)
+    from_ids = lax.broadcasted_iota(jnp.int32, (toks, toks), 0)
+    to_ids = lax.broadcasted_iota(jnp.int32, (toks, toks), 1)
+    before = jnp.where(from_ids < to_ids, 1.0, 0.0).astype(BF)
     earlier = jnp.dot(named, before, preferred_element_type=F32)
-    slots = [jnp.sum(jnp.where(h, earlier, 0.0), axis=0) for h in hits]
-    return jnp.stack(slots).astype(jnp.int32)
-
-
-def one_hot_rows(row_t, rows):
-    ids = jnp.arange(rows, dtype=jnp.int32)[:, None]
-    total = 0
-    for k in range(TOP):
-        total = total + jnp.where(row_t[k][None, :] == ids, 1.0, 0.0)
+    slots = [jnp.sum(jnp.where(h, earlier, 0.0), axis=0, keepdims=True) for h in hits]
+    return jnp.concatenate(slots, axis=0).astype(jnp.int32)
+
+
+def dispatch_rows(pairs, block, first):
+    total = None
+    for places, values in pairs:
+        ids = lax.broadcasted_iota(jnp.int32, (block, places.shape[1]), 0) + first
+        hot = jnp.zeros(ids.shape, F32)
+        for k in range(TOP):
+            hot = hot + jnp.where(places[k : k + 1] == ids, 1.0, 0.0)
+        term = jnp.dot(hot.astype(BF), values, preferred_element_type=F32)
+        total = term if total is None else total + term
     return total.astype(BF)
+
+
+def dispatch_own_kernel(route_ref, tokens, grads, rows):
+    block = rows.shape[0]
+    first = pl.program_id(0) * block
+    route = route_ref[...]
+    slot = slots_of(route)
+    base = (route // 2) * OWN_ROWS + (route % 2) * 16 + slot
+    kept = slot < 8
+    x_place, g_place = jnp.where(kept, base, -1), jnp.where(kept, base + 8, -1)
+    rows[...] = dispatch_rows([(x_place, tokens[...]), (g_place, grads[...])], block, first)
+
+
+def dispatch_other_kernel(route_ref, route_other_ref, tokens, grads, tokens_other, grads_other, rows):
+    block = rows.shape[0]
+    first = pl.program_id(0) * block
+    route = route_ref[...]
+    odd = route % 2
+    ninth = slots_of(route) == 8
+    base = (route // 2) * OTHER_ROWS
+    x_place = jnp.where(ninth, base + 16 + 4 * odd, -1)
+    g_place = jnp.where(ninth, base + 18 + 3 * odd, -1)
+    route = route_other_ref[...]
+    even = route % 2 == 0
+    slot = slots_of(route)
+    base = (route // 2) * OTHER_ROWS
+    x_far = jnp.where(even, base + jnp.where(slot < 8, slot, 17), -1)
+    g_far = jnp.where(even, base + jnp.where(slot < 8, slot + 8, 19), -1)
+    rows[...] = dispatch_rows(
+        [(x_place, tokens[...]), (g_place, grads[...]), (x_far, tokens_other[...]), (g_far, grads_other[...])],
+        block,
+        first,
+    )
+
+
+def dispatch(kernel, rows, *args):
+    width = args[-1].shape[1]
+    steps = 4
+
+    def whole(x):
+        return pl.BlockSpec(x.shape, lambda i: (0, 0))
+
+    return pl.pallas_call(
+        kernel,
+        grid=(steps,),
+        out_shape=jax.ShapeDtypeStruct((rows, width), BF),
+        in_specs=[whole(x) for x in args],
+        out_specs=pl.BlockSpec((rows // steps, width), lambda i: (i, 0)),
+        cost_estimate=pl.CostEstimate(
+            flops=4 * rows * 128 * width, transcendentals=0, bytes_accessed=4 * rows * width
+        ),
+    )(*args)
 
 
 def landed(dst, sem):
@@ -157,22 +213,37 @@
     landed(wg, sems.at[3])
     landed(wu, sems.at[4])
     landed(wd, sems.at[5])
+    size = (main + small) // 2
+
+    def block(b, carry):
+        at = pl.ds(pl.multiple_of(b * size, 16), size)
+        hidden, d_gate, d_up = inner(xs[at], gs[at], wg[...], wu[...], wd[...])
+        out_part[at] = by_row(hidden, wd[...])
+        back_part[at] = by_row(d_gate, wg[...]) + by_row(d_up, wu[...])
+        return carry
+
+    lax.fori_loop(0, 2, block, 0)
+
+
+def expert_far_kernel(nodes, n_pieces, *refs):
+    near, pieces, home = refs[:4], refs[4 : 4 + n_pieces], refs[4 + n_pieces]
+    xs, gs, out_part, back_part, wg, wu, wd, outs, backs, out_rest, sems = refs[5 + n_pieces :]
+    main, small = nodes * 8, nodes
+    pltpu.make_async_copy(near[0], xs, sems.at[6]).start()
+    fetch_weights(pieces, (wg, wu, wd), sems, 3)
+    pltpu.make_async_copy(near[1], gs, sems.at[7]).start()
+    pltpu.make_async_copy(near[2], out_part, sems.at[8]).start()
+    pltpu.make_async_copy(near[3], back_part, sems.at[9]).start()
+    landed(xs, sems.at[6])
+    landed(wg, sems.at[3])
+    landed(wu, sems.at[4])
+    landed(wd, sems.at[5])
+    landed(gs, sems.at[7])
     hidden, d_gate, d_up = inner(xs[...], gs[...], wg[...], wu[...], wd[...])
-    out_part[...] = by_row(hidden, wd[...])
-    back_part[...] = by_row(d_gate, wg[...]) + by_row(d_up, wu[...])
-
-
-def expert_far_kernel(nodes, n_pieces, *refs):
-    xs, gs, out_part, back_part = refs[:4]
-    pieces, home = refs[4 : 4 + n_pieces], refs[4 + n_pieces]
-    wg, wu, wd, outs, backs, out_rest, sems = refs[5 + n_pieces :]
-    main, small = nodes * 8, nodes
-    fetch_weights(pieces, (wg, wu, wd), sems, 3)
-    for j, w in enumerate((wg, wu, wd)):
-        landed(w, sems.at[3 + j])
-    hidden, d_gate, d_up = inner(xs[...], gs[...], wg[...], wu[...], wd[...])
+    landed(out_part, sems.at[8])
     outs[...] = (by_row(hidden, wd[...]) + out_part[...]).astype(BF)
     put_rows(nodes, outs, 0, home, OUT1_ROWS, 0, sems.at[0])
+    landed(back_part, sems.at[9])
     backs[...] = (by_row(d_gate, wg[...]) + by_row(d_up, wu[...]) + back_part[...]).astype(BF)
     put_rows(nodes, backs, 0, home, OUT1_ROWS, 8, sems.at[1])
     out_rest[...] = (
@@ -185,7 +256,7 @@
     landed(out_rest, sems.at[2])
 
 
-ANY = pl.BlockSpec(memory_space=pl.ANY)
+ANY = pl.BlockSpec(memory_space=pltpu.HBM)
 WHOLE = pl.BlockSpec(memory_space=pltpu.VMEM)
 PARAMS = pltpu.CompilerParams(vmem_limit_bytes=60 * 1024 * 1024)
 
@@ -235,83 +306,74 @@
     out_part, back_part, xs, gs = near
     rows, width = xs.shape
     hidden = len(pieces) * pieces[0].shape[1]
-    scratch = [(hidden, width)] * 3 + [(rows, width), (rows, width), (nodes * 8, width)]
+    scratch = [((rows, width), BF)] * 2 + [((rows, width), F32)] * 2 + [((hidden, width), BF)] * 3
+    scratch += [((rows, width), BF)] * 2 + [((nodes * 8, width), BF)]
     return pl.pallas_call(
         functools.partial(expert_far_kernel, nodes, len(pieces)),
         name="expert_far",
         out_shape=jax.ShapeDtypeStruct((nodes * OUT1_ROWS, width), BF),
-        in_specs=[WHOLE] * 4 + [ANY] * len(pieces),
+        in_specs=[ANY] * (4 + len(pieces)),
         out_specs=ANY,
-        scratch_shapes=[pltpu.VMEM(s, BF) for s in scratch] + [pltpu.SemaphoreType.DMA((6,))],
+        scratch_shapes=[pltpu.VMEM(s, t) for s, t in scratch] + [pltpu.SemaphoreType.DMA((10,))],
         compiler_params=PARAMS,
         cost_estimate=expert_cost(rows, hidden, width),
     )(xs, gs, out_part, back_part, *pieces)
 
 
-def mixed(rows_ref, places, first, values, ids):
-    total = 0.0
+def mixed(rows, places, values):
+    ids = lax.broadcasted_iota(jnp.int32, (places.shape[0], rows.shape[0]), 1)
+    total = jnp.zeros(ids.shape, F32)
     for k in range(TOP):
-        total = total + jnp.where(places[:, first + k : first + k + 1] == ids, values[:, k : k + 1], 0.0)
-    return jnp.dot(total.astype(BF), rows_ref[...], preferred_element_type=F32)
-
-
-def weight_grads(rows_ref, grads, places, first, ids):
-    table = lax.dot_general(grads, rows_ref[...], (((1,), (1,)), ((), ())), preferred_element_type=F32)
-    return jnp.concatenate(
-        [
-            jnp.sum(jnp.where(places[:, first + k : first + k + 1] == ids, table, 0.0), axis=1, keepdims=True)
-            for k in range(TOP)
-        ],
-        axis=1,
-    )
+        total = total + jnp.where(places[:, k : k + 1] == ids, values[:, k : k + 1], 0.0)
+    return jnp.dot(total.astype(BF), rows, preferred_element_type=F32)
+
+
+def weight_grads(rows, grads, places):
+    table = lax.dot_general(grads, rows, (((1,), (1,)), ((), ())), preferred_element_type=F32)
+    ids = lax.broadcasted_iota(jnp.int32, table.shape, 1)
+    lane = lax.broadcasted_iota(jnp.int32, (table.shape[0], 128), 1)
+    result = jnp.zeros(lane.shape, F32)
+    for k in range(TOP):
+        column = jnp.sum(jnp.where(places[:, k : k + 1] == ids, table, 0.0), axis=1, keepdims=True)
+        result = result + jnp.where(lane == k, column, 0.0)
+    return result
 
 
 def combine_pair_kernel(home, places_ref, values_ref, grads, grads_other, back, own, dw_other, dw_own):
     toks = grads.shape[0]
-    ids = lax.broadcasted_iota(jnp.int32, (toks, home.shape[0]), 1)
-    places = places_ref[...]
-    values, values_other = values_ref[:, :TOP], values_ref[:, TOP:]
-    back[:toks] = mixed(home, places, 2 * TOP, values_other, ids).astype(BF)
-    back[toks:] = mixed(home, places, 3 * TOP, values_other, ids).astype(BF)
-    dw_other[...] = weight_grads(home, grads_other[...], places, 2 * TOP, ids)
-    own[:toks] = mixed(home, places, 0, values, ids)
-    own[toks:] = mixed(home, places, TOP, values, ids)
-    dw_own[...] = weight_grads(home, grads[...], places, 0, ids)
+    rows = home[...]
+    total = mixed(rows, places_ref[...], values_ref[...])
+    back[...] = total[: 2 * toks].astype(BF)
+    own[...] = total[2 * toks :]
+    dw_other[...] = jnp.transpose(weight_grads(rows, grads_other[...], places_ref[:toks]))[:8]
+    dw_own[...] = jnp.transpose(weight_grads(rows, grads[...], places_ref[2 * toks : 3 * toks]))[:8]
 
 
 def combine_full_kernel(home, places_ref, values_ref, grads, own, returned, dw_own, dw_back, combined, d_tokens, d_weights):
     toks = grads.shape[0]
-    ids = lax.broadcasted_iota(jnp.int32, (toks, home.shape[0]), 1)
-    places = places_ref[...]
-    values = values_ref[:, :TOP]
-    combined[...] = (
-        mixed(home, places, 0, values, ids) + own[:toks] + returned[:toks].astype(F32)
-    ).astype(BF)
-    d_tokens[...] = (
-        mixed(home, places, TOP, values, ids) + own[toks:] + returned[toks:].astype(F32)
-    ).astype(BF)
-    d_weights[...] = weight_grads(home, grads[...], places, 0, ids) + dw_own[...] + dw_back[...]
-
-
-def combine_pair(home, places, values, grads, other):
+    rows = home[...]
+    total = mixed(rows, places_ref[...], values_ref[...]) + own[...] + returned[...].astype(F32)
+    combined[...] = total[:toks].astype(BF)
+    d_tokens[...] = total[toks:].astype(BF)
+    dw = jnp.transpose(weight_grads(rows, grads[...], places_ref[:toks]))[:8] + dw_own[...] + dw_back[...]
+    d_weights[...] = dw[:TOP]
+
+
+def combine_pair(home, places, values, grads, grads_other):
     toks, width = grads.shape
-    whole = pl.BlockSpec(memory_space=pltpu.VMEM)
     return pl.pallas_call(
         combine_pair_kernel,
         name="combine_pair",
-        grid=(1,),
         out_shape=(
             jax.ShapeDtypeStruct((2 * toks, width), BF),
             jax.ShapeDtypeStruct((2 * toks, width), F32),
-            jax.ShapeDtypeStruct((toks, TOP), F32),
-            jax.ShapeDtypeStruct((toks, TOP), F32),
-        ),
-        in_specs=[whole] * 4 + [pl.BlockSpec((toks, width), lambda i: (1, 0))],
-        out_specs=(whole,) * 4,
+            jax.ShapeDtypeStruct((8, toks), F32),
+            jax.ShapeDtypeStruct((8, toks), F32),
+        ),
         cost_estimate=pl.CostEstimate(
             flops=12 * toks * home.shape[0] * width, transcendentals=0, bytes_accessed=12 * 1024 * 1024
         ),
-    )(home, places, values, grads, other)
+    )(home, places, values, grads, grads_other)
 
 
 def combine_full(home, places, values, grads, own, returned, dw_own, dw_back):
@@ -322,7 +384,7 @@
         out_shape=(
             jax.ShapeDtypeStruct((toks, width), BF),
             jax.ShapeDtypeStruct((toks, width), BF),
-            jax.ShapeDtypeStruct((toks, TOP), F32),
+            jax.ShapeDtypeStruct((TOP, toks), F32),
         ),
         cost_estimate=pl.CostEstimate(
             flops=6 * toks * home.shape[0] * width, transcendentals=0, bytes_accessed=8 * 1024 * 1024
@@ -333,6 +395,7 @@
 def shards(tokens, route, combine_weights, w_gate, w_up, w_down, grad_out):
     nodes = lax.axis_size("node")
     planes = lax.axis_size("local")
+    toks, _ = tokens.shape
     up = [(i, (i + 1) % planes) for i in range(planes)]
     down = [(i, (i - 1) % planes) for i in range(planes)]
     across = [(i, (i + 2) % planes) for i in range(planes)]
@@ -343,8 +406,7 @@
     def exchange(rows):
         return lax.all_to_all(rows, "node", split_axis=0, concat_axis=0, tiled=True)
 
-    own = jnp.concatenate([tokens, grad_out], axis=0)
-    other = send(own, across)
+    tokens_other, grads_other = send(tokens, across), send(grad_out, across)
     route_t = route.T
     weight_t = combine_weights.T
     small = send(jnp.concatenate([weight_t, route_t.astype(F32)], axis=0), across)
@@ -368,49 +430,11 @@
 
     slot_own, slot_other = slots_of(route_t), slots_of(route_other)
 
-    def places(route_rows, row, keep):
-        chunk, index = row
-        return jnp.where(keep, (route_rows // 2) * chunk + index, -1)
-
-    own_even, other_even = route_t % 2 == 0, route_other % 2 == 0
-    own_main, other_main = slot_own < 8, slot_other < 8
-
-    def own_place(first_even, first_odd):
-        index = jnp.where(own_even, first_even, first_odd) + slot_own
-        return places(route_t, (OWN_ROWS, index), own_main)
-
-    def rest_place(even, odd):
-        return places(route_t, (OTHER_ROWS, jnp.where(own_even, even, odd)), ~own_main)
-
-    def other_place(main, rest, chunk):
-        index = jnp.where(other_main, main + slot_other, rest)
-        return places(route_other, (chunk, index), other_even)
-
-    own_rows = jnp.dot(
-        jnp.concatenate(
-            [
-                one_hot_rows(own_place(0, 16), nodes * OWN_ROWS),
-                one_hot_rows(own_place(8, 24), nodes * OWN_ROWS),
-            ],
-            axis=1,
-        ),
-        own,
-        preferred_element_type=F32,
-    ).astype(BF)
+    own_rows = dispatch(dispatch_own_kernel, nodes * OWN_ROWS, route_t, tokens, grad_out)
     arrived = exchange(own_rows)
-    other_rows = jnp.dot(
-        jnp.concatenate(
-            [
-                one_hot_rows(rest_place(16, 20), nodes * OTHER_ROWS),
-                one_hot_rows(rest_place(18, 21), nodes * OTHER_ROWS),
-                one_hot_rows(other_place(0, 17, OTHER_ROWS), nodes * OTHER_ROWS),
-                one_hot_rows(other_place(8, 19, OTHER_ROWS), nodes * OTHER_ROWS),
-            ],
-            axis=1,
-        ),
-        jnp.concatenate([own, other], axis=0),
-        preferred_element_type=F32,
-    ).astype(BF)
+    other_rows = dispatch(
+        dispatch_other_kernel, nodes * OTHER_ROWS, route_t, route_other, tokens, grad_out, tokens_other, grads_other
+    )
     arrived_other = exchange(other_rows)
 
     rows0 = expert_pair(arrived, arrived_other, w0, nodes)
@@ -419,29 +443,36 @@
     rows1 = expert_far(near, w1[6:], nodes)
     home1 = exchange(rows1)
 
+    own_even, other_even = route_t % 2 == 0, route_other % 2 == 0
+
+    def places(route_rows, row, keep):
+        chunk, index = row
+        return jnp.where(keep, (route_rows // 2) * chunk + index, -1)
+
+    def other_place(main, rest):
+        index = jnp.where(slot_other < 8, main + slot_other, rest)
+        return places(route_other, (OUT0_ROWS, index), other_even)
+
     def home_place(main, rest):
-        index = jnp.where(own_main, main + slot_own, rest)
+        index = jnp.where(slot_own < 8, main + slot_own, rest)
         return places(route_t, (OUT0_ROWS, index), own_even)
 
     def full_place(main, rest):
-        index = jnp.where(own_main, main + slot_own, rest)
+        index = jnp.where(slot_own < 8, main + slot_own, rest)
         return places(route_t, (OUT1_ROWS, index), ~own_even)
 
-    places0 = jnp.concatenate(
-        [
-            home_place(0, 32),
-            home_place(16, 34),
-            other_place(8, 33, OUT0_ROWS),
-            other_place(24, 35, OUT0_ROWS),
-        ],
-        axis=0,
-    ).T
-    places1 = jnp.concatenate([full_place(0, 16), full_place(8, 17)], axis=0).T
-    values = jnp.concatenate([weight_t, weight_other], axis=0).T
-    back, kept, dw_other, dw_own = combine_pair(home0, places0, values, grad_out, other)
+    def stacked(*parts):
+        return jnp.concatenate([p.T for p in parts], axis=0)
+
+    places0 = stacked(other_place(8, 33), other_place(24, 35), home_place(0, 32), home_place(16, 34))
+    places1 = stacked(full_place(0, 16), full_place(8, 17))
+    values0 = stacked(weight_other, weight_other, weight_t, weight_t)
+    values1 = values0[2 * toks :]
+    back, kept, dw_other, dw_own = combine_pair(home0, places0, values0, grad_out, grads_other)
     returned = send(back, across)
     dw_back = send(dw_other, across)
-    return combine_full(home1, places1, values, grad_out, kept, returned, dw_own, dw_back)
+    combined, d_tokens, d_weights_t = combine_full(home1, places1, values1, grad_out, kept, returned, dw_own, dw_back)
+    return combined, d_tokens, d_weights_t.T
 
 
 def solution(mesh):

time: 383 us -> 388 us (1.013); the launches traced: 376 us -> 386 us
  Pallas kernels: 65.6 us -> 80.7 us
  matrix products: 7.06 us -> 0.33 us
  local copies, waits for them, and re-layouts: 22.7 us -> 16.1 us
  starting transfers between devices: 52 us -> 56.2 us
    pallas_call x1 -> x3, Pallas kernels: 11.2 us -> 24.4 us  [the longest x2 12.7 us: dispatch(): pl.pallas_call(kernel, grid=(steps,), out_shape=jax.ShapeDtypeStruct((row...]
    all_to_all x4, waiting for transfers between devices: 37.2 us -> 49.4 us  [exchange(): return lax.all_to_all(rows, 'node', split_axis=0, concat_axis=0, tiled=True)]
    ppermute x12 -> x13, waiting for transfers between devices: 188 us -> 178 us  [send(): return lax.ppermute(value, 'local', pairs)]
    dot_general x2 -> x0, matrix products: 6.73 us -> none  [the longest x1 3.48 us: shards(): jnp.dot(jnp.concatenate([one_hot_rows(rest_place(16, 20), nodes * OTHER_R...]
    ppermute x12 -> x13, starting transfers between devices: 19.5 us -> 25.7 us  [send(): return lax.ppermute(value, 'local', pairs)]
    pallas_call x1, Pallas kernels: 17.1 us -> 21.2 us  [expert_near(): pl.pallas_call(functools.partial(expert_near_kernel, nodes, len(pieces)),...]
    unnamed x55 -> x34, local copies, waits for them, and re-layouts: 9.22 us -> 8.83 us
  transfers between devices with their start and end apart: 16 -> 17, of which waited for: 11 -> 8; matrix products, arithmetic and copies ran while one was open for 4% -> 3% of each run, Pallas kernels for 11% -> 12%
where the time goes in v2:
time: 388 us; the launch traced here: 386 us
  waiting for transfers between devices  228 us (59%)
  Pallas kernels  80.7 us (21%)
  starting transfers between devices  56.2 us (14%)
  local copies, waits for them, and re-layouts  16.1 us (4%)
  other arithmetic  4.28 us (1%)
    ppermute x13, waiting for transfers between devices, send(): return lax.ppermute(value, 'local', pairs)  178 us
    all_to_all x4, waiting for transfers between devices, exchange(): return lax.all_to_all(rows, 'node', split_axis=0, concat_axis=0, tiled=True)  49.4 us
    all_to_all x4, starting transfers between devices, exchange(): return lax.all_to_all(rows, 'node', split_axis=0, concat_axis=0, tiled=True)  30.5 us
    ppermute x13, starting transfers between devices, send(): return lax.ppermute(value, 'local', pairs)  25.7 us
    pallas_call x1, Pallas kernels, expert_near(): pl.pallas_call(functools.partial(expert_near_kernel, nodes, len(pieces)),...  21.2 us
    pallas_call x1, Pallas kernels, expert_pair(): pl.pallas_call(functools.partial(expert_pair_kernel, nodes, len(pieces)),...  19.3 us
    pallas_call x2, Pallas kernels, dispatch(): pl.pallas_call(kernel, grid=(steps,), out_shape=jax.ShapeDtypeStruct((row...  12.7 us
    pallas_call x1, Pallas kernels, combine_pair(): pl.pallas_call(combine_pair_kernel, name='combine_pair', out_shape=(jax.S...  11.6 us
  transfers between devices with their start and end apart: 17, of which 8 were waited for; matrix products, arithmetic and copies ran while one was open for 3% of the time, Pallas kernels for 12%

profile of v2, /device:TPU:2, one launch (start us, length us, event | category | flops | bytes accessed | tf_op | source)
XLA Modules:
  0.0 386.3 jit_solution(14912763055187201370)
XLA Ops:
  0.6 4.0 %collective-permute-start.2 = (bf16[128,2048]{1,0:T(8,128)(2,1)}, bf16[128,2048]{1,0:T(8,128)(2,1)S(1)}, u32[]{:S(2)}, u32[]{:S(2)}) collective-permute-start(bf16[128,2048]{1,0:T(8,128)(2,1)} %grads.7), channel_id=1, source_target_pairs={{0,2},{1,3},{2,0},{3,1},{4,6},{5,7},{6,4},{7,5},{8,10},{9,11},{10,... | collective-permute-start | bytes 1572872 | tf_op jit(solution)/shard_map/ppermute | solution.py:404
  4.6 0.1 collective-permute-start.1
  4.7 0.7 bitcast_convert_fusion
  5.4 0.7 pad_maximum_fusion.5
  6.1 3.4 collective-permute-start
  9.5 18.6 %collective-permute-done = f32[8,128]{1,0:T(8,128)S(1)} collective-permute-done((f32[8,128]{1,0:T(8,128)S(1)}, f32[8,128]{1,0:T(8,128)S(1)}, u32[]{:S(2)}, u32[]{:S(2)}) %collective-permute-start) | collective-permute-done | bytes 4128 | tf_op jit(solution)/shard_map/ppermute | solution.py:404
  28.0 0.6 slice_bitcast_fusion
  28.6 0.0 collective-permute-done.2.grads_other
  28.6 0.0 collective-permute-done.1.tokens_other
  28.6 0.0 copy-start.10
  28.7 0.8 copy-done.9
  29.4 0.2 copy-done.10
  29.6 6.9 %shard_map.95 = bf16[768,2048]{1,0:T(8,128)(2,1)} custom-call(s32[4,128]{1,0:T(4,128)} %bitcast.79, s32[4,128]{1,0:T(4,128)} %get-tuple-element.48.route_other_ref, bf16[128,2048]{1,0:T(8,128)(2,1)} %tokens.3, bf16[128,2048]{1,0:T(8,128)(2,1)} %grads.7, bf16[128,2048]{1,0:T(8,128)(2,1)} %copy-done.10, bf16[128,2048]{1,0:T(8,128)(2,1)} %copy-done.9), custom_call_target="tpu_custom_call" | custom-call | flops 805306368 | bytes 6291456 | tf_op jit(solution)/shard_map/pallas_call | solution.py:86
  36.5 7.6 %all-to-all-start.1 = ((bf16[32,24,2048]{2,1,0:T(8,128)(2,1)}), bf16[32,24,2048]{2,1,0:T(8,128)(2,1)S(1)}, u32[]{:S(2)}, u32[]{:S(2)}) async-start(bf16[32,24,2048]{2,1,0:T(8,128)(2,1)} %bitcast.73), calls=%async_computation.1 | async-start | bytes 6291456 | tf_op jit(solution)/shard_map/all_to_all | solution.py:407
  44.2 5.8 %shard_map.94 = bf16[1024,2048]{1,0:T(8,128)(2,1)} custom-call(s32[4,128]{1,0:T(4,128)} %bitcast.80, bf16[128,2048]{1,0:T(8,128)(2,1)} %tokens.3, bf16[128,2048]{1,0:T(8,128)(2,1)} %grads.7), custom_call_target="tpu_custom_call" | custom-call | flops 1073741824 | bytes 8388608 | tf_op jit(solution)/shard_map/pallas_call | solution.py:86
  50.0 31.3 %all-to-all-done.1 = bf16[32,24,2048]{2,1,0:T(8,128)(2,1)S(1)} async-done(((bf16[32,24,2048]{2,1,0:T(8,128)(2,1)}), bf16[32,24,2048]{2,1,0:T(8,128)(2,1)S(1)}, u32[]{:S(2)}, u32[]{:S(2)}) %all-to-all-start.1) | async-done | bytes 3145760 | tf_op jit(solution)/shard_map/all_to_all | solution.py:407
  81.2 1.7 copy-done.1
  82.9 7.8 %all-to-all-start = ((bf16[32,32,2048]{2,1,0:T(8,128)(2,1)}), bf16[32,32,2048]{2,1,0:T(8,128)(2,1)}, u32[]{:S(2)}, u32[]{:S(2)}) async-start(bf16[32,32,2048]{2,1,0:T(8,128)(2,1)} %bitcast.70), calls=%async_computation | async-start | bytes 8388608 | tf_op jit(solution)/shard_map/all_to_all | solution.py:407
  90.7 0.0 copy-start.2
  90.7 0.0 copy-start.3
  90.8 2.1 fusion.29
  92.9 0.5 copy-done.2
  93.4 0.9 copy-done.3
  94.3 1.8 fusion.27
  96.1 0.2 pad_maximum_fusion.3.refs_3_
  96.4 1.3 collective-permute-start.10
  97.7 0.2 pad_maximum_fusion.2.refs_2_
  98.0 3.2 collective-permute-start.9
  101.2 46.0 %collective-permute-done.10.refs_5_ = bf16[3,176,2048]{2,1,0:T(8,128)(2,1)S(1)} collective-permute-done((bf16[3,176,2048]{2,1,0:T(8,128)(2,1)S(1)}, bf16[3,176,2048]{2,1,0:T(8,128)(2,1)S(1)}, u32[]{:S(2)}, u32[]{:S(2)}) %collective-permute-start.10) | collective-permute-done | bytes 2162720 | tf_op jit(solution)/shard_map/ppermute | solution.py:404
  147.2 1.4 copy-done.16
  148.6 0.0 collective-permute-done.9.refs_4_
  148.6 0.0 all-to-all-done
  148.6 19.3 %expert_pair.1 = bf16[1280,2048]{1,0:T(8,128)(2,1)} custom-call(bf16[1024,2048]{1,0:T(8,128)(2,1)} %bitcast.2.refs_0_, bf16[768,2048]{1,0:T(8,128)(2,1)} %bitcast.75, bf16[3,176,2048]{2,1,0:T(8,128)(2,1)} %copy-done.8, bf16[3,176,2048]{2,1,0:T(8,128)(2,1)} %copy-done.7, bf16[3,176,2048]{2,1,0:T(8,128)(2,1)} %collective-permute-done.9.refs_4_, ...), custom_call_target="tpu_custom_call" | custom-call | flops 9965666304 | bytes 18087936 | tf_op jit(solution)/shard_map/expert_pair/pallas_call | solution.py:277
  167.9 7.5 %all-to-all-start.3 = ((bf16[32,40,2048]{2,1,0:T(8,128)(2,1)}), bf16[32,40,2048]{2,1,0:T(8,128)(2,1)}, u32[]{:S(2)}, u32[]{:S(2)}) async-start(bf16[32,40,2048]{2,1,0:T(8,128)(2,1)} %bitcast.74), calls=%async_computation.3 | async-start | bytes 10485760 | tf_op jit(solution)/shard_map/all_to_all | solution.py:407
  175.4 1.6 pad_maximum_fusion.refs_2_
  177.0 0.4 collective-permute-start.3
  177.4 0.2 pad_maximum_fusion.1.refs_3_
  177.6 3.0 collective-permute-start.6
  180.6 3.2 collective-permute-start.5
  183.9 44.4 %collective-permute-done.3.refs_4_ = bf16[3,176,2048]{2,1,0:T(8,128)(2,1)} collective-permute-done((bf16[3,176,2048]{2,1,0:T(8,128)(2,1)S(1)}, bf16[3,176,2048]{2,1,0:T(8,128)(2,1)}, u32[]{:S(2)}, u32[]{:S(2)}) %collective-permute-start.3) | collective-permute-done | bytes 2162720 | tf_op jit(solution)/shard_map/ppermute | solution.py:404
  228.3 3.5 collective-permute-start.8
  231.9 42.7 %collective-permute-done.4.refs_5_ = bf16[3,176,2048]{2,1,0:T(8,128)(2,1)S(1)} collective-permute-done((bf16[3,176,2048]{2,1,0:T(8,128)(2,1)S(1)}, bf16[3,176,2048]{2,1,0:T(8,128)(2,1)S(1)}, u32[]{:S(2)}, u32[]{:S(2)}) %collective-permute-start.4) | collective-permute-done | bytes 2162720 | tf_op jit(solution)/shard_map/ppermute | solution.py:404
  274.6 1.4 copy-done.15
  276.0 21.2 %expert_near.1 = (f32[288,2048]{1,0:T(8,128)}, f32[288,2048]{1,0:T(8,128)}, bf16[288,2048]{1,0:T(8,128)(2,1)}, bf16[288,2048]{1,0:T(8,128)(2,1)}) custom-call(bf16[1024,2048]{1,0:T(8,128)(2,1)} %bitcast.2.refs_0_, bf16[768,2048]{1,0:T(8,128)(2,1)} %bitcast.76, bf16[3,176,2048]{2,1,0:T(8,128)(2,1)} %copy-done.5, bf16[3,176,2048]{2,1,0:T(8,128)(2,1)} %copy-done.6, ...), custom_call_target="tpu_custom_call" | custom-call | flops 7474249728 | bytes 17694720 | tf_op jit(solution)/shard_map/expert_near/pallas_call | solution.py:293
  297.2 22.9 %collective-permute-done.7.refs_4_ = bf16[3,176,2048]{2,1,0:T(8,128)(2,1)S(1)} collective-permute-done((bf16[3,176,2048]{2,1,0:T(8,128)(2,1)}, bf16[3,176,2048]{2,1,0:T(8,128)(2,1)S(1)}, u32[]{:S(2)}, u32[]{:S(2)}) %collective-permute-start.7) | collective-permute-done | bytes 2162720 | tf_op jit(solution)/shard_map/ppermute | solution.py:404
  320.1 1.4 copy-done.4
  321.4 9.5 %expert_far.1 = bf16[768,2048]{1,0:T(8,128)(2,1)} custom-call(bf16[288,2048]{1,0:T(8,128)(2,1)} %get-tuple-element.14.refs_0_, bf16[288,2048]{1,0:T(8,128)(2,1)} %get-tuple-element.15.refs_1_, f32[288,2048]{1,0:T(8,128)} %get-tuple-element.16.refs_2_, f32[288,2048]{1,0:T(8,128)} %get-tuple-element.17.refs_3_, bf16[3,176,2048]{2,1,0:T(8,128)(2,1)} %copy-done.4, ...), custom_call_target="tpu_custom_call" | custom-call | flops 2491416576 | bytes 9043968 | tf_op jit(solution)/shard_map/expert_far/pallas_call | solution.py:311
  330.9 0.0 copy-start.11
  330.9 0.0 copy-start.12
  330.9 0.0 copy-start.13
  330.9 7.5 %all-to-all-start.2 = ((bf16[32,24,2048]{2,1,0:T(8,128)(2,1)}), bf16[32,24,2048]{2,1,0:T(8,128)(2,1)S(1)}, u32[]{:S(2)}, u32[]{:S(2)}) async-start(bf16[32,24,2048]{2,1,0:T(8,128)(2,1)} %bitcast.71), calls=%async_computation.2 | async-start | bytes 6291456 | tf_op jit(solution)/shard_map/all_to_all | solution.py:407
  338.5 0.2 select_reduce_fusion.7
  338.7 0.2 select_reduce_fusion.3
  338.9 0.9 copy.44.places_ref
  339.8 0.9 copy.45.values_ref
  340.6 11.6 %combine_pair.1 = (bf16[256,2048]{1,0:T(8,128)(2,1)}, f32[256,2048]{1,0:T(8,128)}, f32[8,128]{1,0:T(8,128)}, f32[8,128]{1,0:T(8,128)}) custom-call(bf16[1280,2048]{1,0:T(8,128)(2,1)} %bitcast.21.home, s32[512,4]{1,0:T(8,128)} %copy.44.places_ref, f32[512,4]{1,0:T(8,128)} %copy.45.values_ref, bf16[128,2048]{1,0:T(8,128)(2,1)} %grads.7, ...), custom_call_target="tpu_custom_call" | custom-call | flops 4026531840 | bytes 12582912 | tf_op jit(solution)/shard_map/combine_pair/pallas_call | solution.py:364
  352.3 2.0 collective-permute-start.11
  354.3 1.5 collective-permute-start.12
  355.8 0.8 copy.46.places_ref
  356.6 0.8 copy.47.values_ref
  357.4 18.1 %all-to-all-done.2 = bf16[32,24,2048]{2,1,0:T(8,128)(2,1)S(1)} async-done(((bf16[32,24,2048]{2,1,0:T(8,128)(2,1)}), bf16[32,24,2048]{2,1,0:T(8,128)(2,1)S(1)}, u32[]{:S(2)}, u32[]{:S(2)}) %all-to-all-start.2) | async-done | bytes 3145760 | tf_op jit(solution)/shard_map/all_to_all | solution.py:407
  375.5 3.8 collective-permute-done.12.dw_back
  379.4 0.6 copy-done.14
  379.9 6.3 %combine_full.1 = (bf16[128,2048]{1,0:T(8,128)(2,1)}, bf16[128,2048]{1,0:T(8,128)(2,1)}, f32[4,128]{1,0:T(4,128)}) custom-call(bf16[768,2048]{1,0:T(8,128)(2,1)} %bitcast.72, s32[256,4]{1,0:T(8,128)} %copy.46.places_ref, f32[256,4]{1,0:T(8,128)} %copy.47.values_ref, bf16[128,2048]{1,0:T(8,128)(2,1)} %grads.7, f32[256,2048]{1,0:T(8,128)} %get-tuple-element.18.own, ...), custom_call_target="tpu_custom_call" | custom-call | flops 1207959552 | bytes 8388608 | tf_op jit(solution)/shard_map/combine_full/pallas_call | solution.py:381
  (34 shorter events, 0.1 us)
Async XLA Ops:
  0.6 28.0 %collective-permute-start.2 = (bf16[128,2048]{1,0:T(8,128)(2,1)}, bf16[128,2048]{1,0:T(8,128)(2,1)S(1)}, u32[]{:S(2)}, u32[]{:S(2)}) collective-permute-start(bf16[128,2048]{1,0:T(8,128)(2,1)} %grads.7), channel_id=1, source_target_pairs={{0,2},{1,3},{2,0},{3,1},{4,6},{5,7},{6,4},{7,5},{8,10},{9,11},{10,... | collective-permute-start | bytes 1572872 | tf_op jit(solution)/shard_map/ppermute | solution.py:404
  4.6 24.1 %collective-permute-start.1 = (bf16[128,2048]{1,0:T(8,128)(2,1)}, bf16[128,2048]{1,0:T(8,128)(2,1)S(1)}, u32[]{:S(2)}, u32[]{:S(2)}) collective-permute-start(bf16[128,2048]{1,0:T(8,128)(2,1)} %tokens.3), channel_id=1, source_target_pairs={{0,2},{1,3},{2,0},{3,1},{4,6},{5,7},{6,4},{7,5},{8,10},{9,11},{10,... | collective-permute-start | bytes 1572872 | tf_op jit(solution)/shard_map/ppermute | solution.py:404
  6.1 22.0 %collective-permute-start = (f32[8,128]{1,0:T(8,128)S(1)}, f32[8,128]{1,0:T(8,128)S(1)}, u32[]{:S(2)}, u32[]{:S(2)}) collective-permute-start(f32[8,128]{1,0:T(8,128)S(1)} %pad_maximum_fusion.5), channel_id=1, source_target_pairs={{0,2},{1,3},{2,0},{3,1},{4,6},{5,7},{6,4},{7,5},{8,10},{9,11},{10,... | collective-permute-start | bytes 12296 | tf_op jit(solution)/shard_map/ppermute | solution.py:404
  28.6 0.8 copy-start.9
  28.6 1.0 copy-start.10
  36.5 44.7 %all-to-all-start.1 = ((bf16[32,24,2048]{2,1,0:T(8,128)(2,1)}), bf16[32,24,2048]{2,1,0:T(8,128)(2,1)S(1)}, u32[]{:S(2)}, u32[]{:S(2)}) async-start(bf16[32,24,2048]{2,1,0:T(8,128)(2,1)} %bitcast.73), calls=%async_computation.1 | async-start | bytes 6291456 | tf_op jit(solution)/shard_map/all_to_all | solution.py:407
  81.2 1.7 copy-start.1
  82.9 65.7 %all-to-all-start = ((bf16[32,32,2048]{2,1,0:T(8,128)(2,1)}), bf16[32,32,2048]{2,1,0:T(8,128)(2,1)}, u32[]{:S(2)}, u32[]{:S(2)}) async-start(bf16[32,32,2048]{2,1,0:T(8,128)(2,1)} %bitcast.70), calls=%async_computation | async-start | bytes 8388608 | tf_op jit(solution)/shard_map/all_to_all | solution.py:407
  90.7 2.7 copy-start.2
  90.7 3.5 copy-start.3
  96.4 1.6 copy-start.7
  96.4 50.8 %collective-permute-start.10 = (bf16[3,176,2048]{2,1,0:T(8,128)(2,1)S(1)}, bf16[3,176,2048]{2,1,0:T(8,128)(2,1)S(1)}, u32[]{:S(2)}, u32[]{:S(2)}) collective-permute-start(bf16[3,176,2048]{2,1,0:T(8,128)(2,1)S(1)} %pad_maximum_fusion.3.refs_3_), channel_id=1, source_target_pairs={{0,1},{1,2},{2,3},{3,0},{4,5},{5,6},{6,7},{7,4},{8,9},{9,10},{10,1... | collective-permute-start | bytes 6488072 | tf_op jit(solution)/shard_map/ppermute | solution.py:404
  98.0 49.2 %copy-start.8 = (bf16[3,176,2048]{2,1,0:T(8,128)(2,1)}, bf16[3,176,2048]{2,1,0:T(8,128)(2,1)S(1)}, u32[]{:S(2)}) copy-start(bf16[3,176,2048]{2,1,0:T(8,128)(2,1)S(1)} %pad_maximum_fusion.2.refs_2_) | copy-start | bytes 6488068
  98.0 50.6 %collective-permute-start.9 = (bf16[3,176,2048]{2,1,0:T(8,128)(2,1)S(1)}, bf16[3,176,2048]{2,1,0:T(8,128)(2,1)}, u32[]{:S(2)}, u32[]{:S(2)}) collective-permute-start(bf16[3,176,2048]{2,1,0:T(8,128)(2,1)S(1)} %pad_maximum_fusion.2.refs_2_), channel_id=1, source_target_pairs={{0,3},{1,0},{2,1},{3,2},{4,7},{5,4},{6,5},{7,6},{8,11},{9,8},{10,9... | collective-permute-start | bytes 6488072 | tf_op jit(solution)/shard_map/ppermute | solution.py:404
  147.2 1.4 copy-start.16
  167.9 163.0 %all-to-all-start.3 = ((bf16[32,40,2048]{2,1,0:T(8,128)(2,1)}), bf16[32,40,2048]{2,1,0:T(8,128)(2,1)}, u32[]{:S(2)}, u32[]{:S(2)}) async-start(bf16[32,40,2048]{2,1,0:T(8,128)(2,1)} %bitcast.74), calls=%async_computation.3 | async-start | bytes 10485760 | tf_op jit(solution)/shard_map/all_to_all | solution.py:407
  177.0 3.6 copy-start.5
  177.0 51.3 %collective-permute-start.3 = (bf16[3,176,2048]{2,1,0:T(8,128)(2,1)S(1)}, bf16[3,176,2048]{2,1,0:T(8,128)(2,1)}, u32[]{:S(2)}, u32[]{:S(2)}) collective-permute-start(bf16[3,176,2048]{2,1,0:T(8,128)(2,1)S(1)} %pad_maximum_fusion.refs_2_), channel_id=1, source_target_pairs={{0,1},{1,2},{2,3},{3,0},{4,5},{5,6},{6,7},{7,4},{8,9},{9,10},{10,1... | collective-permute-start | bytes 6488072 | tf_op jit(solution)/shard_map/ppermute | solution.py:404
  177.6 50.7 %copy-start.6 = (bf16[3,176,2048]{2,1,0:T(8,128)(2,1)}, bf16[3,176,2048]{2,1,0:T(8,128)(2,1)S(1)}, u32[]{:S(2)}) copy-start(bf16[3,176,2048]{2,1,0:T(8,128)(2,1)S(1)} %pad_maximum_fusion.1.refs_3_) | copy-start | bytes 6488068
  177.6 50.7 %collective-permute-start.6 = (bf16[3,176,2048]{2,1,0:T(8,128)(2,1)S(1)}, bf16[3,176,2048]{2,1,0:T(8,128)(2,1)}, u32[]{:S(2)}, u32[]{:S(2)}) collective-permute-start(bf16[3,176,2048]{2,1,0:T(8,128)(2,1)S(1)} %pad_maximum_fusion.1.refs_3_), channel_id=1, source_target_pairs={{0,3},{1,0},{2,1},{3,2},{4,7},{5,4},{6,5},{7,6},{8,11},{9,8},{10,9... | collective-permute-start | bytes 6488072 | tf_op jit(solution)/shard_map/ppermute | solution.py:404
  180.6 93.9 %collective-permute-start.4 = (bf16[3,176,2048]{2,1,0:T(8,128)(2,1)S(1)}, bf16[3,176,2048]{2,1,0:T(8,128)(2,1)S(1)}, u32[]{:S(2)}, u32[]{:S(2)}) collective-permute-start(bf16[3,176,2048]{2,1,0:T(8,128)(2,1)S(1)} %pad_maximum_fusion.1.refs_3_), channel_id=1, source_target_pairs={{0,1},{1,2},{2,3},{3,0},{4,5},{5,6},{6,7},{7,4},{8,9},{9,10},{10,1... | collective-permute-start | bytes 6488072 | tf_op jit(solution)/shard_map/ppermute | solution.py:404
  180.6 95.3 %collective-permute-start.5 = (bf16[3,176,2048]{2,1,0:T(8,128)(2,1)S(1)}, bf16[3,176,2048]{2,1,0:T(8,128)(2,1)}, u32[]{:S(2)}, u32[]{:S(2)}) collective-permute-start(bf16[3,176,2048]{2,1,0:T(8,128)(2,1)S(1)} %pad_maximum_fusion.refs_2_), channel_id=1, source_target_pairs={{0,3},{1,0},{2,1},{3,2},{4,7},{5,4},{6,5},{7,6},{8,11},{9,8},{10,9... | collective-permute-start | bytes 6488072 | tf_op jit(solution)/shard_map/ppermute | solution.py:404
  228.3 91.7 %collective-permute-start.7 = (bf16[3,176,2048]{2,1,0:T(8,128)(2,1)}, bf16[3,176,2048]{2,1,0:T(8,128)(2,1)S(1)}, u32[]{:S(2)}, u32[]{:S(2)}) collective-permute-start(bf16[3,176,2048]{2,1,0:T(8,128)(2,1)} %collective-permute-done.3.refs_4_), channel_id=1, source_target_pairs={{0,1},{1,2},{2,3},{3,0},{4,5},{5,6},{6,7},{7,4},{8,9},{9,10},{10,1... | collective-permute-start | bytes 6488072 | tf_op jit(solution)/shard_map/ppermute | solution.py:404
  228.3 91.7 %collective-permute-start.8 = (bf16[3,176,2048]{2,1,0:T(8,128)(2,1)}, bf16[3,176,2048]{2,1,0:T(8,128)(2,1)}, u32[]{:S(2)}, u32[]{:S(2)}) collective-permute-start(bf16[3,176,2048]{2,1,0:T(8,128)(2,1)} %collective-permute-done.6.refs_7_), channel_id=1, source_target_pairs={{0,3},{1,0},{2,1},{3,2},{4,7},{5,4},{6,5},{7,6},{8,11},{9,8},{10,9... | collective-permute-start | bytes 6488072 | tf_op jit(solution)/shard_map/ppermute | solution.py:404
  274.6 1.4 copy-start.15
  320.1 1.4 copy-start.4
  330.9 7.6 %copy-start.11 = (s32[128,4]{0,1:T(4,128)S(1)}, s32[128,4]{0,1:T(4,128)}, u32[]{:S(2)}) copy-start(s32[128,4]{0,1:T(4,128)} %param.8) | copy-start | bytes 6148
  330.9 7.8 %copy-start.12 = (s32[4,128]{1,0:T(4,128)S(1)}, s32[4,128]{1,0:T(4,128)}, u32[]{:S(2)}) copy-start(s32[4,128]{1,0:T(4,128)} %get-tuple-element.48.route_other_ref) | copy-start | bytes 6148
  330.9 8.8 %copy-start.13 = (f32[128,4]{0,1:T(4,128)S(1)}, f32[128,4]{0,1:T(4,128)}, u32[]{:S(2)}) copy-start(f32[128,4]{0,1:T(4,128)} %param.9) | copy-start | bytes 6148
  330.9 44.6 %all-to-all-start.2 = ((bf16[32,24,2048]{2,1,0:T(8,128)(2,1)}), bf16[32,24,2048]{2,1,0:T(8,128)(2,1)S(1)}, u32[]{:S(2)}, u32[]{:S(2)}) async-start(bf16[32,24,2048]{2,1,0:T(8,128)(2,1)} %bitcast.71), calls=%async_computation.2 | async-start | bytes 6291456 | tf_op jit(solution)/shard_map/all_to_all | solution.py:407
  352.3 27.1 %collective-permute-start.11 = (bf16[256,2048]{1,0:T(8,128)(2,1)}, bf16[256,2048]{1,0:T(8,128)(2,1)}, u32[]{:S(2)}, u32[]{:S(2)}) collective-permute-start(bf16[256,2048]{1,0:T(8,128)(2,1)} %get-tuple-element.19), channel_id=1, source_target_pairs={{0,2},{1,3},{2,0},{3,1},{4,6},{5,7},{6,4},{7,5},{8,10},{9,11},{10,... | collective-permute-start | bytes 3145736 | tf_op jit(solution)/shard_map/ppermute | solution.py:404
  354.3 25.1 %collective-permute-start.12 = (f32[8,128]{1,0:T(8,128)}, f32[8,128]{1,0:T(8,128)S(1)}, u32[]{:S(2)}, u32[]{:S(2)}) collective-permute-start(f32[8,128]{1,0:T(8,128)} %get-tuple-element.21), channel_id=1, source_target_pairs={{0,2},{1,3},{2,0},{3,1},{4,6},{5,7},{6,4},{7,5},{8,10},{9,11},{10,... | collective-permute-start | bytes 12296 | tf_op jit(solution)/shard_map/ppermute | solution.py:404
  375.5 3.8 copy-start
  379.3 0.6 copy-start.14

commit v3 on v2

--- a/solution.py
+++ b/solution.py
@@ -226,24 +226,21 @@
 
 
 def expert_far_kernel(nodes, n_pieces, *refs):
-    near, pieces, home = refs[:4], refs[4 : 4 + n_pieces], refs[4 + n_pieces]
-    xs, gs, out_part, back_part, wg, wu, wd, outs, backs, out_rest, sems = refs[5 + n_pieces :]
+    xs, gs, out_at, back_at = refs[:4]
+    pieces, home = refs[4 : 4 + n_pieces], refs[4 + n_pieces]
+    out_part, back_part, wg, wu, wd, outs, backs, out_rest, sems = refs[5 + n_pieces :]
     main, small = nodes * 8, nodes
-    pltpu.make_async_copy(near[0], xs, sems.at[6]).start()
     fetch_weights(pieces, (wg, wu, wd), sems, 3)
-    pltpu.make_async_copy(near[1], gs, sems.at[7]).start()
-    pltpu.make_async_copy(near[2], out_part, sems.at[8]).start()
-    pltpu.make_async_copy(near[3], back_part, sems.at[9]).start()
-    landed(xs, sems.at[6])
+    pltpu.make_async_copy(out_at, out_part, sems.at[6]).start()
+    pltpu.make_async_copy(back_at, back_part, sems.at[7]).start()
     landed(wg, sems.at[3])
     landed(wu, sems.at[4])
     landed(wd, sems.at[5])
-    landed(gs, sems.at[7])
     hidden, d_gate, d_up = inner(xs[...], gs[...], wg[...], wu[...], wd[...])
-    landed(out_part, sems.at[8])
+    landed(out_part, sems.at[6])
     outs[...] = (by_row(hidden, wd[...]) + out_part[...]).astype(BF)
     put_rows(nodes, outs, 0, home, OUT1_ROWS, 0, sems.at[0])
-    landed(back_part, sems.at[9])
+    landed(back_part, sems.at[7])
     backs[...] = (by_row(d_gate, wg[...]) + by_row(d_up, wu[...]) + back_part[...]).astype(BF)
     put_rows(nodes, backs, 0, home, OUT1_ROWS, 8, sems.at[1])
     out_rest[...] = (
@@ -256,9 +253,16 @@
     landed(out_rest, sems.at[2])
 
 
+def on_chip(value):
+    return pltpu.with_memory_space_constraint(value, pltpu.VMEM)
+
+
 ANY = pl.BlockSpec(memory_space=pltpu.HBM)
 WHOLE = pl.BlockSpec(memory_space=pltpu.VMEM)
-PARAMS = pltpu.CompilerParams(vmem_limit_bytes=60 * 1024 * 1024)
+
+
+def room(mib):
+    return pltpu.CompilerParams(vmem_limit_bytes=mib * 1024 * 1024)
 
 
 def expert_cost(rows, hidden, width):
@@ -278,10 +282,10 @@
         functools.partial(expert_pair_kernel, nodes, len(pieces)),
         name="expert_pair",
         out_shape=jax.ShapeDtypeStruct((nodes * OUT0_ROWS, width), BF),
-        in_specs=[ANY] * (2 + len(pieces)),
+        in_specs=[ANY, WHOLE] + [ANY] * len(pieces),
         out_specs=ANY,
         scratch_shapes=[pltpu.VMEM(s, BF) for s in scratch] + [pltpu.SemaphoreType.DMA((6,))],
-        compiler_params=PARAMS,
+        compiler_params=room(46),
         cost_estimate=expert_cost(rows, hidden, width),
     )(arrived, arrived_other, *pieces)
 
@@ -294,10 +298,10 @@
         functools.partial(expert_near_kernel, nodes, len(pieces)),
         name="expert_near",
         out_shape=tuple(jax.ShapeDtypeStruct((rows, width), t) for t in (F32, F32, BF, BF)),
-        in_specs=[ANY] * (2 + len(pieces)),
+        in_specs=[ANY, WHOLE] + [ANY] * len(pieces),
         out_specs=(WHOLE,) * 4,
         scratch_shapes=[pltpu.VMEM(s, BF) for s in scratch] + [pltpu.SemaphoreType.DMA((6,))],
-        compiler_params=PARAMS,
+        compiler_params=room(46),
         cost_estimate=expert_cost(rows, hidden, width),
     )(arrived, arrived_other, *pieces)
 
@@ -306,18 +310,18 @@
     out_part, back_part, xs, gs = near
     rows, width = xs.shape
     hidden = len(pieces) * pieces[0].shape[1]
-    scratch = [((rows, width), BF)] * 2 + [((rows, width), F32)] * 2 + [((hidden, width), BF)] * 3
+    scratch = [((rows, width), F32)] * 2 + [((hidden, width), BF)] * 3
     scratch += [((rows, width), BF)] * 2 + [((nodes * 8, width), BF)]
     return pl.pallas_call(
         functools.partial(expert_far_kernel, nodes, len(pieces)),
         name="expert_far",
         out_shape=jax.ShapeDtypeStruct((nodes * OUT1_ROWS, width), BF),
-        in_specs=[ANY] * (4 + len(pieces)),
+        in_specs=[WHOLE] * 2 + [ANY] * (2 + len(pieces)),
         out_specs=ANY,
-        scratch_shapes=[pltpu.VMEM(s, t) for s, t in scratch] + [pltpu.SemaphoreType.DMA((10,))],
-        compiler_params=PARAMS,
+        scratch_shapes=[pltpu.VMEM(s, t) for s, t in scratch] + [pltpu.SemaphoreType.DMA((8,))],
+        compiler_params=room(57),
         cost_estimate=expert_cost(rows, hidden, width),
-    )(xs, gs, out_part, back_part, *pieces)
+    )(on_chip(xs), on_chip(gs), out_part, back_part, *pieces)
 
 
 def mixed(rows, places, values):
@@ -349,12 +353,25 @@
     dw_own[...] = jnp.transpose(weight_grads(rows, grads[...], places_ref[2 * toks : 3 * toks]))[:8]
 
 
-def combine_full_kernel(home, places_ref, values_ref, grads, own, returned, dw_own, dw_back, combined, d_tokens, d_weights):
+def combine_full_kernel(
+    home, places_ref, values_ref, dw_own, dw_back, grads_at, own_at, returned_at, combined, d_tokens, d_weights, *scratch
+):
+    grads, own, returned, sems = scratch
     toks = grads.shape[0]
+    copies = [
+        pltpu.make_async_copy(src, dst, sems.at[i])
+        for i, (src, dst) in enumerate(((own_at, own), (returned_at, returned), (grads_at, grads)))
+    ]
+    for copy in copies:
+        copy.start()
     rows = home[...]
-    total = mixed(rows, places_ref[...], values_ref[...]) + own[...] + returned[...].astype(F32)
+    total = mixed(rows, places_ref[...], values_ref[...])
+    copies[0].wait()
+    copies[1].wait()
+    total = total + own[...] + returned[...].astype(F32)
     combined[...] = total[:toks].astype(BF)
     d_tokens[...] = total[toks:].astype(BF)
+    copies[2].wait()
     dw = jnp.transpose(weight_grads(rows, grads[...], places_ref[:toks]))[:8] + dw_own[...] + dw_back[...]
     d_weights[...] = dw[:TOP]
 
@@ -370,6 +387,7 @@
             jax.ShapeDtypeStruct((8, toks), F32),
             jax.ShapeDtypeStruct((8, toks), F32),
         ),
+        compiler_params=room(60),
         cost_estimate=pl.CostEstimate(
             flops=12 * toks * home.shape[0] * width, transcendentals=0, bytes_accessed=12 * 1024 * 1024
         ),
@@ -386,10 +404,19 @@
             jax.ShapeDtypeStruct((toks, width), BF),
             jax.ShapeDtypeStruct((TOP, toks), F32),
         ),
+        in_specs=[WHOLE] * 5 + [ANY] * 3,
+        out_specs=(WHOLE,) * 3,
+        scratch_shapes=[
+            pltpu.VMEM((toks, width), BF),
+            pltpu.VMEM((2 * toks, width), F32),
+            pltpu.VMEM((2 * toks, width), BF),
+            pltpu.SemaphoreType.DMA((3,)),
+        ],
+        compiler_params=room(60),
         cost_estimate=pl.CostEstimate(
             flops=6 * toks * home.shape[0] * width, transcendentals=0, bytes_accessed=8 * 1024 * 1024
         ),
-    )(home, places, values, grads, own, returned, dw_own, dw_back)
+    )(on_chip(home), places, values, dw_own, dw_back, grads, own, returned)
 
 
 def shards(tokens, route, combine_weights, w_gate, w_up, w_down, grad_out):
@@ -437,6 +464,7 @@
     )
     arrived_other = exchange(other_rows)
 
+    arrived_other = on_chip(arrived_other)
     rows0 = expert_pair(arrived, arrived_other, w0, nodes)
     home0 = exchange(rows0)
     near = expert_near(arrived, arrived_other, w1[:6], nodes)

time: 388 us -> 390 us (level)
    unnamed x34 -> x40, local copies, waits for them, and re-layouts: 8.83 us -> 9.67 us
where the time goes in v3:
time: 390 us
  waiting for transfers between devices  226 us (58%)
  Pallas kernels  82.8 us (21%)
  starting transfers between devices  56.2 us (14%)
  local copies, waits for them, and re-layouts  18.3 us (5%)
  other arithmetic  4.64 us (1%)
    ppermute x13, waiting for transfers between devices, send(): return lax.ppermute(value, 'local', pairs)  177 us
    all_to_all x4, waiting for transfers between devices, exchange(): return lax.all_to_all(rows, 'node', split_axis=0, concat_axis=0, tiled=True)  49.5 us
    all_to_all x4, starting transfers between devices, exchange(): return lax.all_to_all(rows, 'node', split_axis=0, concat_axis=0, tiled=True)  30.5 us
    ppermute x13, starting transfers between devices, send(): return lax.ppermute(value, 'local', pairs)  25.7 us
    pallas_call x1, Pallas kernels, expert_pair(): pl.pallas_call(functools.partial(expert_pair_kernel, nodes, len(pieces)),...  21.8 us
    pallas_call x1, Pallas kernels, expert_near(): pl.pallas_call(functools.partial(expert_near_kernel, nodes, len(pieces)),...  21.6 us
    pallas_call x2, Pallas kernels, dispatch(): pl.pallas_call(kernel, grid=(steps,), out_shape=jax.ShapeDtypeStruct((row...  12.7 us
    pallas_call x1, Pallas kernels, combine_pair(): pl.pallas_call(combine_pair_kernel, name='combine_pair', out_shape=(jax.S...  11.6 us
  transfers between devices with their start and end apart: 17, of which 8 were waited for; matrix products, arithmetic and copies ran while one was open for 3% of the time, Pallas kernels for 12%

profile of v3, /device:TPU:2, one launch (start us, length us, event | category | flops | bytes accessed | tf_op | source)
XLA Modules:
  0.0 389.6 jit_solution(145653409259376410)
XLA Ops:
  0.6 4.0 %collective-permute-start.2 = (bf16[128,2048]{1,0:T(8,128)(2,1)}, bf16[128,2048]{1,0:T(8,128)(2,1)S(1)}, u32[]{:S(2)}, u32[]{:S(2)}) collective-permute-start(bf16[128,2048]{1,0:T(8,128)(2,1)} %grads_at.1), channel_id=1, source_target_pairs={{0,2},{1,3},{2,0},{3,1},{4,6},{5,7},{6,4},{7,5},{8,10},{9,11},{10,... | collective-permute-start | bytes 1572872 | tf_op jit(solution)/shard_map/ppermute | solution.py:431
  4.6 0.1 collective-permute-start.1
  4.7 0.7 bitcast_convert_fusion
  5.4 0.7 pad_maximum_fusion.5
  6.1 3.4 collective-permute-start
  9.5 18.6 %collective-permute-done = f32[8,128]{1,0:T(8,128)S(1)} collective-permute-done((f32[8,128]{1,0:T(8,128)S(1)}, f32[8,128]{1,0:T(8,128)S(1)}, u32[]{:S(2)}, u32[]{:S(2)}) %collective-permute-start) | collective-permute-done | bytes 4128 | tf_op jit(solution)/shard_map/ppermute | solution.py:431
  28.0 0.6 slice_bitcast_fusion
  28.6 0.0 collective-permute-done.2.grads_other
  28.6 0.0 collective-permute-done.1.tokens_other
  28.6 0.0 copy-start.11
  28.7 0.8 copy-done.10
  29.4 0.2 copy-done.11
  29.6 6.9 %shard_map.95 = bf16[768,2048]{1,0:T(8,128)(2,1)} custom-call(s32[4,128]{1,0:T(4,128)} %bitcast.79, s32[4,128]{1,0:T(4,128)} %get-tuple-element.48.route_other_ref, bf16[128,2048]{1,0:T(8,128)(2,1)} %tokens.3, bf16[128,2048]{1,0:T(8,128)(2,1)} %grads_at.1, bf16[128,2048]{1,0:T(8,128)(2,1)} %copy-done.11, bf16[128,2048]{1,0:T(8,128)(2,1)} %copy-done.10), custom_call_target="tpu_custom_call" | custom-call | flops 805306368 | bytes 6291456 | tf_op jit(solution)/shard_map/pallas_call | solution.py:86
  36.5 7.6 %all-to-all-start.1 = ((bf16[32,24,2048]{2,1,0:T(8,128)(2,1)}), bf16[32,24,2048]{2,1,0:T(8,128)(2,1)S(1)}, u32[]{:S(2)}, u32[]{:S(2)}) async-start(bf16[32,24,2048]{2,1,0:T(8,128)(2,1)} %bitcast.75), calls=%async_computation.1 | async-start | bytes 6291456 | tf_op jit(solution)/shard_map/all_to_all | solution.py:434
  44.2 5.8 %shard_map.94 = bf16[1024,2048]{1,0:T(8,128)(2,1)} custom-call(s32[4,128]{1,0:T(4,128)} %bitcast.80, bf16[128,2048]{1,0:T(8,128)(2,1)} %tokens.3, bf16[128,2048]{1,0:T(8,128)(2,1)} %grads_at.1), custom_call_target="tpu_custom_call" | custom-call | flops 1073741824 | bytes 8388608 | tf_op jit(solution)/shard_map/pallas_call | solution.py:86
  49.9 31.3 %all-to-all-done.1 = bf16[32,24,2048]{2,1,0:T(8,128)(2,1)S(1)} async-done(((bf16[32,24,2048]{2,1,0:T(8,128)(2,1)}), bf16[32,24,2048]{2,1,0:T(8,128)(2,1)S(1)}, u32[]{:S(2)}, u32[]{:S(2)}) %all-to-all-start.1) | async-done | bytes 3145760 | tf_op jit(solution)/shard_map/all_to_all | solution.py:434
  81.2 7.8 %all-to-all-start = ((bf16[32,32,2048]{2,1,0:T(8,128)(2,1)}), bf16[32,32,2048]{2,1,0:T(8,128)(2,1)}, u32[]{:S(2)}, u32[]{:S(2)}) async-start(bf16[32,32,2048]{2,1,0:T(8,128)(2,1)} %bitcast.73), calls=%async_computation | async-start | bytes 8388608 | tf_op jit(solution)/shard_map/all_to_all | solution.py:434
  89.1 0.0 copy-start.4
  89.1 0.0 copy-start.5
  89.1 3.3 fusion.29
  92.4 0.8 copy-done.5
  93.1 2.0 fusion.27
  95.2 0.2 pad_maximum_fusion.3.refs_3_
  95.4 1.3 collective-permute-start.10
  96.8 0.2 pad_maximum_fusion.2.refs_2_
  97.0 3.2 collective-permute-start.9
  100.2 1.4 copy-done.2
  101.6 44.6 %collective-permute-done.10.refs_5_ = bf16[3,176,2048]{2,1,0:T(8,128)(2,1)S(1)} collective-permute-done((bf16[3,176,2048]{2,1,0:T(8,128)(2,1)S(1)}, bf16[3,176,2048]{2,1,0:T(8,128)(2,1)S(1)}, u32[]{:S(2)}, u32[]{:S(2)}) %collective-permute-start.10) | collective-permute-done | bytes 2162720 | tf_op jit(solution)/shard_map/ppermute | solution.py:431
  146.2 1.4 copy-done.19
  147.6 0.0 collective-permute-done.9.refs_4_
  147.6 0.0 all-to-all-done
  147.6 1.6 copy-done.1
  149.2 1.6 copy-done.3
  150.8 21.8 %expert_pair.1 = bf16[1280,2048]{1,0:T(8,128)(2,1)} custom-call(bf16[1024,2048]{1,0:T(8,128)(2,1)} %bitcast.2.refs_0_, bf16[768,2048]{1,0:T(8,128)(2,1)S(1)} %bitcast.71, bf16[3,176,2048]{2,1,0:T(8,128)(2,1)S(1)} %copy-done.3, bf16[3,176,2048]{2,1,0:T(8,128)(2,1)S(1)} %copy-done.1, bf16[3,176,2048]{2,1,0:T(8,128)(2,1)} %collective-permute-done.9.refs_4_, ...), custom_call_target="tpu_custom_call" | custom-call | flops 9965666304 | bytes 18087936 | tf_op jit(solution)/shard_map/expert_pair/pallas_call | solution.py:281
  172.6 7.5 %all-to-all-start.3 = ((bf16[32,40,2048]{2,1,0:T(8,128)(2,1)}), bf16[32,40,2048]{2,1,0:T(8,128)(2,1)}, u32[]{:S(2)}, u32[]{:S(2)}) async-start(bf16[32,40,2048]{2,1,0:T(8,128)(2,1)} %bitcast.76), calls=%async_computation.3 | async-start | bytes 10485760 | tf_op jit(solution)/shard_map/all_to_all | solution.py:434
  180.2 1.9 pad_maximum_fusion.refs_2_
  182.1 0.4 collective-permute-start.3
  182.4 0.2 pad_maximum_fusion.1.refs_3_
  182.7 3.0 collective-permute-start.6
  185.7 3.2 collective-permute-start.5
  189.0 44.3 %collective-permute-done.3.refs_4_ = bf16[3,176,2048]{2,1,0:T(8,128)(2,1)S(1)} collective-permute-done((bf16[3,176,2048]{2,1,0:T(8,128)(2,1)S(1)}, bf16[3,176,2048]{2,1,0:T(8,128)(2,1)S(1)}, u32[]{:S(2)}, u32[]{:S(2)}) %collective-permute-start.3) | collective-permute-done | bytes 2162720 | tf_op jit(solution)/shard_map/ppermute | solution.py:431
  233.3 3.5 collective-permute-start.8
  236.8 42.8 %collective-permute-done.4.refs_5_ = bf16[3,176,2048]{2,1,0:T(8,128)(2,1)S(1)} collective-permute-done((bf16[3,176,2048]{2,1,0:T(8,128)(2,1)S(1)}, bf16[3,176,2048]{2,1,0:T(8,128)(2,1)S(1)}, u32[]{:S(2)}, u32[]{:S(2)}) %collective-permute-start.4) | collective-permute-done | bytes 2162720 | tf_op jit(solution)/shard_map/ppermute | solution.py:431
  279.6 1.3 copy-done.18
  280.9 21.6 %expert_near.1 = (f32[288,2048]{1,0:T(8,128)}, f32[288,2048]{1,0:T(8,128)}, bf16[288,2048]{1,0:T(8,128)(2,1)S(1)}, bf16[288,2048]{1,0:T(8,128)(2,1)S(1)}) custom-call(bf16[1024,2048]{1,0:T(8,128)(2,1)} %bitcast.2.refs_0_, bf16[768,2048]{1,0:T(8,128)(2,1)S(1)} %bitcast.72, bf16[3,176,2048]{2,1,0:T(8,128)(2,1)S(1)} %pad_maximum_fusion.refs_2_, ...), custom_call_target="tpu_custom_call" | custom-call | flops 7474249728 | bytes 17694720 | tf_op jit(solution)/shard_map/expert_near/pallas_call | solution.py:297
  302.5 22.7 %collective-permute-done.7.refs_4_ = bf16[3,176,2048]{2,1,0:T(8,128)(2,1)} collective-permute-done((bf16[3,176,2048]{2,1,0:T(8,128)(2,1)S(1)}, bf16[3,176,2048]{2,1,0:T(8,128)(2,1)}, u32[]{:S(2)}, u32[]{:S(2)}) %collective-permute-start.7) | collective-permute-done | bytes 2162720 | tf_op jit(solution)/shard_map/ppermute | solution.py:431
  325.3 8.6 %expert_far.1 = bf16[768,2048]{1,0:T(8,128)(2,1)} custom-call(bf16[288,2048]{1,0:T(8,128)(2,1)S(1)} %get-tuple-element.14.refs_0_, bf16[288,2048]{1,0:T(8,128)(2,1)S(1)} %get-tuple-element.15.refs_1_, f32[288,2048]{1,0:T(8,128)} %get-tuple-element.16.refs_2_, f32[288,2048]{1,0:T(8,128)} %get-tuple-element.17.refs_3_, ...), custom_call_target="tpu_custom_call" | custom-call | flops 2491416576 | bytes 9043968 | tf_op jit(solution)/shard_map/expert_far/pallas_call | solution.py:315
  333.9 0.0 copy-start.12
  333.9 0.0 copy-start.13
  333.9 0.0 copy-start.14
  333.9 7.5 %all-to-all-start.2 = ((bf16[32,24,2048]{2,1,0:T(8,128)(2,1)}), bf16[32,24,2048]{2,1,0:T(8,128)(2,1)S(1)}, u32[]{:S(2)}, u32[]{:S(2)}) async-start(bf16[32,24,2048]{2,1,0:T(8,128)(2,1)} %bitcast.74), calls=%async_computation.2 | async-start | bytes 6291456 | tf_op jit(solution)/shard_map/all_to_all | solution.py:434
  341.5 0.2 select_reduce_fusion.7
  341.7 0.2 select_reduce_fusion.3
  341.9 0.9 copy.44.places_ref
  342.8 0.9 copy.45.values_ref
  343.6 11.6 %combine_pair.1 = (bf16[256,2048]{1,0:T(8,128)(2,1)}, f32[256,2048]{1,0:T(8,128)}, f32[8,128]{1,0:T(8,128)}, f32[8,128]{1,0:T(8,128)}) custom-call(bf16[1280,2048]{1,0:T(8,128)(2,1)} %bitcast.21.home, s32[512,4]{1,0:T(8,128)} %copy.44.places_ref, f32[512,4]{1,0:T(8,128)} %copy.45.values_ref, bf16[128,2048]{1,0:T(8,128)(2,1)} %grads_at.1, ...), custom_call_target="tpu_custom_call" | custom-call | flops 4026531840 | bytes 12582912 | tf_op jit(solution)/shard_map/combine_pair/pallas_call | solution.py:381
  355.2 3.3 collective-permute-start.12
  358.5 0.3 collective-permute-start.11
  358.8 0.8 copy.46.places_ref
  359.6 0.8 copy.47.values_ref
  360.4 18.2 %all-to-all-done.2 = bf16[32,24,2048]{2,1,0:T(8,128)(2,1)S(1)} async-done(((bf16[32,24,2048]{2,1,0:T(8,128)(2,1)}), bf16[32,24,2048]{2,1,0:T(8,128)(2,1)S(1)}, u32[]{:S(2)}, u32[]{:S(2)}) %all-to-all-start.2) | async-done | bytes 3145760 | tf_op jit(solution)/shard_map/all_to_all | solution.py:434
  378.5 3.8 collective-permute-done.11.dw_back
  382.3 0.6 copy-done.15
  382.9 6.6 %combine_full.1 = (bf16[128,2048]{1,0:T(8,128)(2,1)}, bf16[128,2048]{1,0:T(8,128)(2,1)}, f32[4,128]{1,0:T(4,128)}) custom-call(bf16[768,2048]{1,0:T(8,128)(2,1)S(1)} %bitcast.70, s32[256,4]{1,0:T(8,128)} %copy.46.places_ref, f32[256,4]{1,0:T(8,128)} %copy.47.values_ref, f32[8,128]{1,0:T(8,128)} %get-tuple-element.18.dw_own, f32[8,128]{1,0:T(8,128)} %copy-done.15, ...), custom_call_target="tpu_custom_call" | custom-call | flops 1207959552 | bytes 8388608 | tf_op jit(solution)/shard_map/combine_full/pallas_call | solution.py:399
  (40 shorter events, 0.1 us)
Async XLA Ops:
  0.6 28.0 %collective-permute-start.2 = (bf16[128,2048]{1,0:T(8,128)(2,1)}, bf16[128,2048]{1,0:T(8,128)(2,1)S(1)}, u32[]{:S(2)}, u32[]{:S(2)}) collective-permute-start(bf16[128,2048]{1,0:T(8,128)(2,1)} %grads_at.1), channel_id=1, source_target_pairs={{0,2},{1,3},{2,0},{3,1},{4,6},{5,7},{6,4},{7,5},{8,10},{9,11},{10,... | collective-permute-start | bytes 1572872 | tf_op jit(solution)/shard_map/ppermute | solution.py:431
  4.6 24.1 %collective-permute-start.1 = (bf16[128,2048]{1,0:T(8,128)(2,1)}, bf16[128,2048]{1,0:T(8,128)(2,1)S(1)}, u32[]{:S(2)}, u32[]{:S(2)}) collective-permute-start(bf16[128,2048]{1,0:T(8,128)(2,1)} %tokens.3), channel_id=1, source_target_pairs={{0,2},{1,3},{2,0},{3,1},{4,6},{5,7},{6,4},{7,5},{8,10},{9,11},{10,... | collective-permute-start | bytes 1572872 | tf_op jit(solution)/shard_map/ppermute | solution.py:431
  6.1 22.0 %collective-permute-start = (f32[8,128]{1,0:T(8,128)S(1)}, f32[8,128]{1,0:T(8,128)S(1)}, u32[]{:S(2)}, u32[]{:S(2)}) collective-permute-start(f32[8,128]{1,0:T(8,128)S(1)} %pad_maximum_fusion.5), channel_id=1, source_target_pairs={{0,2},{1,3},{2,0},{3,1},{4,6},{5,7},{6,4},{7,5},{8,10},{9,11},{10,... | collective-permute-start | bytes 12296 | tf_op jit(solution)/shard_map/ppermute | solution.py:431
  28.6 0.8 copy-start.10
  28.6 1.0 copy-start.11
  36.5 44.7 %all-to-all-start.1 = ((bf16[32,24,2048]{2,1,0:T(8,128)(2,1)}), bf16[32,24,2048]{2,1,0:T(8,128)(2,1)S(1)}, u32[]{:S(2)}, u32[]{:S(2)}) async-start(bf16[32,24,2048]{2,1,0:T(8,128)(2,1)} %bitcast.75), calls=%async_computation.1 | async-start | bytes 6291456 | tf_op jit(solution)/shard_map/all_to_all | solution.py:434
  81.2 66.3 %all-to-all-start = ((bf16[32,32,2048]{2,1,0:T(8,128)(2,1)}), bf16[32,32,2048]{2,1,0:T(8,128)(2,1)}, u32[]{:S(2)}, u32[]{:S(2)}) async-start(bf16[32,32,2048]{2,1,0:T(8,128)(2,1)} %bitcast.73), calls=%async_computation | async-start | bytes 8388608 | tf_op jit(solution)/shard_map/all_to_all | solution.py:434
  89.1 3.3 copy-start.4
  89.1 4.1 %copy-start.5 = (bf16[2,2048,352]{1,2,0:T(8,128)(2,1)S(1)}, bf16[2,2048,352]{1,2,0:T(8,128)(2,1)}, u32[]{:S(2)}) copy-start(bf16[2,2048,352]{1,2,0:T(8,128)(2,1)} %param.11) | copy-start | bytes 8650756
  95.4 1.6 copy-start
  95.4 50.8 %collective-permute-start.10 = (bf16[3,176,2048]{2,1,0:T(8,128)(2,1)S(1)}, bf16[3,176,2048]{2,1,0:T(8,128)(2,1)S(1)}, u32[]{:S(2)}, u32[]{:S(2)}) collective-permute-start(bf16[3,176,2048]{2,1,0:T(8,128)(2,1)S(1)} %pad_maximum_fusion.3.refs_3_), channel_id=1, source_target_pairs={{0,1},{1,2},{2,3},{3,0},{4,5},{5,6},{6,7},{7,4},{8,9},{9,10},{10,1... | collective-permute-start | bytes 6488072 | tf_op jit(solution)/shard_map/ppermute | solution.py:431
  97.0 50.6 %collective-permute-start.9 = (bf16[3,176,2048]{2,1,0:T(8,128)(2,1)S(1)}, bf16[3,176,2048]{2,1,0:T(8,128)(2,1)}, u32[]{:S(2)}, u32[]{:S(2)}) collective-permute-start(bf16[3,176,2048]{2,1,0:T(8,128)(2,1)S(1)} %pad_maximum_fusion.2.refs_2_), channel_id=1, source_target_pairs={{0,3},{1,0},{2,1},{3,2},{4,7},{5,4},{6,5},{7,6},{8,11},{9,8},{10,9... | collective-permute-start | bytes 6488072 | tf_op jit(solution)/shard_map/ppermute | solution.py:431
  100.2 1.4 copy-start.2
  146.2 1.4 copy-start.19
  147.6 1.6 copy-start.1
  149.2 1.6 copy-start.3
  172.6 161.3 %all-to-all-start.3 = ((bf16[32,40,2048]{2,1,0:T(8,128)(2,1)}), bf16[32,40,2048]{2,1,0:T(8,128)(2,1)}, u32[]{:S(2)}, u32[]{:S(2)}) async-start(bf16[32,40,2048]{2,1,0:T(8,128)(2,1)} %bitcast.76), calls=%async_computation.3 | async-start | bytes 10485760 | tf_op jit(solution)/shard_map/all_to_all | solution.py:434
  180.1 2.3 copy-start.6
  180.1 2.3 copy-start.7
  180.1 2.3 copy-start.8
  182.1 51.2 %collective-permute-start.3 = (bf16[3,176,2048]{2,1,0:T(8,128)(2,1)S(1)}, bf16[3,176,2048]{2,1,0:T(8,128)(2,1)S(1)}, u32[]{:S(2)}, u32[]{:S(2)}) collective-permute-start(bf16[3,176,2048]{2,1,0:T(8,128)(2,1)S(1)} %pad_maximum_fusion.refs_2_), channel_id=1, source_target_pairs={{0,1},{1,2},{2,3},{3,0},{4,5},{5,6},{6,7},{7,4},{8,9},{9,10},{10,1... | collective-permute-start | bytes 6488072 | tf_op jit(solution)/shard_map/ppermute | solution.py:431
  182.7 96.9 %copy-start.9 = (bf16[3,176,2048]{2,1,0:T(8,128)(2,1)}, bf16[3,176,2048]{2,1,0:T(8,128)(2,1)S(1)}, u32[]{:S(2)}) copy-start(bf16[3,176,2048]{2,1,0:T(8,128)(2,1)S(1)} %pad_maximum_fusion.1.refs_3_) | copy-start | bytes 6488068
  182.7 50.6 %collective-permute-start.6 = (bf16[3,176,2048]{2,1,0:T(8,128)(2,1)S(1)}, bf16[3,176,2048]{2,1,0:T(8,128)(2,1)S(1)}, u32[]{:S(2)}, u32[]{:S(2)}) collective-permute-start(bf16[3,176,2048]{2,1,0:T(8,128)(2,1)S(1)} %pad_maximum_fusion.1.refs_3_), channel_id=1, source_target_pairs={{0,3},{1,0},{2,1},{3,2},{4,7},{5,4},{6,5},{7,6},{8,11},{9,8},{10,9... | collective-permute-start | bytes 6488072 | tf_op jit(solution)/shard_map/ppermute | solution.py:431
  185.7 93.9 %collective-permute-start.4 = (bf16[3,176,2048]{2,1,0:T(8,128)(2,1)S(1)}, bf16[3,176,2048]{2,1,0:T(8,128)(2,1)S(1)}, u32[]{:S(2)}, u32[]{:S(2)}) collective-permute-start(bf16[3,176,2048]{2,1,0:T(8,128)(2,1)S(1)} %pad_maximum_fusion.1.refs_3_), channel_id=1, source_target_pairs={{0,1},{1,2},{2,3},{3,0},{4,5},{5,6},{6,7},{7,4},{8,9},{9,10},{10,1... | collective-permute-start | bytes 6488072 | tf_op jit(solution)/shard_map/ppermute | solution.py:431
  185.7 93.9 %collective-permute-start.5 = (bf16[3,176,2048]{2,1,0:T(8,128)(2,1)S(1)}, bf16[3,176,2048]{2,1,0:T(8,128)(2,1)}, u32[]{:S(2)}, u32[]{:S(2)}) collective-permute-start(bf16[3,176,2048]{2,1,0:T(8,128)(2,1)S(1)} %pad_maximum_fusion.refs_2_), channel_id=1, source_target_pairs={{0,3},{1,0},{2,1},{3,2},{4,7},{5,4},{6,5},{7,6},{8,11},{9,8},{10,9... | collective-permute-start | bytes 6488072 | tf_op jit(solution)/shard_map/ppermute | solution.py:431
  233.3 46.4 %copy-start.16 = (bf16[3,176,2048]{2,1,0:T(8,128)(2,1)}, bf16[3,176,2048]{2,1,0:T(8,128)(2,1)S(1)}, u32[]{:S(2)}) copy-start(bf16[3,176,2048]{2,1,0:T(8,128)(2,1)S(1)} %collective-permute-done.3.refs_4_) | copy-start | bytes 6488068
  233.3 92.0 %collective-permute-start.7 = (bf16[3,176,2048]{2,1,0:T(8,128)(2,1)S(1)}, bf16[3,176,2048]{2,1,0:T(8,128)(2,1)}, u32[]{:S(2)}, u32[]{:S(2)}) collective-permute-start(bf16[3,176,2048]{2,1,0:T(8,128)(2,1)S(1)} %collective-permute-done.3.refs_4_), channel_id=1, source_target_pairs={{0,1},{1,2},{2,3},{3,0},{4,5},{5,6},{6,7},{7,4},{8,9},{9,10},{10,1... | collective-permute-start | bytes 6488072 | tf_op jit(solution)/shard_map/ppermute | solution.py:431
  233.3 46.4 %copy-start.17 = (bf16[3,176,2048]{2,1,0:T(8,128)(2,1)}, bf16[3,176,2048]{2,1,0:T(8,128)(2,1)S(1)}, u32[]{:S(2)}) copy-start(bf16[3,176,2048]{2,1,0:T(8,128)(2,1)S(1)} %collective-permute-done.6.refs_7_) | copy-start | bytes 6488068
  233.3 92.0 %collective-permute-start.8 = (bf16[3,176,2048]{2,1,0:T(8,128)(2,1)S(1)}, bf16[3,176,2048]{2,1,0:T(8,128)(2,1)}, u32[]{:S(2)}, u32[]{:S(2)}) collective-permute-start(bf16[3,176,2048]{2,1,0:T(8,128)(2,1)S(1)} %collective-permute-done.6.refs_7_), channel_id=1, source_target_pairs={{0,3},{1,0},{2,1},{3,2},{4,7},{5,4},{6,5},{7,6},{8,11},{9,8},{10,9... | collective-permute-start | bytes 6488072 | tf_op jit(solution)/shard_map/ppermute | solution.py:431
  279.6 1.3 copy-start.18
  333.9 7.6 %copy-start.12 = (s32[128,4]{0,1:T(4,128)S(1)}, s32[128,4]{0,1:T(4,128)}, u32[]{:S(2)}) copy-start(s32[128,4]{0,1:T(4,128)} %param.8) | copy-start | bytes 6148
  333.9 7.8 %copy-start.13 = (s32[4,128]{1,0:T(4,128)S(1)}, s32[4,128]{1,0:T(4,128)}, u32[]{:S(2)}) copy-start(s32[4,128]{1,0:T(4,128)} %get-tuple-element.48.route_other_ref) | copy-start | bytes 6148
  333.9 8.8 %copy-start.14 = (f32[128,4]{0,1:T(4,128)S(1)}, f32[128,4]{0,1:T(4,128)}, u32[]{:S(2)}) copy-start(f32[128,4]{0,1:T(4,128)} %param.9) | copy-start | bytes 6148
  333.9 44.6 %all-to-all-start.2 = ((bf16[32,24,2048]{2,1,0:T(8,128)(2,1)}), bf16[32,24,2048]{2,1,0:T(8,128)(2,1)S(1)}, u32[]{:S(2)}, u32[]{:S(2)}) async-start(bf16[32,24,2048]{2,1,0:T(8,128)(2,1)} %bitcast.74), calls=%async_computation.2 | async-start | bytes 6291456 | tf_op jit(solution)/shard_map/all_to_all | solution.py:434
  355.2 27.0 %collective-permute-start.12 = (bf16[256,2048]{1,0:T(8,128)(2,1)}, bf16[256,2048]{1,0:T(8,128)(2,1)}, u32[]{:S(2)}, u32[]{:S(2)}) collective-permute-start(bf16[256,2048]{1,0:T(8,128)(2,1)} %get-tuple-element.21), channel_id=1, source_target_pairs={{0,2},{1,3},{2,0},{3,1},{4,6},{5,7},{6,4},{7,5},{8,10},{9,11},{10,... | collective-permute-start | bytes 3145736 | tf_op jit(solution)/shard_map/ppermute | solution.py:431
  358.5 23.8 %collective-permute-start.11 = (f32[8,128]{1,0:T(8,128)}, f32[8,128]{1,0:T(8,128)S(1)}, u32[]{:S(2)}, u32[]{:S(2)}) collective-permute-start(f32[8,128]{1,0:T(8,128)} %get-tuple-element.19), channel_id=1, source_target_pairs={{0,2},{1,3},{2,0},{3,1},{4,6},{5,7},{6,4},{7,5},{8,10},{9,11},{10,... | collective-permute-start | bytes 12296 | tf_op jit(solution)/shard_map/ppermute | solution.py:431
  382.3 0.6 copy-start.15

commit v4 on v3

--- a/solution.py
+++ b/solution.py
@@ -15,7 +15,7 @@
 OWN_ROWS = 32
 OTHER_ROWS = 24
 OUT0_ROWS = 40
-OUT1_ROWS = 24
+OUT1_ROWS = 16
 
 
 def slots_of(route_t):
@@ -62,13 +62,15 @@
     ninth = slots_of(route) == 8
     base = (route // 2) * OTHER_ROWS
     x_place = jnp.where(ninth, base + 16 + 4 * odd, -1)
-    g_place = jnp.where(ninth, base + 18 + 3 * odd, -1)
+    g_place = jnp.where(ninth, base + 18 + 4 * odd, -1)
     route = route_other_ref[...]
-    even = route % 2 == 0
+    odd = route % 2
     slot = slots_of(route)
+    ninth = slot == 8
     base = (route // 2) * OTHER_ROWS
-    x_far = jnp.where(even, base + jnp.where(slot < 8, slot, 17), -1)
-    g_far = jnp.where(even, base + jnp.where(slot < 8, slot + 8, 19), -1)
+    kept = (odd == 0) | ninth
+    x_far = jnp.where(kept, base + jnp.where(ninth, 17 + 4 * odd, slot), -1)
+    g_far = jnp.where(kept, base + jnp.where(ninth, 19 + 4 * odd, slot + 8), -1)
     rows[...] = dispatch_rows(
         [(x_place, tokens[...]), (g_place, grads[...]), (x_far, tokens_other[...]), (g_far, grads_other[...])],
         block,
@@ -155,8 +157,9 @@
 
 
 def expert_pair_kernel(nodes, n_pieces, *refs):
-    arrived, arrived_other, pieces, home = refs[0], refs[1], refs[2 : 2 + n_pieces], refs[2 + n_pieces]
-    xs, gs, rest, wg, wu, wd, outs, backs, out_rest, sems = refs[3 + n_pieces :]
+    arrived, arrived_other, pieces = refs[0], refs[1], refs[2 : 2 + n_pieces]
+    home, ninth_out, ninth_back = refs[2 + n_pieces : 5 + n_pieces]
+    xs, gs, rest, wg, wu, wd, outs, backs, sems = refs[5 + n_pieces :]
     main, small = nodes * 16, nodes * 2
     fetch_rows(nodes, arrived, OWN_ROWS, 0, xs, 0, sems.at[0])
     fetch_rows(nodes, arrived_other, OTHER_ROWS, 0, xs, nodes * 8, sems.at[0])
@@ -172,7 +175,7 @@
     landed(wu, sems.at[4])
     landed(gs.at[pl.ds(0, main)], sems.at[2])
     landed(wd, sems.at[5])
-    size = (main + small) // 2
+    size = (main + small) // 3
 
     def block(b, carry):
         at = pl.ds(pl.multiple_of(b * size, 16), size)
@@ -181,39 +184,53 @@
         backs[at] = (by_row(d_gate, wg[...]) + by_row(d_up, wu[...])).astype(BF)
         return carry
 
-    lax.fori_loop(0, 2, block, 0)
+    lax.fori_loop(0, 3, block, 0)
     put_rows(nodes, outs, 0, home, OUT0_ROWS, 0, sems.at[0])
     put_rows(nodes, outs, nodes * 8, home, OUT0_ROWS, 8, sems.at[0])
     put_rows(nodes, backs, 0, home, OUT0_ROWS, 16, sems.at[1])
     put_rows(nodes, backs, nodes * 8, home, OUT0_ROWS, 24, sems.at[1])
-    out_rest[...] = (
-        by_row(picked(nodes, 2, 0, True), outs[pl.ds(main, small)])
-        + by_row(picked(nodes, 2, 2, True), backs[pl.ds(main, small)])
-    ).astype(BF)
-    put_rows(nodes, out_rest, 0, home, OUT0_ROWS, 32, sems.at[2])
+    ninth_out[...] = outs[pl.ds(main, small)]
+    ninth_back[...] = backs[pl.ds(main, small)]
     landed(outs.at[pl.ds(0, main)], sems.at[0])
     landed(backs.at[pl.ds(0, main)], sems.at[1])
-    landed(out_rest, sems.at[2])
-
-
-def expert_near_kernel(nodes, n_pieces, *refs):
-    arrived, arrived_other, pieces = refs[0], refs[1], refs[2 : 2 + n_pieces]
-    out_part, back_part, xs, gs = refs[2 + n_pieces : 6 + n_pieces]
-    rest, wg, wu, wd, sems = refs[6 + n_pieces :]
-    main, small = nodes * 8, nodes
-    fetch_rows(nodes, arrived, OWN_ROWS, 16, xs, 0, sems.at[0])
-    fetch_rows(nodes, arrived, OWN_ROWS, 24, gs, 0, sems.at[2])
+
+
+def expert_ninth_kernel(nodes, n_pieces, *refs):
+    arrived_other, pair_out, pair_back, pieces = refs[0], refs[1], refs[2], refs[3 : 3 + n_pieces]
+    home = refs[4 + n_pieces]
+    rest, wg, wu, wd, out_rest, sems = refs[5 + n_pieces :]
     fetch_rows(nodes, arrived_other, OTHER_ROWS, 16, rest, 0, sems.at[1])
     fetch_weights(pieces, (wg, wu, wd), sems, 3)
     landed(rest, sems.at[1])
-    landed(xs.at[pl.ds(0, main)], sems.at[0])
-    landed(gs.at[pl.ds(0, main)], sems.at[2])
-    xs[pl.ds(main, small)] = by_row(picked(nodes, 1, 4, False), rest[...]).astype(BF)
-    gs[pl.ds(main, small)] = by_row(picked(nodes, 1, 5, False), rest[...]).astype(BF)
+    xs = by_row(picked(nodes, 2, 4, False), rest[...]).astype(BF)
+    gs = by_row(picked(nodes, 2, 6, False), rest[...]).astype(BF)
+    carried = by_row(picked(nodes, 2, 0, True), pair_out[...]) + by_row(picked(nodes, 2, 2, True), pair_back[...])
     landed(wg, sems.at[3])
     landed(wu, sems.at[4])
     landed(wd, sems.at[5])
-    size = (main + small) // 2
+    hidden, d_gate, d_up = inner(xs, gs, wg[...], wu[...], wd[...])
+    out = by_row(hidden, wd[...]).astype(BF)
+    back = (by_row(d_gate, wg[...]) + by_row(d_up, wu[...])).astype(BF)
+    out_rest[...] = (
+        carried + by_row(picked(nodes, 2, 4, True), out) + by_row(picked(nodes, 2, 6, True), back)
+    ).astype(BF)
+    put_rows(nodes, out_rest, 0, home, OUT0_ROWS, 32, sems.at[2])
+    landed(out_rest, sems.at[2])
+
+
+def expert_near_kernel(nodes, n_pieces, *refs):
+    arrived, pieces = refs[0], refs[1 : 1 + n_pieces]
+    out_part, back_part, xs, gs = refs[1 + n_pieces : 5 + n_pieces]
+    wg, wu, wd, sems = refs[5 + n_pieces :]
+    fetch_rows(nodes, arrived, OWN_ROWS, 16, xs, 0, sems.at[0])
+    fetch_rows(nodes, arrived, OWN_ROWS, 24, gs, 0, sems.at[2])
+    fetch_weights(pieces, (wg, wu, wd), sems, 3)
+    landed(xs, sems.at[0])
+    landed(gs, sems.at[2])
+    landed(wg, sems.at[3])
+    landed(wu, sems.at[4])
+    landed(wd, sems.at[5])
+    size = nodes * 4
 
     def block(b, carry):
         at = pl.ds(pl.multiple_of(b * size, 16), size)
@@ -228,8 +245,7 @@
 def expert_far_kernel(nodes, n_pieces, *refs):
     xs, gs, out_at, back_at = refs[:4]
     pieces, home = refs[4 : 4 + n_pieces], refs[4 + n_pieces]
-    out_part, back_part, wg, wu, wd, outs, backs, out_rest, sems = refs[5 + n_pieces :]
-    main, small = nodes * 8, nodes
+    out_part, back_part, wg, wu, wd, outs, backs, sems = refs[5 + n_pieces :]
     fetch_weights(pieces, (wg, wu, wd), sems, 3)
     pltpu.make_async_copy(out_at, out_part, sems.at[6]).start()
     pltpu.make_async_copy(back_at, back_part, sems.at[7]).start()
@@ -243,14 +259,8 @@
     landed(back_part, sems.at[7])
     backs[...] = (by_row(d_gate, wg[...]) + by_row(d_up, wu[...]) + back_part[...]).astype(BF)
     put_rows(nodes, backs, 0, home, OUT1_ROWS, 8, sems.at[1])
-    out_rest[...] = (
-        by_row(picked(nodes, 1, 0, True), outs[pl.ds(main, small)])
-        + by_row(picked(nodes, 1, 1, True), backs[pl.ds(main, small)])
-    ).astype(BF)
-    put_rows(nodes, out_rest, 0, home, OUT1_ROWS, 16, sems.at[2])
-    landed(outs.at[pl.ds(0, main)], sems.at[0])
-    landed(backs.at[pl.ds(0, main)], sems.at[1])
-    landed(out_rest, sems.at[2])
+    landed(outs, sems.at[0])
+    landed(backs, sems.at[1])
 
 
 def on_chip(value):
@@ -276,42 +286,59 @@
 def expert_pair(arrived, arrived_other, pieces, nodes):
     width = arrived.shape[1]
     rows, hidden = nodes * 18, len(pieces) * pieces[0].shape[1]
+    ninth = jax.ShapeDtypeStruct((nodes * 2, width), BF)
     scratch = [(rows, width), (rows, width), (nodes * 8, width)] + [(hidden, width)] * 3
-    scratch += [(rows, width), (rows, width), (nodes * 8, width)]
+    scratch += [(rows, width), (rows, width)]
     return pl.pallas_call(
         functools.partial(expert_pair_kernel, nodes, len(pieces)),
         name="expert_pair",
-        out_shape=jax.ShapeDtypeStruct((nodes * OUT0_ROWS, width), BF),
+        out_shape=(jax.ShapeDtypeStruct((nodes * OUT0_ROWS, width), BF), ninth, ninth),
         in_specs=[ANY, WHOLE] + [ANY] * len(pieces),
-        out_specs=ANY,
+        out_specs=(ANY, WHOLE, WHOLE),
         scratch_shapes=[pltpu.VMEM(s, BF) for s in scratch] + [pltpu.SemaphoreType.DMA((6,))],
         compiler_params=room(46),
         cost_estimate=expert_cost(rows, hidden, width),
     )(arrived, arrived_other, *pieces)
 
 
-def expert_near(arrived, arrived_other, pieces, nodes):
+def expert_ninth(arrived_other, pair_rows, pieces, nodes):
+    home, pair_out, pair_back = pair_rows
+    width = home.shape[1]
+    rows, hidden = nodes * 2, len(pieces) * pieces[0].shape[1]
+    scratch = [(nodes * 8, width)] + [(hidden, width)] * 3 + [(nodes * 8, width)]
+    return pl.pallas_call(
+        functools.partial(expert_ninth_kernel, nodes, len(pieces)),
+        name="expert_ninth",
+        out_shape=jax.ShapeDtypeStruct(home.shape, BF),
+        in_specs=[WHOLE] * 3 + [ANY] * (len(pieces) + 1),
+        out_specs=ANY,
+        input_output_aliases={3 + len(pieces): 0},
+        scratch_shapes=[pltpu.VMEM(s, BF) for s in scratch] + [pltpu.SemaphoreType.DMA((6,))],
+        compiler_params=room(40),
+        cost_estimate=expert_cost(rows, hidden, width),
+    )(arrived_other, pair_out, pair_back, *pieces, home)
+
+
+def expert_near(arrived, pieces, nodes):
     width = arrived.shape[1]
-    rows, hidden = nodes * 9, len(pieces) * pieces[0].shape[1]
-    scratch = [(nodes * 8, width)] + [(hidden, width)] * 3
+    rows, hidden = nodes * 8, len(pieces) * pieces[0].shape[1]
     return pl.pallas_call(
         functools.partial(expert_near_kernel, nodes, len(pieces)),
         name="expert_near",
         out_shape=tuple(jax.ShapeDtypeStruct((rows, width), t) for t in (F32, F32, BF, BF)),
-        in_specs=[ANY, WHOLE] + [ANY] * len(pieces),
+        in_specs=[ANY] * (1 + len(pieces)),
         out_specs=(WHOLE,) * 4,
-        scratch_shapes=[pltpu.VMEM(s, BF) for s in scratch] + [pltpu.SemaphoreType.DMA((6,))],
+        scratch_shapes=[pltpu.VMEM((hidden, width), BF)] * 3 + [pltpu.SemaphoreType.DMA((6,))],
         compiler_params=room(46),
         cost_estimate=expert_cost(rows, hidden, width),
-    )(arrived, arrived_other, *pieces)
+    )(arrived, *pieces)
 
 
 def expert_far(near, pieces, nodes):
     out_part, back_part, xs, gs = near
     rows, width = xs.shape
     hidden = len(pieces) * pieces[0].shape[1]
-    scratch = [((rows, width), F32)] * 2 + [((hidden, width), BF)] * 3
-    scratch += [((rows, width), BF)] * 2 + [((nodes * 8, width), BF)]
+    scratch = [((rows, width), F32)] * 2 + [((hidden, width), BF)] * 3 + [((rows, width), BF)] * 2
     return pl.pallas_call(
         functools.partial(expert_far_kernel, nodes, len(pieces)),
         name="expert_far",
@@ -319,7 +346,7 @@
         in_specs=[WHOLE] * 2 + [ANY] * (2 + len(pieces)),
         out_specs=ANY,
         scratch_shapes=[pltpu.VMEM(s, t) for s, t in scratch] + [pltpu.SemaphoreType.DMA((8,))],
-        compiler_params=room(57),
+        compiler_params=room(61),
         cost_estimate=expert_cost(rows, hidden, width),
     )(on_chip(xs), on_chip(gs), out_part, back_part, *pieces)
 
@@ -349,8 +376,11 @@
     total = mixed(rows, places_ref[...], values_ref[...])
     back[...] = total[: 2 * toks].astype(BF)
     own[...] = total[2 * toks :]
-    dw_other[...] = jnp.transpose(weight_grads(rows, grads_other[...], places_ref[:toks]))[:8]
-    dw_own[...] = jnp.transpose(weight_grads(rows, grads[...], places_ref[2 * toks : 3 * toks]))[:8]
+    both = jnp.concatenate([grads_other[...], grads[...]], axis=0)
+    heads = jnp.concatenate([places_ref[:toks], places_ref[2 * toks : 3 * toks]], axis=0)
+    dw = weight_grads(rows, both, heads)
+    dw_other[...] = jnp.transpose(dw[:toks])[:8]
+    dw_own[...] = jnp.transpose(dw[toks:])[:8]
 
 
 def combine_full_kernel(
@@ -412,7 +442,7 @@
             pltpu.VMEM((2 * toks, width), BF),
             pltpu.SemaphoreType.DMA((3,)),
         ],
-        compiler_params=room(60),
+        compiler_params=room(57),
         cost_estimate=pl.CostEstimate(
             flops=6 * toks * home.shape[0] * width, transcendentals=0, bytes_accessed=8 * 1024 * 1024
         ),
@@ -450,56 +480,65 @@
 
     p0a, p0b, p1a, p1b = piece(0, 0), piece(0, 1), piece(1, 0), piece(1, 1)
     w0 = [p0a, p0b, send(p0a, down), send(p0b, up)]
+    below_b, above_a = send(p1b, up), send(p1a, down)
     below_a, above_b = send(p1a, up), send(p1b, down)
-    below_b, above_a = send(p1b, up), send(p1a, down)
-    far_a, far_b = send(below_a, up), send(above_b, down)
-    w1 = [p1a, p1b, below_a, below_b, above_a, above_b, far_a, far_b]
+    pair1 = [p1a, p1b, below_b, above_a]
+    near1 = pair1 + [below_a, above_b]
+    far1 = [send(p1a, across), send(p1b, across)]
 
     slot_own, slot_other = slots_of(route_t), slots_of(route_other)
 
     own_rows = dispatch(dispatch_own_kernel, nodes * OWN_ROWS, route_t, tokens, grad_out)
     arrived = exchange(own_rows)
     other_rows = dispatch(
-        dispatch_other_kernel, nodes * OTHER_ROWS, route_t, route_other, tokens, grad_out, tokens_other, grads_other
+        dispatch_other_kernel,
+        nodes * OTHER_ROWS,
+        route_t,
+        route_other,
+        tokens,
+        grad_out,
+        tokens_other,
+        grads_other,
     )
     arrived_other = exchange(other_rows)
 
     arrived_other = on_chip(arrived_other)
-    rows0 = expert_pair(arrived, arrived_other, w0, nodes)
+    pair_rows = expert_pair(arrived, arrived_other, w0, nodes)
+    rows0 = expert_ninth(arrived_other, pair_rows, pair1, nodes)
     home0 = exchange(rows0)
-    near = expert_near(arrived, arrived_other, w1[:6], nodes)
-    rows1 = expert_far(near, w1[6:], nodes)
+    near = expert_near(arrived, near1, nodes)
+    rows1 = expert_far(near, far1, nodes)
     home1 = exchange(rows1)
 
-    own_even, other_even = route_t % 2 == 0, route_other % 2 == 0
-
-    def places(route_rows, row, keep):
-        chunk, index = row
-        return jnp.where(keep, (route_rows // 2) * chunk + index, -1)
+    def pair_place(route_rows, slot, main, rest):
+        odd = route_rows % 2
+        ninth = slot == 8
+        index = jnp.where(ninth, rest + 4 * odd, main + slot)
+        return jnp.where((odd == 0) | ninth, (route_rows // 2) * OUT0_ROWS + index, -1)
+
+    def home_place(main, rest):
+        return pair_place(route_t, slot_own, main, rest)
 
     def other_place(main, rest):
-        index = jnp.where(slot_other < 8, main + slot_other, rest)
-        return places(route_other, (OUT0_ROWS, index), other_even)
-
-    def home_place(main, rest):
-        index = jnp.where(slot_own < 8, main + slot_own, rest)
-        return places(route_t, (OUT0_ROWS, index), own_even)
-
-    def full_place(main, rest):
-        index = jnp.where(slot_own < 8, main + slot_own, rest)
-        return places(route_t, (OUT1_ROWS, index), ~own_even)
+        return pair_place(route_other, slot_other, main, rest)
+
+    def full_place(main):
+        kept = (route_t % 2 == 1) & (slot_own < 8)
+        return jnp.where(kept, (route_t // 2) * OUT1_ROWS + main + slot_own, -1)
 
     def stacked(*parts):
         return jnp.concatenate([p.T for p in parts], axis=0)
 
     places0 = stacked(other_place(8, 33), other_place(24, 35), home_place(0, 32), home_place(16, 34))
-    places1 = stacked(full_place(0, 16), full_place(8, 17))
+    places1 = stacked(full_place(0), full_place(8))
     values0 = stacked(weight_other, weight_other, weight_t, weight_t)
     values1 = values0[2 * toks :]
     back, kept, dw_other, dw_own = combine_pair(home0, places0, values0, grad_out, grads_other)
     returned = send(back, across)
     dw_back = send(dw_other, across)
-    combined, d_tokens, d_weights_t = combine_full(home1, places1, values1, grad_out, kept, returned, dw_own, dw_back)
+    combined, d_tokens, d_weights_t = combine_full(
+        home1, places1, values1, grad_out, kept, returned, dw_own, dw_back
+    )
     return combined, d_tokens, d_weights_t.T
 
 

time: 390 us -> 440 us (1.13)
  waiting for transfers between devices: 226 us -> 270 us
  Pallas kernels: 82.8 us -> 88 us
    ppermute x13, waiting for transfers between devices: 177 us -> 229 us  [send(): return lax.ppermute(value, 'local', pairs)]
    pallas_call x0 -> x1, Pallas kernels: none -> 10.8 us  [expert_ninth(): pl.pallas_call(functools.partial(expert_ninth_kernel, nodes, len(pieces))...]
    all_to_all x4, waiting for transfers between devices: 49.5 us -> 40.3 us  [exchange(): return lax.all_to_all(rows, 'node', split_axis=0, concat_axis=0, tiled=True)]
    unnamed x40 -> x36, local copies, waits for them, and re-layouts: 9.67 us -> 12 us
  transfers between devices with their start and end apart: 17 -> 17, of which waited for: 8 -> 9; matrix products, arithmetic and copies ran while one was open for 3% -> 3% of each run, Pallas kernels for 12% -> 15%
where the time goes in v4:
time: 440 us
  waiting for transfers between devices  270 us (61%)
  Pallas kernels  88 us (20%)
  starting transfers between devices  56.5 us (13%)
  local copies, waits for them, and re-layouts  18.5 us (4%)
  other arithmetic  5.64 us (1%)
    ppermute x13, waiting for transfers between devices, send(): return lax.ppermute(value, 'local', pairs)  229 us
    all_to_all x4, waiting for transfers between devices, exchange(): return lax.all_to_all(rows, 'node', split_axis=0, concat_axis=0, tiled=True)  40.3 us
    all_to_all x4, starting transfers between devices, exchange(): return lax.all_to_all(rows, 'node', split_axis=0, concat_axis=0, tiled=True)  30.4 us
    ppermute x13, starting transfers between devices, send(): return lax.ppermute(value, 'local', pairs)  26.1 us
    pallas_call x1, Pallas kernels, expert_pair(): pl.pallas_call(functools.partial(expert_pair_kernel, nodes, len(pieces)),...  23.3 us
    pallas_call x1, Pallas kernels, expert_near(): pl.pallas_call(functools.partial(expert_near_kernel, nodes, len(pieces)),...  18.8 us
    pallas_call x2, Pallas kernels, dispatch(): pl.pallas_call(kernel, grid=(steps,), out_shape=jax.ShapeDtypeStruct((row...  12.7 us
    unnamed x36, local copies, waits for them, and re-layouts  12 us
  transfers between devices with their start and end apart: 17, of which 9 were waited for; matrix products, arithmetic and copies ran while one was open for 3% of the time, Pallas kernels for 15%

profile of v4, /device:TPU:2, one launch (start us, length us, event | category | flops | bytes accessed | tf_op | source)
XLA Modules:
  0.0 439.6 jit_solution(18394752607418719575)
XLA Ops:
  0.6 4.0 collective-permute-start.8
  4.6 0.1 collective-permute-start.7
  4.7 0.7 bitcast_convert_fusion
  5.4 0.7 pad_maximum_fusion.6
  6.1 3.4 collective-permute-start.6
  9.5 18.6 %collective-permute-done.6 = f32[8,128]{1,0:T(8,128)S(1)} collective-permute-done((f32[8,128]{1,0:T(8,128)S(1)}, f32[8,128]{1,0:T(8,128)S(1)}, u32[]{:S(2)}, u32[]{:S(2)}) %collective-permute-start.6) | collective-permute-done | bytes 4128 | tf_op jit(solution)/shard_map/ppermute | solution.py:461
  28.0 0.6 slice_bitcast_fusion
  28.6 0.0 copy-start.10
  28.7 0.8 copy-done.9
  29.4 0.2 copy-done.10
  29.6 6.9 %shard_map.95 = bf16[768,2048]{1,0:T(8,128)(2,1)} custom-call(s32[4,128]{1,0:T(4,128)} %bitcast.81, s32[4,128]{1,0:T(4,128)} %get-tuple-element.54.route_other_ref, bf16[128,2048]{1,0:T(8,128)(2,1)} %tokens.3, bf16[128,2048]{1,0:T(8,128)(2,1)} %grads_at.1, bf16[128,2048]{1,0:T(8,128)(2,1)} %copy-done.10, bf16[128,2048]{1,0:T(8,128)(2,1)} %copy-done.9), custom_call_target="tpu_custom_call" | custom-call | flops 805306368 | bytes 6291456 | tf_op jit(solution)/shard_map/pallas_call | solution.py:88
  36.5 7.6 %all-to-all-start.2 = ((bf16[32,24,2048]{2,1,0:T(8,128)(2,1)}), bf16[32,24,2048]{2,1,0:T(8,128)(2,1)S(1)}, u32[]{:S(2)}, u32[]{:S(2)}) async-start(bf16[32,24,2048]{2,1,0:T(8,128)(2,1)} %bitcast.77), calls=%async_computation.2 | async-start | bytes 6291456 | tf_op jit(solution)/shard_map/all_to_all | solution.py:464
  44.2 5.8 %shard_map.94 = bf16[1024,2048]{1,0:T(8,128)(2,1)} custom-call(s32[4,128]{1,0:T(4,128)} %bitcast.82, bf16[128,2048]{1,0:T(8,128)(2,1)} %tokens.3, bf16[128,2048]{1,0:T(8,128)(2,1)} %grads_at.1), custom_call_target="tpu_custom_call" | custom-call | flops 1073741824 | bytes 8388608 | tf_op jit(solution)/shard_map/pallas_call | solution.py:88
  50.0 31.3 %all-to-all-done.2 = bf16[32,24,2048]{2,1,0:T(8,128)(2,1)S(1)} async-done(((bf16[32,24,2048]{2,1,0:T(8,128)(2,1)}), bf16[32,24,2048]{2,1,0:T(8,128)(2,1)S(1)}, u32[]{:S(2)}, u32[]{:S(2)}) %all-to-all-start.2) | async-done | bytes 3145760 | tf_op jit(solution)/shard_map/all_to_all | solution.py:464
  81.2 7.8 %all-to-all-start = ((bf16[32,32,2048]{2,1,0:T(8,128)(2,1)}), bf16[32,32,2048]{2,1,0:T(8,128)(2,1)}, u32[]{:S(2)}, u32[]{:S(2)}) async-start(bf16[32,32,2048]{2,1,0:T(8,128)(2,1)} %bitcast.76), calls=%async_computation | async-start | bytes 8388608 | tf_op jit(solution)/shard_map/all_to_all | solution.py:464
  89.1 0.0 copy-start.6
  89.1 0.0 copy-start.7
  89.1 2.1 fusion.27
  91.2 0.5 copy-done.6
  91.7 0.9 copy-done.7
  92.6 1.0 fusion.25
  93.6 0.2 pad_maximum_fusion.3.refs_3_
  93.9 1.4 collective-permute-start.10
  95.2 0.2 pad_maximum_fusion.2.refs_2_
  95.5 3.2 collective-permute-start.9
  98.7 1.6 pad_maximum_fusion.1.refs_2_.refs_4_
  100.3 1.6 pad_maximum_fusion.refs_1_.refs_3_
  101.8 3.2 collective-permute-start.1
  105.1 40.1 %collective-permute-done.10.refs_5_ = bf16[3,176,2048]{2,1,0:T(8,128)(2,1)S(1)} collective-permute-done((bf16[3,176,2048]{2,1,0:T(8,128)(2,1)S(1)}, bf16[3,176,2048]{2,1,0:T(8,128)(2,1)S(1)}, u32[]{:S(2)}, u32[]{:S(2)}) %collective-permute-start.10) | collective-permute-done | bytes 2162720 | tf_op jit(solution)/shard_map/ppermute | solution.py:461
  145.2 1.4 copy-done.17
  146.6 1.6 copy-done.1
  148.2 1.6 copy-done.3
  149.8 23.3 %expert_pair.1 = (bf16[1280,2048]{1,0:T(8,128)(2,1)}, bf16[64,2048]{1,0:T(8,128)(2,1)S(1)}, bf16[64,2048]{1,0:T(8,128)(2,1)S(1)}) custom-call(bf16[1024,2048]{1,0:T(8,128)(2,1)} %bitcast.2.refs_0_, bf16[768,2048]{1,0:T(8,128)(2,1)S(1)} %bitcast.72, bf16[3,176,2048]{2,1,0:T(8,128)(2,1)S(1)} %copy-done.3, bf16[3,176,2048]{2,1,0:T(8,128)(2,1)S(1)} %copy-done.1, ...), custom_call_target="tpu_custom_call" | custom-call | flops 9965666304 | bytes 18087936 | tf_op jit(solution)/shard_map/expert_pair/pallas_call | solution.py:292
  173.1 18.0 %collective-permute-done.refs_3_.refs_5_ = bf16[3,176,2048]{2,1,0:T(8,128)(2,1)} collective-permute-done((bf16[3,176,2048]{2,1,0:T(8,128)(2,1)}, bf16[3,176,2048]{2,1,0:T(8,128)(2,1)}, u32[]{:S(2)}, u32[]{:S(2)}) %collective-permute-start) | collective-permute-done | bytes 2162720 | tf_op jit(solution)/shard_map/ppermute | solution.py:461
  191.1 0.6 collective-permute-done.1.refs_4_.refs_6_
  191.7 10.8 %expert_ninth.1 = bf16[1280,2048]{1,0:T(8,128)(2,1)} custom-call(bf16[768,2048]{1,0:T(8,128)(2,1)S(1)} %bitcast.73, bf16[64,2048]{1,0:T(8,128)(2,1)S(1)} %get-tuple-element.21.refs_1_, bf16[64,2048]{1,0:T(8,128)(2,1)S(1)} %get-tuple-element.22.refs_2_, bf16[3,176,2048]{2,1,0:T(8,128)(2,1)} %pad_maximum_fusion.refs_1_.refs_3_, ...), custom_call_target="tpu_custom_call", output_to_operand_aliasing={{}: (7, {})} | custom-call | flops 1107296256 | bytes 9699328 | tf_op jit(solution)/shard_map/expert_ninth/pallas_call | solution.py:309
  202.5 0.0 copy-start.11
  202.5 7.5 %all-to-all-start.3 = ((bf16[32,40,2048]{2,1,0:T(8,128)(2,1)}), bf16[32,40,2048]{2,1,0:T(8,128)(2,1)}, u32[]{:S(2)}, u32[]{:S(2)}) async-start(bf16[32,40,2048]{2,1,0:T(8,128)(2,1)} %bitcast.75), calls=%async_computation.3 | async-start | bytes 10485760 | tf_op jit(solution)/shard_map/all_to_all | solution.py:464
  210.0 3.8 collective-permute-start.3
  213.8 1.5 collective-permute-start.5
  215.4 2.0 collective-permute-start.4
  217.4 0.2 select_reduce_fusion.7
  217.5 135.9 %collective-permute-done.3.refs_6_ = bf16[3,176,2048]{2,1,0:T(8,128)(2,1)S(1)} collective-permute-done((bf16[3,176,2048]{2,1,0:T(8,128)(2,1)}, bf16[3,176,2048]{2,1,0:T(8,128)(2,1)S(1)}, u32[]{:S(2)}, u32[]{:S(2)}) %collective-permute-start.3) | collective-permute-done | bytes 2162720 | tf_op jit(solution)/shard_map/ppermute | solution.py:461
  353.4 3.3 collective-permute-done.2.refs_5_
  356.7 1.4 copy-done.16
  358.1 18.8 %expert_near.1 = (f32[256,2048]{1,0:T(8,128)S(1)}, f32[256,2048]{1,0:T(8,128)S(1)}, bf16[256,2048]{1,0:T(8,128)(2,1)S(1)}, bf16[256,2048]{1,0:T(8,128)(2,1)S(1)}) custom-call(bf16[1024,2048]{1,0:T(8,128)(2,1)} %bitcast.2.refs_0_, bf16[3,176,2048]{2,1,0:T(8,128)(2,1)} %pad_maximum_fusion.refs_1_.refs_3_, ...), custom_call_target="tpu_custom_call" | custom-call | flops 6643777536 | bytes 17170432 | tf_op jit(solution)/shard_map/expert_near/pallas_call | solution.py:325
  377.0 1.3 copy-done.4
  378.3 1.3 copy-done.5
  379.6 7.3 %expert_far.1 = bf16[512,2048]{1,0:T(8,128)(2,1)} custom-call(bf16[256,2048]{1,0:T(8,128)(2,1)S(1)} %get-tuple-element.17.refs_0_, bf16[256,2048]{1,0:T(8,128)(2,1)S(1)} %get-tuple-element.18.refs_1_, f32[256,2048]{1,0:T(8,128)} %copy-done.4, f32[256,2048]{1,0:T(8,128)} %copy-done.5, bf16[3,176,2048]{2,1,0:T(8,128)(2,1)} %collective-permute-done.4.refs_4_, ...), custom_call_target="tpu_custom_call" | custom-call | flops 2214592512 | bytes 8519680 | tf_op jit(solution)/shard_map/expert_far/pallas_call | solution.py:342
  386.9 0.0 copy-start.12
  387.0 0.0 copy-start.13
  387.0 7.4 %all-to-all-start.1 = ((bf16[32,16,2048]{2,1,0:T(8,128)(2,1)}), bf16[32,16,2048]{2,1,0:T(8,128)(2,1)S(1)}, u32[]{:S(2)}, u32[]{:S(2)}) async-start(bf16[32,16,2048]{2,1,0:T(8,128)(2,1)} %bitcast.78), calls=%async_computation.1 | async-start | bytes 4194304 | tf_op jit(solution)/shard_map/all_to_all | solution.py:464
  394.4 0.2 select_reduce_fusion.3
  394.6 0.9 copy.45.places_ref
  395.5 0.9 copy.46.values_ref
  396.4 9.7 %combine_pair.1 = (bf16[256,2048]{1,0:T(8,128)(2,1)}, f32[256,2048]{1,0:T(8,128)}, f32[8,128]{1,0:T(8,128)}, f32[8,128]{1,0:T(8,128)}) custom-call(bf16[1280,2048]{1,0:T(8,128)(2,1)} %bitcast.21.home, s32[512,4]{1,0:T(8,128)} %copy.45.places_ref, f32[512,4]{1,0:T(8,128)} %copy.46.values_ref, bf16[128,2048]{1,0:T(8,128)(2,1)} %grads_at.1, ...), custom_call_target="tpu_custom_call" | custom-call | flops 4026531840 | bytes 12582912 | tf_op jit(solution)/shard_map/combine_pair/pallas_call | solution.py:411
  406.1 3.5 collective-permute-start.11
  409.6 0.8 copy.47.places_ref
  410.5 0.8 copy.48.values_ref
  411.3 9.0 %all-to-all-done.1 = bf16[32,16,2048]{2,1,0:T(8,128)(2,1)S(1)} async-done(((bf16[32,16,2048]{2,1,0:T(8,128)(2,1)}), bf16[32,16,2048]{2,1,0:T(8,128)(2,1)S(1)}, u32[]{:S(2)}, u32[]{:S(2)}) %all-to-all-start.1) | async-done | bytes 2097184 | tf_op jit(solution)/shard_map/all_to_all | solution.py:464
  420.3 12.8 %collective-permute-done.11.dw_back = f32[8,128]{1,0:T(8,128)S(1)} collective-permute-done((f32[8,128]{1,0:T(8,128)}, f32[8,128]{1,0:T(8,128)S(1)}, u32[]{:S(2)}, u32[]{:S(2)}) %collective-permute-start.11) | collective-permute-done | bytes 4128 | tf_op jit(solution)/shard_map/ppermute | solution.py:461
  433.1 0.6 copy-done.14
  433.7 0.4 copy-done.8
  434.1 5.3 %combine_full.1 = (bf16[128,2048]{1,0:T(8,128)(2,1)}, bf16[128,2048]{1,0:T(8,128)(2,1)}, f32[4,128]{1,0:T(4,128)}) custom-call(bf16[512,2048]{1,0:T(8,128)(2,1)S(1)} %bitcast.74, s32[256,4]{1,0:T(8,128)} %copy.47.places_ref, f32[256,4]{1,0:T(8,128)} %copy.48.values_ref, f32[8,128]{1,0:T(8,128)} %get-tuple-element.24.dw_own, f32[8,128]{1,0:T(8,128)} %copy-done.14, ...), custom_call_target="tpu_custom_call" | custom-call | flops 805306368 | bytes 8388608 | tf_op jit(solution)/shard_map/combine_full/pallas_call | solution.py:429
  (37 shorter events, 0.1 us)
Async XLA Ops:
  0.6 28.0 %collective-permute-start.8 = (bf16[128,2048]{1,0:T(8,128)(2,1)}, bf16[128,2048]{1,0:T(8,128)(2,1)S(1)}, u32[]{:S(2)}, u32[]{:S(2)}) collective-permute-start(bf16[128,2048]{1,0:T(8,128)(2,1)} %grads_at.1), channel_id=1, source_target_pairs={{0,2},{1,3},{2,0},{3,1},{4,6},{5,7},{6,4},{7,5},{8,10},{9,11},{10,... | collective-permute-start | bytes 1572872 | tf_op jit(solution)/shard_map/ppermute | solution.py:461
  4.6 24.1 %collective-permute-start.7 = (bf16[128,2048]{1,0:T(8,128)(2,1)}, bf16[128,2048]{1,0:T(8,128)(2,1)S(1)}, u32[]{:S(2)}, u32[]{:S(2)}) collective-permute-start(bf16[128,2048]{1,0:T(8,128)(2,1)} %tokens.3), channel_id=1, source_target_pairs={{0,2},{1,3},{2,0},{3,1},{4,6},{5,7},{6,4},{7,5},{8,10},{9,11},{10,... | collective-permute-start | bytes 1572872 | tf_op jit(solution)/shard_map/ppermute | solution.py:461
  6.1 22.0 %collective-permute-start.6 = (f32[8,128]{1,0:T(8,128)S(1)}, f32[8,128]{1,0:T(8,128)S(1)}, u32[]{:S(2)}, u32[]{:S(2)}) collective-permute-start(f32[8,128]{1,0:T(8,128)S(1)} %pad_maximum_fusion.6), channel_id=1, source_target_pairs={{0,2},{1,3},{2,0},{3,1},{4,6},{5,7},{6,4},{7,5},{8,10},{9,11},{10,... | collective-permute-start | bytes 12296 | tf_op jit(solution)/shard_map/ppermute | solution.py:461
  28.6 0.8 copy-start.9
  28.6 1.0 copy-start.10
  36.5 44.7 %all-to-all-start.2 = ((bf16[32,24,2048]{2,1,0:T(8,128)(2,1)}), bf16[32,24,2048]{2,1,0:T(8,128)(2,1)S(1)}, u32[]{:S(2)}, u32[]{:S(2)}) async-start(bf16[32,24,2048]{2,1,0:T(8,128)(2,1)} %bitcast.77), calls=%async_computation.2 | async-start | bytes 6291456 | tf_op jit(solution)/shard_map/all_to_all | solution.py:464
  81.2 65.3 %all-to-all-start = ((bf16[32,32,2048]{2,1,0:T(8,128)(2,1)}), bf16[32,32,2048]{2,1,0:T(8,128)(2,1)}, u32[]{:S(2)}, u32[]{:S(2)}) async-start(bf16[32,32,2048]{2,1,0:T(8,128)(2,1)} %bitcast.76), calls=%async_computation | async-start | bytes 8388608 | tf_op jit(solution)/shard_map/all_to_all | solution.py:464
  89.1 2.7 copy-start.6
  89.1 3.5 copy-start.7
  93.8 1.6 copy-start
  93.9 51.4 %collective-permute-start.10 = (bf16[3,176,2048]{2,1,0:T(8,128)(2,1)S(1)}, bf16[3,176,2048]{2,1,0:T(8,128)(2,1)S(1)}, u32[]{:S(2)}, u32[]{:S(2)}) collective-permute-start(bf16[3,176,2048]{2,1,0:T(8,128)(2,1)S(1)} %pad_maximum_fusion.3.refs_3_), channel_id=1, source_target_pairs={{0,1},{1,2},{2,3},{3,0},{4,5},{5,6},{6,7},{7,4},{8,9},{9,10},{10,1... | collective-permute-start | bytes 6488072 | tf_op jit(solution)/shard_map/ppermute | solution.py:461
  95.5 4.8 %copy-start.2 = (bf16[3,176,2048]{2,1,0:T(8,128)(2,1)}, bf16[3,176,2048]{2,1,0:T(8,128)(2,1)S(1)}, u32[]{:S(2)}) copy-start(bf16[3,176,2048]{2,1,0:T(8,128)(2,1)S(1)} %pad_maximum_fusion.2.refs_2_) | copy-start | bytes 6488068
  95.5 51.1 %collective-permute-start.9 = (bf16[3,176,2048]{2,1,0:T(8,128)(2,1)S(1)}, bf16[3,176,2048]{2,1,0:T(8,128)(2,1)}, u32[]{:S(2)}, u32[]{:S(2)}) collective-permute-start(bf16[3,176,2048]{2,1,0:T(8,128)(2,1)S(1)} %pad_maximum_fusion.2.refs_2_), channel_id=1, source_target_pairs={{0,3},{1,0},{2,1},{3,2},{4,7},{5,4},{6,5},{7,6},{8,11},{9,8},{10,9... | collective-permute-start | bytes 6488072 | tf_op jit(solution)/shard_map/ppermute | solution.py:461
  100.3 90.9 %collective-permute-start = (bf16[3,176,2048]{2,1,0:T(8,128)(2,1)}, bf16[3,176,2048]{2,1,0:T(8,128)(2,1)}, u32[]{:S(2)}, u32[]{:S(2)}) collective-permute-start(bf16[3,176,2048]{2,1,0:T(8,128)(2,1)} %pad_maximum_fusion.1.refs_2_.refs_4_), channel_id=1, source_target_pairs={{0,1},{1,2},{2,3},{3,0},{4,5},{5,6},{6,7},{7,4},{8,9},{9,10},{10,1... | collective-permute-start | bytes 6488072 | tf_op jit(solution)/shard_map/ppermute | solution.py:461
  101.8 89.9 %collective-permute-start.1 = (bf16[3,176,2048]{2,1,0:T(8,128)(2,1)}, bf16[3,176,2048]{2,1,0:T(8,128)(2,1)}, u32[]{:S(2)}, u32[]{:S(2)}) collective-permute-start(bf16[3,176,2048]{2,1,0:T(8,128)(2,1)} %pad_maximum_fusion.refs_1_.refs_3_), channel_id=1, source_target_pairs={{0,3},{1,0},{2,1},{3,2},{4,7},{5,4},{6,5},{7,6},{8,11},{9,8},{10,9... | collective-permute-start | bytes 6488072 | tf_op jit(solution)/shard_map/ppermute | solution.py:461
  145.2 1.4 copy-start.17
  146.6 1.6 copy-start.1
  148.2 1.6 copy-start.3
  202.5 14.8 %copy-start.11 = (s32[128,4]{0,1:T(4,128)S(1)}, s32[128,4]{0,1:T(4,128)}, u32[]{:S(2)}) copy-start(s32[128,4]{0,1:T(4,128)} %param.8) | copy-start | bytes 6148
  202.5 184.4 %all-to-all-start.3 = ((bf16[32,40,2048]{2,1,0:T(8,128)(2,1)}), bf16[32,40,2048]{2,1,0:T(8,128)(2,1)}, u32[]{:S(2)}, u32[]{:S(2)}) async-start(bf16[32,40,2048]{2,1,0:T(8,128)(2,1)} %bitcast.75), calls=%async_computation.3 | async-start | bytes 10485760 | tf_op jit(solution)/shard_map/all_to_all | solution.py:464
  210.0 143.3 %collective-permute-start.3 = (bf16[3,176,2048]{2,1,0:T(8,128)(2,1)}, bf16[3,176,2048]{2,1,0:T(8,128)(2,1)S(1)}, u32[]{:S(2)}, u32[]{:S(2)}) collective-permute-start(bf16[3,176,2048]{2,1,0:T(8,128)(2,1)} %pad_maximum_fusion.1.refs_2_.refs_4_), channel_id=1, source_target_pairs={{0,3},{1,0},{2,1},{3,2},{4,7},{5,4},{6,5},{7,6},{8,11},{9,8},{10,9... | collective-permute-start | bytes 6488072 | tf_op jit(solution)/shard_map/ppermute | solution.py:461
  213.8 142.9 %collective-permute-start.2 = (bf16[3,176,2048]{2,1,0:T(8,128)(2,1)}, bf16[3,176,2048]{2,1,0:T(8,128)(2,1)S(1)}, u32[]{:S(2)}, u32[]{:S(2)}) collective-permute-start(bf16[3,176,2048]{2,1,0:T(8,128)(2,1)} %pad_maximum_fusion.refs_1_.refs_3_), channel_id=1, source_target_pairs={{0,1},{1,2},{2,3},{3,0},{4,5},{5,6},{6,7},{7,4},{8,9},{9,10},{10,1... | collective-permute-start | bytes 6488072 | tf_op jit(solution)/shard_map/ppermute | solution.py:461
  213.8 165.8 %collective-permute-start.5 = (bf16[3,176,2048]{2,1,0:T(8,128)(2,1)}, bf16[3,176,2048]{2,1,0:T(8,128)(2,1)}, u32[]{:S(2)}, u32[]{:S(2)}) collective-permute-start(bf16[3,176,2048]{2,1,0:T(8,128)(2,1)} %pad_maximum_fusion.1.refs_2_.refs_4_), channel_id=1, source_target_pairs={{0,2},{1,3},{2,0},{3,1},{4,6},{5,7},{6,4},{7,5},{8,10},{9,11},{10,... | collective-permute-start | bytes 6488072 | tf_op jit(solution)/shard_map/ppermute | solution.py:461
  215.4 164.2 %collective-permute-start.4 = (bf16[3,176,2048]{2,1,0:T(8,128)(2,1)}, bf16[3,176,2048]{2,1,0:T(8,128)(2,1)}, u32[]{:S(2)}, u32[]{:S(2)}) collective-permute-start(bf16[3,176,2048]{2,1,0:T(8,128)(2,1)} %pad_maximum_fusion.refs_1_.refs_3_), channel_id=1, source_target_pairs={{0,2},{1,3},{2,0},{3,1},{4,6},{5,7},{6,4},{7,5},{8,10},{9,11},{10,... | collective-permute-start | bytes 6488072 | tf_op jit(solution)/shard_map/ppermute | solution.py:461
  353.4 3.3 copy-start.15
  356.7 1.4 copy-start.16
  376.9 1.3 copy-start.4
  378.2 1.3 copy-start.5
  386.9 7.5 %copy-start.12 = (s32[4,128]{1,0:T(4,128)S(1)}, s32[4,128]{1,0:T(4,128)}, u32[]{:S(2)}) copy-start(s32[4,128]{1,0:T(4,128)} %get-tuple-element.54.route_other_ref) | copy-start | bytes 6148
  387.0 8.5 %copy-start.13 = (f32[128,4]{0,1:T(4,128)S(1)}, f32[128,4]{0,1:T(4,128)}, u32[]{:S(2)}) copy-start(f32[128,4]{0,1:T(4,128)} %param.9) | copy-start | bytes 6148
  387.0 33.3 %all-to-all-start.1 = ((bf16[32,16,2048]{2,1,0:T(8,128)(2,1)}), bf16[32,16,2048]{2,1,0:T(8,128)(2,1)S(1)}, u32[]{:S(2)}, u32[]{:S(2)}) async-start(bf16[32,16,2048]{2,1,0:T(8,128)(2,1)} %bitcast.78), calls=%async_computation.1 | async-start | bytes 4194304 | tf_op jit(solution)/shard_map/all_to_all | solution.py:464
  406.1 27.0 %collective-permute-start.12 = (bf16[256,2048]{1,0:T(8,128)(2,1)}, bf16[256,2048]{1,0:T(8,128)(2,1)S(1)}, u32[]{:S(2)}, u32[]{:S(2)}) collective-permute-start(bf16[256,2048]{1,0:T(8,128)(2,1)} %get-tuple-element.27), channel_id=1, source_target_pairs={{0,2},{1,3},{2,0},{3,1},{4,6},{5,7},{6,4},{7,5},{8,10},{9,11},{10,... | collective-permute-start | bytes 3145736 | tf_op jit(solution)/shard_map/ppermute | solution.py:461
  406.1 27.0 %collective-permute-start.11 = (f32[8,128]{1,0:T(8,128)}, f32[8,128]{1,0:T(8,128)S(1)}, u32[]{:S(2)}, u32[]{:S(2)}) collective-permute-start(f32[8,128]{1,0:T(8,128)} %get-tuple-element.25), channel_id=1, source_target_pairs={{0,2},{1,3},{2,0},{3,1},{4,6},{5,7},{6,4},{7,5},{8,10},{9,11},{10,... | collective-permute-start | bytes 12296 | tf_op jit(solution)/shard_map/ppermute | solution.py:461
  433.1 0.6 copy-start.14
  433.1 1.0 copy-start.8

commit v5 on v4

--- a/solution.py
+++ b/solution.py
@@ -175,7 +175,7 @@
     landed(wu, sems.at[4])
     landed(gs.at[pl.ds(0, main)], sems.at[2])
     landed(wd, sems.at[5])
-    size = (main + small) // 3
+    size = (main + small) // 2
 
     def block(b, carry):
         at = pl.ds(pl.multiple_of(b * size, 16), size)
@@ -184,7 +184,7 @@
         backs[at] = (by_row(d_gate, wg[...]) + by_row(d_up, wu[...])).astype(BF)
         return carry
 
-    lax.fori_loop(0, 3, block, 0)
+    lax.fori_loop(0, 2, block, 0)
     put_rows(nodes, outs, 0, home, OUT0_ROWS, 0, sems.at[0])
     put_rows(nodes, outs, nodes * 8, home, OUT0_ROWS, 8, sems.at[0])
     put_rows(nodes, backs, 0, home, OUT0_ROWS, 16, sems.at[1])
@@ -351,42 +351,57 @@
     )(on_chip(xs), on_chip(gs), out_part, back_part, *pieces)
 
 
-def mixed(rows, places, values):
-    ids = lax.broadcasted_iota(jnp.int32, (places.shape[0], rows.shape[0]), 1)
+def weighted_hot(places, values, rows):
+    ids = lax.broadcasted_iota(jnp.int32, (places.shape[0], rows), 1)
     total = jnp.zeros(ids.shape, F32)
     for k in range(TOP):
         total = total + jnp.where(places[:, k : k + 1] == ids, values[:, k : k + 1], 0.0)
-    return jnp.dot(total.astype(BF), rows, preferred_element_type=F32)
-
-
-def weight_grads(rows, grads, places):
-    table = lax.dot_general(grads, rows, (((1,), (1,)), ((), ())), preferred_element_type=F32)
+    return total.astype(BF)
+
+
+def weight_grads(table, places):
     ids = lax.broadcasted_iota(jnp.int32, table.shape, 1)
     lane = lax.broadcasted_iota(jnp.int32, (table.shape[0], 128), 1)
     result = jnp.zeros(lane.shape, F32)
     for k in range(TOP):
         column = jnp.sum(jnp.where(places[:, k : k + 1] == ids, table, 0.0), axis=1, keepdims=True)
         result = result + jnp.where(lane == k, column, 0.0)
-    return result
-
-
-def combine_pair_kernel(home, places_ref, values_ref, grads, grads_other, back, own, dw_other, dw_own):
+    return jnp.transpose(result)[:8]
+
+
+COLUMNS = 512
+
+
+def sweep(home, hot, grads, table, use):
+    matrix = hot[...]
+    table[...] = jnp.zeros_like(table)
+
+    def block(c, carry):
+        cols = pl.ds(pl.multiple_of(c * COLUMNS, COLUMNS), COLUMNS)
+        rows = home[:, cols]
+        use(cols, jnp.dot(matrix, rows, preferred_element_type=F32))
+        part = by_hidden(grads[:, cols], rows)
+        table[...] += part
+        return carry
+
+    lax.fori_loop(0, home.shape[1] // COLUMNS, block, 0)
+
+
+def combine_pair_kernel(home, places, values, grads, mix, dw, hot, table):
     toks = grads.shape[0]
-    rows = home[...]
-    total = mixed(rows, places_ref[...], values_ref[...])
-    back[...] = total[: 2 * toks].astype(BF)
-    own[...] = total[2 * toks :]
-    both = jnp.concatenate([grads_other[...], grads[...]], axis=0)
-    heads = jnp.concatenate([places_ref[:toks], places_ref[2 * toks : 3 * toks]], axis=0)
-    dw = weight_grads(rows, both, heads)
-    dw_other[...] = jnp.transpose(dw[:toks])[:8]
-    dw_own[...] = jnp.transpose(dw[toks:])[:8]
+    hot[...] = weighted_hot(places[...], values[...], home.shape[0])
+
+    def use(cols, total):
+        mix[:, cols] = total.astype(mix.dtype)
+
+    sweep(home, hot, grads, table, use)
+    dw[...] = weight_grads(table[...], places[:toks])
 
 
 def combine_full_kernel(
-    home, places_ref, values_ref, dw_own, dw_back, grads_at, own_at, returned_at, combined, d_tokens, d_weights, *scratch
+    home, places, values, dw_own, dw_back, grads_at, own_at, returned_at, combined, d_tokens, d_weights, *scratch
 ):
-    grads, own, returned, sems = scratch
+    grads, own, returned, hot, table, sems = scratch
     toks = grads.shape[0]
     copies = [
         pltpu.make_async_copy(src, dst, sems.at[i])
@@ -394,34 +409,30 @@
     ]
     for copy in copies:
         copy.start()
-    rows = home[...]
-    total = mixed(rows, places_ref[...], values_ref[...])
-    copies[0].wait()
-    copies[1].wait()
-    total = total + own[...] + returned[...].astype(F32)
-    combined[...] = total[:toks].astype(BF)
-    d_tokens[...] = total[toks:].astype(BF)
-    copies[2].wait()
-    dw = jnp.transpose(weight_grads(rows, grads[...], places_ref[:toks]))[:8] + dw_own[...] + dw_back[...]
-    d_weights[...] = dw[:TOP]
-
-
-def combine_pair(home, places, values, grads, grads_other):
+    hot[...] = weighted_hot(places[...], values[...], home.shape[0])
+    for copy in copies:
+        copy.wait()
+
+    def use(cols, total):
+        total = total + own[:, cols] + returned[:, cols].astype(F32)
+        combined[:, cols] = total[:toks].astype(BF)
+        d_tokens[:, cols] = total[toks:].astype(BF)
+
+    sweep(home, hot, grads, table, use)
+    d_weights[...] = (weight_grads(table[...], places[:toks]) + dw_own[...] + dw_back[...])[:TOP]
+
+
+def combine_pair(home, places, values, grads, kind):
     toks, width = grads.shape
     return pl.pallas_call(
         combine_pair_kernel,
-        name="combine_pair",
-        out_shape=(
-            jax.ShapeDtypeStruct((2 * toks, width), BF),
-            jax.ShapeDtypeStruct((2 * toks, width), F32),
-            jax.ShapeDtypeStruct((8, toks), F32),
-            jax.ShapeDtypeStruct((8, toks), F32),
-        ),
+        out_shape=(jax.ShapeDtypeStruct((2 * toks, width), kind), jax.ShapeDtypeStruct((8, toks), F32)),
+        scratch_shapes=[pltpu.VMEM((2 * toks, home.shape[0]), BF), pltpu.VMEM((toks, home.shape[0]), F32)],
         compiler_params=room(60),
         cost_estimate=pl.CostEstimate(
-            flops=12 * toks * home.shape[0] * width, transcendentals=0, bytes_accessed=12 * 1024 * 1024
+            flops=6 * toks * home.shape[0] * width, transcendentals=0, bytes_accessed=8 * 1024 * 1024
         ),
-    )(home, places, values, grads, grads_other)
+    )(home, places, values, grads)
 
 
 def combine_full(home, places, values, grads, own, returned, dw_own, dw_back):
@@ -440,6 +451,8 @@
             pltpu.VMEM((toks, width), BF),
             pltpu.VMEM((2 * toks, width), F32),
             pltpu.VMEM((2 * toks, width), BF),
+            pltpu.VMEM((2 * toks, home.shape[0]), BF),
+            pltpu.VMEM((toks, home.shape[0]), F32),
             pltpu.SemaphoreType.DMA((3,)),
         ],
         compiler_params=room(57),
@@ -452,7 +465,6 @@
 def shards(tokens, route, combine_weights, w_gate, w_up, w_down, grad_out):
     nodes = lax.axis_size("node")
     planes = lax.axis_size("local")
-    toks, _ = tokens.shape
     up = [(i, (i + 1) % planes) for i in range(planes)]
     down = [(i, (i - 1) % planes) for i in range(planes)]
     across = [(i, (i + 2) % planes) for i in range(planes)]
@@ -484,7 +496,7 @@
     below_a, above_b = send(p1a, up), send(p1b, down)
     pair1 = [p1a, p1b, below_b, above_a]
     near1 = pair1 + [below_a, above_b]
-    far1 = [send(p1a, across), send(p1b, across)]
+    far1 = [send(above_a, down), send(below_b, up)]
 
     slot_own, slot_other = slots_of(route_t), slots_of(route_other)
 
@@ -529,15 +541,16 @@
     def stacked(*parts):
         return jnp.concatenate([p.T for p in parts], axis=0)
 
-    places0 = stacked(other_place(8, 33), other_place(24, 35), home_place(0, 32), home_place(16, 34))
+    places0 = stacked(home_place(0, 32), home_place(16, 34))
+    places_other = stacked(other_place(8, 33), other_place(24, 35))
     places1 = stacked(full_place(0), full_place(8))
-    values0 = stacked(weight_other, weight_other, weight_t, weight_t)
-    values1 = values0[2 * toks :]
-    back, kept, dw_other, dw_own = combine_pair(home0, places0, values0, grad_out, grads_other)
+    values0, values_other = stacked(weight_t, weight_t), stacked(weight_other, weight_other)
+    back, dw_other = combine_pair(home0, places_other, values_other, grads_other, BF)
     returned = send(back, across)
     dw_back = send(dw_other, across)
+    kept, dw_own = combine_pair(home0, places0, values0, grad_out, F32)
     combined, d_tokens, d_weights_t = combine_full(
-        home1, places1, values1, grad_out, kept, returned, dw_own, dw_back
+        home1, places1, values0, grad_out, kept, returned, dw_own, dw_back
     )
     return combined, d_tokens, d_weights_t.T
 

time: 440 us -> 370 us (0.84)
  waiting for transfers between devices: 270 us -> 194 us
  Pallas kernels: 88 us -> 93 us
    ppermute x13, waiting for transfers between devices: 229 us -> 161 us  [send(): return lax.ppermute(value, 'local', pairs)]
    all_to_all x4, waiting for transfers between devices: 40.3 us -> 32.6 us  [exchange(): return lax.all_to_all(rows, 'node', split_axis=0, concat_axis=0, tiled=True)]
    pallas_call x1 -> x2, Pallas kernels: 9.73 us -> 16.6 us  [combine_pair(): pl.pallas_call(combine_pair_kernel, out_shape=(jax.ShapeDtypeStruct((2 *...]
  transfers between devices with their start and end apart: 17 -> 17, of which waited for: 9 -> 10; matrix products, arithmetic and copies ran while one was open for 3% -> 4% of each run, Pallas kernels for 15% -> 19%
where the time goes in v5:
time: 370 us; the launch traced here: 369 us
  waiting for transfers between devices  194 us (52%)
  Pallas kernels  93 us (25%)
  starting transfers between devices  56.2 us (15%)
  local copies, waits for them, and re-layouts  19.1 us (5%)
  other arithmetic  5.7 us (2%)
    ppermute x13, waiting for transfers between devices, send(): return lax.ppermute(value, 'local', pairs)  161 us
    all_to_all x4, waiting for transfers between devices, exchange(): return lax.all_to_all(rows, 'node', split_axis=0, concat_axis=0, tiled=True)  32.6 us
    all_to_all x4, starting transfers between devices, exchange(): return lax.all_to_all(rows, 'node', split_axis=0, concat_axis=0, tiled=True)  30.3 us
    ppermute x13, starting transfers between devices, send(): return lax.ppermute(value, 'local', pairs)  25.8 us
    pallas_call x1, Pallas kernels, expert_pair(): pl.pallas_call(functools.partial(expert_pair_kernel, nodes, len(pieces)),...  21 us
    pallas_call x1, Pallas kernels, expert_near(): pl.pallas_call(functools.partial(expert_near_kernel, nodes, len(pieces)),...  18.8 us
    pallas_call x2, Pallas kernels, combine_pair(): pl.pallas_call(combine_pair_kernel, out_shape=(jax.ShapeDtypeStruct((2 *...  16.6 us
    pallas_call x2, Pallas kernels, dispatch(): pl.pallas_call(kernel, grid=(steps,), out_shape=jax.ShapeDtypeStruct((row...  12.7 us
  transfers between devices with their start and end apart: 17, of which 10 were waited for; matrix products, arithmetic and copies ran while one was open for 4% of the time, Pallas kernels for 19%

profile of v5, /device:TPU:2, one launch (start us, length us, event | category | flops | bytes accessed | tf_op | source)
XLA Modules:
  0.0 369.2 jit_solution(13736464277201340069)
XLA Ops:
  0.6 4.0 %collective-permute-start.8 = (bf16[128,2048]{1,0:T(8,128)(2,1)}, bf16[128,2048]{1,0:T(8,128)(2,1)S(1)}, u32[]{:S(2)}, u32[]{:S(2)}) collective-permute-start(bf16[128,2048]{1,0:T(8,128)(2,1)} %grads_at.1), channel_id=1, source_target_pairs={{0,2},{1,3},{2,0},{3,1},{4,6},{5,7},{6,4},{7,5},{8,10},{9,11},{10,... | collective-permute-start | bytes 1572872 | tf_op jit(solution)/shard_map/ppermute | solution.py:473
  4.6 0.1 collective-permute-start.7
  4.7 0.7 bitcast_convert_fusion
  5.4 0.7 pad_maximum_fusion.5
  6.1 3.4 collective-permute-start.6
  9.5 18.6 %collective-permute-done.6 = f32[8,128]{1,0:T(8,128)S(1)} collective-permute-done((f32[8,128]{1,0:T(8,128)S(1)}, f32[8,128]{1,0:T(8,128)S(1)}, u32[]{:S(2)}, u32[]{:S(2)}) %collective-permute-start.6) | collective-permute-done | bytes 4128 | tf_op jit(solution)/shard_map/ppermute | solution.py:473
  28.0 0.6 slice_bitcast_fusion
  28.6 0.0 copy-start.10
  28.7 0.8 copy-done.9
  29.4 0.2 copy-done.10
  29.6 6.9 %shard_map.95 = bf16[768,2048]{1,0:T(8,128)(2,1)} custom-call(s32[4,128]{1,0:T(4,128)} %bitcast.81, s32[4,128]{1,0:T(4,128)} %get-tuple-element.54.route_other_ref, bf16[128,2048]{1,0:T(8,128)(2,1)} %tokens.3, bf16[128,2048]{1,0:T(8,128)(2,1)} %grads_at.1, bf16[128,2048]{1,0:T(8,128)(2,1)} %copy-done.10, bf16[128,2048]{1,0:T(8,128)(2,1)} %copy-done.9), custom_call_target="tpu_custom_call" | custom-call | flops 805306368 | bytes 6291456 | tf_op jit(solution)/shard_map/pallas_call | solution.py:88
  36.5 7.6 %all-to-all-start.2 = ((bf16[32,24,2048]{2,1,0:T(8,128)(2,1)}), bf16[32,24,2048]{2,1,0:T(8,128)(2,1)S(1)}, u32[]{:S(2)}, u32[]{:S(2)}) async-start(bf16[32,24,2048]{2,1,0:T(8,128)(2,1)} %bitcast.77), calls=%async_computation.2 | async-start | bytes 6291456 | tf_op jit(solution)/shard_map/all_to_all | solution.py:476
  44.2 5.8 %shard_map.94 = bf16[1024,2048]{1,0:T(8,128)(2,1)} custom-call(s32[4,128]{1,0:T(4,128)} %bitcast.82, bf16[128,2048]{1,0:T(8,128)(2,1)} %tokens.3, bf16[128,2048]{1,0:T(8,128)(2,1)} %grads_at.1), custom_call_target="tpu_custom_call" | custom-call | flops 1073741824 | bytes 8388608 | tf_op jit(solution)/shard_map/pallas_call | solution.py:88
  49.9 31.3 %all-to-all-done.2 = bf16[32,24,2048]{2,1,0:T(8,128)(2,1)S(1)} async-done(((bf16[32,24,2048]{2,1,0:T(8,128)(2,1)}), bf16[32,24,2048]{2,1,0:T(8,128)(2,1)S(1)}, u32[]{:S(2)}, u32[]{:S(2)}) %all-to-all-start.2) | async-done | bytes 3145760 | tf_op jit(solution)/shard_map/all_to_all | solution.py:476
  81.2 7.8 %all-to-all-start = ((bf16[32,32,2048]{2,1,0:T(8,128)(2,1)}), bf16[32,32,2048]{2,1,0:T(8,128)(2,1)}, u32[]{:S(2)}, u32[]{:S(2)}) async-start(bf16[32,32,2048]{2,1,0:T(8,128)(2,1)} %bitcast.76), calls=%async_computation | async-start | bytes 8388608 | tf_op jit(solution)/shard_map/all_to_all | solution.py:476
  89.0 0.0 copy-start.6
  89.1 0.0 copy-start.7
  89.1 2.1 fusion.27
  91.2 0.5 copy-done.6
  91.7 0.9 copy-done.7
  92.6 1.0 fusion.25
  93.6 0.2 pad_maximum_fusion.3.refs_3_
  93.8 1.4 collective-permute-start.10
  95.2 0.2 pad_maximum_fusion.2.refs_2_
  95.5 3.2 collective-permute-start.9
  98.7 1.6 pad_maximum_fusion.1.refs_2_.refs_4_
  100.3 1.6 pad_maximum_fusion.refs_1_.refs_3_
  101.9 3.2 collective-permute-start.1
  105.1 40.1 %collective-permute-done.10.refs_5_ = bf16[3,176,2048]{2,1,0:T(8,128)(2,1)S(1)} collective-permute-done((bf16[3,176,2048]{2,1,0:T(8,128)(2,1)S(1)}, bf16[3,176,2048]{2,1,0:T(8,128)(2,1)S(1)}, u32[]{:S(2)}, u32[]{:S(2)}) %collective-permute-start.10) | collective-permute-done | bytes 2162720 | tf_op jit(solution)/shard_map/ppermute | solution.py:473
  145.2 1.4 copy-done.15
  146.6 1.6 copy-done.1
  148.2 1.6 copy-done.3
  149.8 21.0 %expert_pair.1 = (bf16[1280,2048]{1,0:T(8,128)(2,1)}, bf16[64,2048]{1,0:T(8,128)(2,1)S(1)}, bf16[64,2048]{1,0:T(8,128)(2,1)S(1)}) custom-call(bf16[1024,2048]{1,0:T(8,128)(2,1)} %bitcast.2.refs_0_, bf16[768,2048]{1,0:T(8,128)(2,1)S(1)} %bitcast.72, bf16[3,176,2048]{2,1,0:T(8,128)(2,1)S(1)} %copy-done.3, bf16[3,176,2048]{2,1,0:T(8,128)(2,1)S(1)} %copy-done.1, ...), custom_call_target="tpu_custom_call" | custom-call | flops 9965666304 | bytes 18087936 | tf_op jit(solution)/shard_map/expert_pair/pallas_call | solution.py:292
  170.8 20.3 %collective-permute-done.refs_3_.refs_5_ = bf16[3,176,2048]{2,1,0:T(8,128)(2,1)} collective-permute-done((bf16[3,176,2048]{2,1,0:T(8,128)(2,1)}, bf16[3,176,2048]{2,1,0:T(8,128)(2,1)}, u32[]{:S(2)}, u32[]{:S(2)}) %collective-permute-start) | collective-permute-done | bytes 2162720 | tf_op jit(solution)/shard_map/ppermute | solution.py:473
  191.1 0.6 collective-permute-done.1.refs_4_.refs_6_
  191.7 10.7 %expert_ninth.1 = bf16[1280,2048]{1,0:T(8,128)(2,1)} custom-call(bf16[768,2048]{1,0:T(8,128)(2,1)S(1)} %bitcast.73, bf16[64,2048]{1,0:T(8,128)(2,1)S(1)} %get-tuple-element.21.refs_1_, bf16[64,2048]{1,0:T(8,128)(2,1)S(1)} %get-tuple-element.22.refs_2_, bf16[3,176,2048]{2,1,0:T(8,128)(2,1)} %pad_maximum_fusion.refs_1_.refs_3_, ...), custom_call_target="tpu_custom_call", output_to_operand_aliasing={{}: (7, {})} | custom-call | flops 1107296256 | bytes 9699328 | tf_op jit(solution)/shard_map/expert_ninth/pallas_call | solution.py:309
  202.4 7.5 %all-to-all-start.3 = ((bf16[32,40,2048]{2,1,0:T(8,128)(2,1)}), bf16[32,40,2048]{2,1,0:T(8,128)(2,1)}, u32[]{:S(2)}, u32[]{:S(2)}) async-start(bf16[32,40,2048]{2,1,0:T(8,128)(2,1)} %bitcast.75), calls=%async_computation.3 | async-start | bytes 10485760 | tf_op jit(solution)/shard_map/all_to_all | solution.py:476
  210.0 3.8 %collective-permute-start.3 = (bf16[3,176,2048]{2,1,0:T(8,128)(2,1)}, bf16[3,176,2048]{2,1,0:T(8,128)(2,1)S(1)}, u32[]{:S(2)}, u32[]{:S(2)}) collective-permute-start(bf16[3,176,2048]{2,1,0:T(8,128)(2,1)} %pad_maximum_fusion.1.refs_2_.refs_4_), channel_id=1, source_target_pairs={{0,3},{1,0},{2,1},{3,2},{4,7},{5,4},{6,5},{7,6},{8,11},{9,8},{10,9... | collective-permute-start | bytes 6488072 | tf_op jit(solution)/shard_map/ppermute | solution.py:473
  213.7 3.3 collective-permute-start.4
  217.0 44.5 %collective-permute-done.3.refs_6_ = bf16[3,176,2048]{2,1,0:T(8,128)(2,1)S(1)} collective-permute-done((bf16[3,176,2048]{2,1,0:T(8,128)(2,1)}, bf16[3,176,2048]{2,1,0:T(8,128)(2,1)S(1)}, u32[]{:S(2)}, u32[]{:S(2)}) %collective-permute-start.3) | collective-permute-done | bytes 2162720 | tf_op jit(solution)/shard_map/ppermute | solution.py:473
  261.5 3.6 collective-permute-done.2.refs_5_
  265.1 1.4 copy-done.17
  266.5 18.8 %expert_near.1 = (f32[256,2048]{1,0:T(8,128)S(1)}, f32[256,2048]{1,0:T(8,128)S(1)}, bf16[256,2048]{1,0:T(8,128)(2,1)S(1)}, bf16[256,2048]{1,0:T(8,128)(2,1)S(1)}) custom-call(bf16[1024,2048]{1,0:T(8,128)(2,1)} %bitcast.2.refs_0_, bf16[3,176,2048]{2,1,0:T(8,128)(2,1)} %pad_maximum_fusion.refs_1_.refs_3_, ...), custom_call_target="tpu_custom_call" | custom-call | flops 6643777536 | bytes 17170432 | tf_op jit(solution)/shard_map/expert_near/pallas_call | solution.py:325
  285.3 1.3 copy-done.4
  286.6 1.3 copy-done.5
  287.9 22.4 %collective-permute-done.5.refs_5_ = bf16[3,176,2048]{2,1,0:T(8,128)(2,1)} collective-permute-done((bf16[3,176,2048]{2,1,0:T(8,128)(2,1)}, bf16[3,176,2048]{2,1,0:T(8,128)(2,1)}, u32[]{:S(2)}, u32[]{:S(2)}) %collective-permute-start.5) | collective-permute-done | bytes 2162720 | tf_op jit(solution)/shard_map/ppermute | solution.py:473
  310.4 7.3 %expert_far.1 = bf16[512,2048]{1,0:T(8,128)(2,1)} custom-call(bf16[256,2048]{1,0:T(8,128)(2,1)S(1)} %get-tuple-element.17.refs_0_, bf16[256,2048]{1,0:T(8,128)(2,1)S(1)} %get-tuple-element.18.refs_1_, f32[256,2048]{1,0:T(8,128)} %copy-done.4, f32[256,2048]{1,0:T(8,128)} %copy-done.5, bf16[3,176,2048]{2,1,0:T(8,128)(2,1)} %collective-permute-done.4.refs_4_, ...), custom_call_target="tpu_custom_call" | custom-call | flops 2214592512 | bytes 8519680 | tf_op jit(solution)/shard_map/expert_far/pallas_call | solution.py:342
  317.7 0.0 copy-start.12
  317.7 7.4 %all-to-all-start.1 = ((bf16[32,16,2048]{2,1,0:T(8,128)(2,1)}), bf16[32,16,2048]{2,1,0:T(8,128)(2,1)S(1)}, u32[]{:S(2)}, u32[]{:S(2)}) async-start(bf16[32,16,2048]{2,1,0:T(8,128)(2,1)} %bitcast.78), calls=%async_computation.1 | async-start | bytes 4194304 | tf_op jit(solution)/shard_map/all_to_all | solution.py:476
  325.2 0.2 select_reduce_fusion.3
  325.4 0.8 copy.43.places
  326.2 0.8 copy.44.values
  327.0 8.3 %shard_map.97 = (bf16[256,2048]{1,0:T(8,128)(2,1)}, f32[8,128]{1,0:T(8,128)}) custom-call(bf16[1280,2048]{1,0:T(8,128)(2,1)} %bitcast.21.home, s32[256,4]{1,0:T(8,128)} %copy.43.places, f32[256,4]{1,0:T(8,128)} %copy.44.values, bf16[128,2048]{1,0:T(8,128)(2,1)} %copy-done.9), custom_call_target="tpu_custom_call" | custom-call | flops 2013265920 | bytes 8388608 | tf_op jit(solution)/shard_map/pallas_call | solution.py:427
  335.3 0.2 select_reduce_fusion.7
  335.5 0.8 copy.41.places
  336.3 0.8 copy.46.values
  337.1 0.8 copy.45.places
  337.9 3.5 collective-permute-start.11
  341.5 8.3 %shard_map.96 = (f32[256,2048]{1,0:T(8,128)}, f32[8,128]{1,0:T(8,128)}) custom-call(bf16[1280,2048]{1,0:T(8,128)(2,1)} %bitcast.21.home, s32[256,4]{1,0:T(8,128)} %copy.41.places, f32[256,4]{1,0:T(8,128)} %copy.46.values, bf16[128,2048]{1,0:T(8,128)(2,1)} %grads_at.1), custom_call_target="tpu_custom_call" | custom-call | flops 2013265920 | bytes 8388608 | tf_op jit(solution)/shard_map/pallas_call | solution.py:427
  349.8 1.3 all-to-all-done.1
  351.0 11.2 %collective-permute-done.11.dw_back = f32[8,128]{1,0:T(8,128)S(1)} collective-permute-done((f32[8,128]{1,0:T(8,128)}, f32[8,128]{1,0:T(8,128)S(1)}, u32[]{:S(2)}, u32[]{:S(2)}) %collective-permute-start.11) | collective-permute-done | bytes 4128 | tf_op jit(solution)/shard_map/ppermute | solution.py:473
  362.3 0.6 copy-done.14
  362.9 0.4 copy-done.8
  363.3 5.8 %combine_full.1 = (bf16[128,2048]{1,0:T(8,128)(2,1)}, bf16[128,2048]{1,0:T(8,128)(2,1)}, f32[4,128]{1,0:T(4,128)}) custom-call(bf16[512,2048]{1,0:T(8,128)(2,1)S(1)} %bitcast.74, s32[256,4]{1,0:T(8,128)} %copy.45.places, f32[256,4]{1,0:T(8,128)} %copy.46.values, f32[8,128]{1,0:T(8,128)} %get-tuple-element.24.dw_own, f32[8,128]{1,0:T(8,128)} %copy-done.14, ...), custom_call_target="tpu_custom_call" | custom-call | flops 805306368 | bytes 8388608 | tf_op jit(solution)/shard_map/combine_full/pallas_call | solution.py:440
  (40 shorter events, 0.1 us)
Async XLA Ops:
  0.6 28.0 %collective-permute-start.8 = (bf16[128,2048]{1,0:T(8,128)(2,1)}, bf16[128,2048]{1,0:T(8,128)(2,1)S(1)}, u32[]{:S(2)}, u32[]{:S(2)}) collective-permute-start(bf16[128,2048]{1,0:T(8,128)(2,1)} %grads_at.1), channel_id=1, source_target_pairs={{0,2},{1,3},{2,0},{3,1},{4,6},{5,7},{6,4},{7,5},{8,10},{9,11},{10,... | collective-permute-start | bytes 1572872 | tf_op jit(solution)/shard_map/ppermute | solution.py:473
  4.6 24.1 %collective-permute-start.7 = (bf16[128,2048]{1,0:T(8,128)(2,1)}, bf16[128,2048]{1,0:T(8,128)(2,1)S(1)}, u32[]{:S(2)}, u32[]{:S(2)}) collective-permute-start(bf16[128,2048]{1,0:T(8,128)(2,1)} %tokens.3), channel_id=1, source_target_pairs={{0,2},{1,3},{2,0},{3,1},{4,6},{5,7},{6,4},{7,5},{8,10},{9,11},{10,... | collective-permute-start | bytes 1572872 | tf_op jit(solution)/shard_map/ppermute | solution.py:473
  6.1 22.0 %collective-permute-start.6 = (f32[8,128]{1,0:T(8,128)S(1)}, f32[8,128]{1,0:T(8,128)S(1)}, u32[]{:S(2)}, u32[]{:S(2)}) collective-permute-start(f32[8,128]{1,0:T(8,128)S(1)} %pad_maximum_fusion.5), channel_id=1, source_target_pairs={{0,2},{1,3},{2,0},{3,1},{4,6},{5,7},{6,4},{7,5},{8,10},{9,11},{10,... | collective-permute-start | bytes 12296 | tf_op jit(solution)/shard_map/ppermute | solution.py:473
  28.6 0.8 copy-start.9
  28.6 1.0 copy-start.10
  36.5 44.7 %all-to-all-start.2 = ((bf16[32,24,2048]{2,1,0:T(8,128)(2,1)}), bf16[32,24,2048]{2,1,0:T(8,128)(2,1)S(1)}, u32[]{:S(2)}, u32[]{:S(2)}) async-start(bf16[32,24,2048]{2,1,0:T(8,128)(2,1)} %bitcast.77), calls=%async_computation.2 | async-start | bytes 6291456 | tf_op jit(solution)/shard_map/all_to_all | solution.py:476
  81.2 65.3 %all-to-all-start = ((bf16[32,32,2048]{2,1,0:T(8,128)(2,1)}), bf16[32,32,2048]{2,1,0:T(8,128)(2,1)}, u32[]{:S(2)}, u32[]{:S(2)}) async-start(bf16[32,32,2048]{2,1,0:T(8,128)(2,1)} %bitcast.76), calls=%async_computation | async-start | bytes 8388608 | tf_op jit(solution)/shard_map/all_to_all | solution.py:476
  89.0 2.7 copy-start.6
  89.1 3.5 copy-start.7
  93.8 1.6 copy-start
  93.8 51.4 %collective-permute-start.10 = (bf16[3,176,2048]{2,1,0:T(8,128)(2,1)S(1)}, bf16[3,176,2048]{2,1,0:T(8,128)(2,1)S(1)}, u32[]{:S(2)}, u32[]{:S(2)}) collective-permute-start(bf16[3,176,2048]{2,1,0:T(8,128)(2,1)S(1)} %pad_maximum_fusion.3.refs_3_), channel_id=1, source_target_pairs={{0,1},{1,2},{2,3},{3,0},{4,5},{5,6},{6,7},{7,4},{8,9},{9,10},{10,1... | collective-permute-start | bytes 6488072 | tf_op jit(solution)/shard_map/ppermute | solution.py:473
  95.4 4.8 %copy-start.2 = (bf16[3,176,2048]{2,1,0:T(8,128)(2,1)}, bf16[3,176,2048]{2,1,0:T(8,128)(2,1)S(1)}, u32[]{:S(2)}) copy-start(bf16[3,176,2048]{2,1,0:T(8,128)(2,1)S(1)} %pad_maximum_fusion.2.refs_2_) | copy-start | bytes 6488068
  95.5 51.1 %collective-permute-start.9 = (bf16[3,176,2048]{2,1,0:T(8,128)(2,1)S(1)}, bf16[3,176,2048]{2,1,0:T(8,128)(2,1)}, u32[]{:S(2)}, u32[]{:S(2)}) collective-permute-start(bf16[3,176,2048]{2,1,0:T(8,128)(2,1)S(1)} %pad_maximum_fusion.2.refs_2_), channel_id=1, source_target_pairs={{0,3},{1,0},{2,1},{3,2},{4,7},{5,4},{6,5},{7,6},{8,11},{9,8},{10,9... | collective-permute-start | bytes 6488072 | tf_op jit(solution)/shard_map/ppermute | solution.py:473
  100.3 90.8 %collective-permute-start = (bf16[3,176,2048]{2,1,0:T(8,128)(2,1)}, bf16[3,176,2048]{2,1,0:T(8,128)(2,1)}, u32[]{:S(2)}, u32[]{:S(2)}) collective-permute-start(bf16[3,176,2048]{2,1,0:T(8,128)(2,1)} %pad_maximum_fusion.1.refs_2_.refs_4_), channel_id=1, source_target_pairs={{0,1},{1,2},{2,3},{3,0},{4,5},{5,6},{6,7},{7,4},{8,9},{9,10},{10,1... | collective-permute-start | bytes 6488072 | tf_op jit(solution)/shard_map/ppermute | solution.py:473
  101.9 89.8 %collective-permute-start.1 = (bf16[3,176,2048]{2,1,0:T(8,128)(2,1)}, bf16[3,176,2048]{2,1,0:T(8,128)(2,1)}, u32[]{:S(2)}, u32[]{:S(2)}) collective-permute-start(bf16[3,176,2048]{2,1,0:T(8,128)(2,1)} %pad_maximum_fusion.refs_1_.refs_3_), channel_id=1, source_target_pairs={{0,3},{1,0},{2,1},{3,2},{4,7},{5,4},{6,5},{7,6},{8,11},{9,8},{10,9... | collective-permute-start | bytes 6488072 | tf_op jit(solution)/shard_map/ppermute | solution.py:473
  145.2 1.4 copy-start.15
  146.6 1.6 copy-start.1
  148.2 1.6 copy-start.3
  202.4 115.3 %all-to-all-start.3 = ((bf16[32,40,2048]{2,1,0:T(8,128)(2,1)}), bf16[32,40,2048]{2,1,0:T(8,128)(2,1)}, u32[]{:S(2)}, u32[]{:S(2)}) async-start(bf16[32,40,2048]{2,1,0:T(8,128)(2,1)} %bitcast.75), calls=%async_computation.3 | async-start | bytes 10485760 | tf_op jit(solution)/shard_map/all_to_all | solution.py:476
  210.0 51.5 %collective-permute-start.3 = (bf16[3,176,2048]{2,1,0:T(8,128)(2,1)}, bf16[3,176,2048]{2,1,0:T(8,128)(2,1)S(1)}, u32[]{:S(2)}, u32[]{:S(2)}) collective-permute-start(bf16[3,176,2048]{2,1,0:T(8,128)(2,1)} %pad_maximum_fusion.1.refs_2_.refs_4_), channel_id=1, source_target_pairs={{0,3},{1,0},{2,1},{3,2},{4,7},{5,4},{6,5},{7,6},{8,11},{9,8},{10,9... | collective-permute-start | bytes 6488072 | tf_op jit(solution)/shard_map/ppermute | solution.py:473
  213.7 51.3 %collective-permute-start.2 = (bf16[3,176,2048]{2,1,0:T(8,128)(2,1)}, bf16[3,176,2048]{2,1,0:T(8,128)(2,1)S(1)}, u32[]{:S(2)}, u32[]{:S(2)}) collective-permute-start(bf16[3,176,2048]{2,1,0:T(8,128)(2,1)} %pad_maximum_fusion.refs_1_.refs_3_), channel_id=1, source_target_pairs={{0,1},{1,2},{2,3},{3,0},{4,5},{5,6},{6,7},{7,4},{8,9},{9,10},{10,1... | collective-permute-start | bytes 6488072 | tf_op jit(solution)/shard_map/ppermute | solution.py:473
  213.7 96.6 %collective-permute-start.5 = (bf16[3,176,2048]{2,1,0:T(8,128)(2,1)}, bf16[3,176,2048]{2,1,0:T(8,128)(2,1)}, u32[]{:S(2)}, u32[]{:S(2)}) collective-permute-start(bf16[3,176,2048]{2,1,0:T(8,128)(2,1)} %collective-permute-done.refs_3_.refs_5_), channel_id=1, source_target_pairs={{0,1},{1,2},{2,3},{3,0},{4,5},{5,6},{6,7},{7,4},{8,9},{9,10},{10,1... | collective-permute-start | bytes 6488072 | tf_op jit(solution)/shard_map/ppermute | solution.py:473
  213.7 96.6 %collective-permute-start.4 = (bf16[3,176,2048]{2,1,0:T(8,128)(2,1)}, bf16[3,176,2048]{2,1,0:T(8,128)(2,1)}, u32[]{:S(2)}, u32[]{:S(2)}) collective-permute-start(bf16[3,176,2048]{2,1,0:T(8,128)(2,1)} %collective-permute-done.1.refs_4_.refs_6_), channel_id=1, source_target_pairs={{0,3},{1,0},{2,1},{3,2},{4,7},{5,4},{6,5},{7,6},{8,11},{9,8},{10,9... | collective-permute-start | bytes 6488072 | tf_op jit(solution)/shard_map/ppermute | solution.py:473
  261.5 3.6 copy-start.16
  265.1 1.4 copy-start.17
  285.3 1.3 copy-start.4
  286.6 1.3 copy-start.5
  317.7 7.4 %copy-start.12 = (s32[4,128]{1,0:T(4,128)S(1)}, s32[4,128]{1,0:T(4,128)}, u32[]{:S(2)}) copy-start(s32[4,128]{1,0:T(4,128)} %get-tuple-element.54.route_other_ref) | copy-start | bytes 6148
  317.7 33.3 %all-to-all-start.1 = ((bf16[32,16,2048]{2,1,0:T(8,128)(2,1)}), bf16[32,16,2048]{2,1,0:T(8,128)(2,1)S(1)}, u32[]{:S(2)}, u32[]{:S(2)}) async-start(bf16[32,16,2048]{2,1,0:T(8,128)(2,1)} %bitcast.78), calls=%async_computation.1 | async-start | bytes 4194304 | tf_op jit(solution)/shard_map/all_to_all | solution.py:476
  327.0 8.3 %copy-start.11 = (s32[128,4]{0,1:T(4,128)S(1)}, s32[128,4]{0,1:T(4,128)}, u32[]{:S(2)}) copy-start(s32[128,4]{0,1:T(4,128)} %param.8) | copy-start | bytes 6148
  327.0 9.4 %copy-start.13 = (f32[128,4]{0,1:T(4,128)S(1)}, f32[128,4]{0,1:T(4,128)}, u32[]{:S(2)}) copy-start(f32[128,4]{0,1:T(4,128)} %param.9) | copy-start | bytes 6148
  335.3 27.0 %collective-permute-start.12 = (bf16[256,2048]{1,0:T(8,128)(2,1)}, bf16[256,2048]{1,0:T(8,128)(2,1)S(1)}, u32[]{:S(2)}, u32[]{:S(2)}) collective-permute-start(bf16[256,2048]{1,0:T(8,128)(2,1)} %get-tuple-element.27), channel_id=1, source_target_pairs={{0,2},{1,3},{2,0},{3,1},{4,6},{5,7},{6,4},{7,5},{8,10},{9,11},{10,... | collective-permute-start | bytes 3145736 | tf_op jit(solution)/shard_map/ppermute | solution.py:473
  337.9 24.4 %collective-permute-start.11 = (f32[8,128]{1,0:T(8,128)}, f32[8,128]{1,0:T(8,128)S(1)}, u32[]{:S(2)}, u32[]{:S(2)}) collective-permute-start(f32[8,128]{1,0:T(8,128)} %get-tuple-element.25), channel_id=1, source_target_pairs={{0,2},{1,3},{2,0},{3,1},{4,6},{5,7},{6,4},{7,5},{8,10},{9,11},{10,... | collective-permute-start | bytes 12296 | tf_op jit(solution)/shard_map/ppermute | solution.py:473
  362.3 0.6 copy-start.14
  362.3 1.0 copy-start.8

commit v6 on v5

--- a/solution.py
+++ b/solution.py
@@ -387,6 +387,16 @@
     lax.fori_loop(0, home.shape[1] // COLUMNS, block, 0)
 
 
+def combine_other_kernel(home, places, values, mix):
+    matrix = weighted_hot(places[...], values[...], home.shape[0])
+    mix[...] = jnp.dot(matrix, home[...], preferred_element_type=F32).astype(BF)
+
+
+def grads_other_kernel(home, places, grads, dw):
+    table = by_hidden(grads[...], home[...])
+    dw[...] = weight_grads(table, places[: grads.shape[0]])
+
+
 def combine_pair_kernel(home, places, values, grads, mix, dw, hot, table):
     toks = grads.shape[0]
     hot[...] = weighted_hot(places[...], values[...], home.shape[0])
@@ -420,6 +430,30 @@
 
     sweep(home, hot, grads, table, use)
     d_weights[...] = (weight_grads(table[...], places[:toks]) + dw_own[...] + dw_back[...])[:TOP]
+
+
+def combine_other(home, places, values):
+    return pl.pallas_call(
+        combine_other_kernel,
+        name="combine_other",
+        out_shape=jax.ShapeDtypeStruct((places.shape[0], home.shape[1]), BF),
+        compiler_params=room(60),
+        cost_estimate=pl.CostEstimate(
+            flops=2 * places.shape[0] * home.shape[0] * home.shape[1], transcendentals=0, bytes_accessed=6 * 1024 * 1024
+        ),
+    )(home, places, values)
+
+
+def grads_other_rows(home, places, grads):
+    return pl.pallas_call(
+        grads_other_kernel,
+        name="grads_other",
+        out_shape=jax.ShapeDtypeStruct((8, grads.shape[0]), F32),
+        compiler_params=room(60),
+        cost_estimate=pl.CostEstimate(
+            flops=2 * grads.shape[0] * home.shape[0] * home.shape[1], transcendentals=0, bytes_accessed=6 * 1024 * 1024
+        ),
+    )(home, places, grads)
 
 
 def combine_pair(home, places, values, grads, kind):
@@ -503,14 +537,7 @@
     own_rows = dispatch(dispatch_own_kernel, nodes * OWN_ROWS, route_t, tokens, grad_out)
     arrived = exchange(own_rows)
     other_rows = dispatch(
-        dispatch_other_kernel,
-        nodes * OTHER_ROWS,
-        route_t,
-        route_other,
-        tokens,
-        grad_out,
-        tokens_other,
-        grads_other,
+        dispatch_other_kernel, nodes * OTHER_ROWS, route_t, route_other, tokens, grad_out, tokens_other, grads_other
     )
     arrived_other = exchange(other_rows)
 
@@ -545,13 +572,12 @@
     places_other = stacked(other_place(8, 33), other_place(24, 35))
     places1 = stacked(full_place(0), full_place(8))
     values0, values_other = stacked(weight_t, weight_t), stacked(weight_other, weight_other)
-    back, dw_other = combine_pair(home0, places_other, values_other, grads_other, BF)
+    back = combine_other(home0, places_other, values_other)
     returned = send(back, across)
+    dw_other = grads_other_rows(home0, places_other, grads_other)
     dw_back = send(dw_other, across)
     kept, dw_own = combine_pair(home0, places0, values0, grad_out, F32)
-    combined, d_tokens, d_weights_t = combine_full(
-        home1, places1, values0, grad_out, kept, returned, dw_own, dw_back
-    )
+    combined, d_tokens, d_weights_t = combine_full(home1, places1, values0, grad_out, kept, returned, dw_own, dw_back)
     return combined, d_tokens, d_weights_t.T
 
 

time: 370 us -> 368 us (level)
  waiting for transfers between devices: 194 us -> 188 us
    pallas_call x0 -> x2, Pallas kernels: none -> 11.4 us  [the longest x1 5.9 us: combine_other(): pl.pallas_call(combine_other_kernel, name='combine_other', out_shape=jax....]
    pallas_call x2 -> x1, Pallas kernels: 16.6 us -> 8.31 us  [combine_pair(): pl.pallas_call(combine_pair_kernel, out_shape=(jax.ShapeDtypeStruct((2 *...]
    ppermute x13, waiting for transfers between devices: 161 us -> 157 us  [send(): return lax.ppermute(value, 'local', pairs)]
  transfers between devices with their start and end apart: 17 -> 17, of which waited for: 10 -> 9; matrix products, arithmetic and copies ran while one was open for 4% -> 4% of each run, Pallas kernels for 19% -> 20%
where the time goes in v6:
time: 368 us; the launch traced here: 367 us
  waiting for transfers between devices  188 us (51%)
  Pallas kernels  96.2 us (26%)
  starting transfers between devices  56.2 us (15%)
  local copies, waits for them, and re-layouts  19.2 us (5%)
  other arithmetic  5.71 us (2%)
    ppermute x13, waiting for transfers between devices, send(): return lax.ppermute(value, 'local', pairs)  157 us
    all_to_all x4, waiting for transfers between devices, exchange(): return lax.all_to_all(rows, 'node', split_axis=0, concat_axis=0, tiled=True)  31.3 us
    all_to_all x4, starting transfers between devices, exchange(): return lax.all_to_all(rows, 'node', split_axis=0, concat_axis=0, tiled=True)  30.3 us
    ppermute x13, starting transfers between devices, send(): return lax.ppermute(value, 'local', pairs)  25.8 us
    pallas_call x1, Pallas kernels, expert_pair(): pl.pallas_call(functools.partial(expert_pair_kernel, nodes, len(pieces)),...  21.1 us
    pallas_call x1, Pallas kernels, expert_near(): pl.pallas_call(functools.partial(expert_near_kernel, nodes, len(pieces)),...  18.8 us
    pallas_call x2, Pallas kernels, dispatch(): pl.pallas_call(kernel, grid=(steps,), out_shape=jax.ShapeDtypeStruct((row...  12.7 us
    unnamed x36, local copies, waits for them, and re-layouts  12 us
  transfers between devices with their start and end apart: 17, of which 9 were waited for; matrix products, arithmetic and copies ran while one was open for 4% of the time, Pallas kernels for 20%

profile of v6, /device:TPU:2, one launch (start us, length us, event | category | flops | bytes accessed | tf_op | source)
XLA Modules:
  0.0 366.9 jit_solution(14021142494029616704)
XLA Ops:
  0.6 4.0 %collective-permute-start.8 = (bf16[128,2048]{1,0:T(8,128)(2,1)}, bf16[128,2048]{1,0:T(8,128)(2,1)S(1)}, u32[]{:S(2)}, u32[]{:S(2)}) collective-permute-start(bf16[128,2048]{1,0:T(8,128)(2,1)} %grads_at.1), channel_id=1, source_target_pairs={{0,2},{1,3},{2,0},{3,1},{4,6},{5,7},{6,4},{7,5},{8,10},{9,11},{10,... | collective-permute-start | bytes 1572872 | tf_op jit(solution)/shard_map/ppermute | solution.py:507
  4.6 0.1 collective-permute-start.7
  4.7 0.7 bitcast_convert_fusion
  5.4 0.7 pad_maximum_fusion.5
  6.1 3.4 collective-permute-start.6
  9.5 18.6 %collective-permute-done.6 = f32[8,128]{1,0:T(8,128)S(1)} collective-permute-done((f32[8,128]{1,0:T(8,128)S(1)}, f32[8,128]{1,0:T(8,128)S(1)}, u32[]{:S(2)}, u32[]{:S(2)}) %collective-permute-start.6) | collective-permute-done | bytes 4128 | tf_op jit(solution)/shard_map/ppermute | solution.py:507
  28.0 0.6 slice_bitcast_fusion
  28.6 0.0 copy-start.10
  28.7 0.8 copy-done.8
  29.4 0.2 copy-done.10
  29.6 6.9 %shard_map.95 = bf16[768,2048]{1,0:T(8,128)(2,1)} custom-call(s32[4,128]{1,0:T(4,128)} %bitcast.81, s32[4,128]{1,0:T(4,128)} %get-tuple-element.50.route_other_ref, bf16[128,2048]{1,0:T(8,128)(2,1)} %tokens.3, bf16[128,2048]{1,0:T(8,128)(2,1)} %grads_at.1, bf16[128,2048]{1,0:T(8,128)(2,1)} %copy-done.10, bf16[128,2048]{1,0:T(8,128)(2,1)} %copy-done.8), custom_call_target="tpu_custom_call" | custom-call | flops 805306368 | bytes 6291456 | tf_op jit(solution)/shard_map/pallas_call | solution.py:88
  36.5 7.6 %all-to-all-start.2 = ((bf16[32,24,2048]{2,1,0:T(8,128)(2,1)}), bf16[32,24,2048]{2,1,0:T(8,128)(2,1)S(1)}, u32[]{:S(2)}, u32[]{:S(2)}) async-start(bf16[32,24,2048]{2,1,0:T(8,128)(2,1)} %bitcast.77), calls=%async_computation.2 | async-start | bytes 6291456 | tf_op jit(solution)/shard_map/all_to_all | solution.py:510
  44.2 5.8 %shard_map.94 = bf16[1024,2048]{1,0:T(8,128)(2,1)} custom-call(s32[4,128]{1,0:T(4,128)} %bitcast.82, bf16[128,2048]{1,0:T(8,128)(2,1)} %tokens.3, bf16[128,2048]{1,0:T(8,128)(2,1)} %grads_at.1), custom_call_target="tpu_custom_call" | custom-call | flops 1073741824 | bytes 8388608 | tf_op jit(solution)/shard_map/pallas_call | solution.py:88
  50.0 31.3 %all-to-all-done.2 = bf16[32,24,2048]{2,1,0:T(8,128)(2,1)S(1)} async-done(((bf16[32,24,2048]{2,1,0:T(8,128)(2,1)}), bf16[32,24,2048]{2,1,0:T(8,128)(2,1)S(1)}, u32[]{:S(2)}, u32[]{:S(2)}) %all-to-all-start.2) | async-done | bytes 3145760 | tf_op jit(solution)/shard_map/all_to_all | solution.py:510
  81.2 7.8 %all-to-all-start = ((bf16[32,32,2048]{2,1,0:T(8,128)(2,1)}), bf16[32,32,2048]{2,1,0:T(8,128)(2,1)}, u32[]{:S(2)}, u32[]{:S(2)}) async-start(bf16[32,32,2048]{2,1,0:T(8,128)(2,1)} %bitcast.76), calls=%async_computation | async-start | bytes 8388608 | tf_op jit(solution)/shard_map/all_to_all | solution.py:510
  89.1 0.0 copy-start.6
  89.1 0.0 copy-start.7
  89.1 2.1 fusion.27
  91.2 0.5 copy-done.6
  91.7 0.9 copy-done.7
  92.6 1.0 fusion.25
  93.6 0.2 pad_maximum_fusion.3.refs_3_
  93.9 1.4 collective-permute-start.10
  95.2 0.2 pad_maximum_fusion.2.refs_2_
  95.5 3.2 collective-permute-start.9
  98.7 1.6 pad_maximum_fusion.1.refs_2_.refs_4_
  100.3 1.6 pad_maximum_fusion.refs_1_.refs_3_
  101.9 3.2 collective-permute-start.1
  105.1 40.1 %collective-permute-done.10.refs_5_ = bf16[3,176,2048]{2,1,0:T(8,128)(2,1)S(1)} collective-permute-done((bf16[3,176,2048]{2,1,0:T(8,128)(2,1)S(1)}, bf16[3,176,2048]{2,1,0:T(8,128)(2,1)S(1)}, u32[]{:S(2)}, u32[]{:S(2)}) %collective-permute-start.10) | collective-permute-done | bytes 2162720 | tf_op jit(solution)/shard_map/ppermute | solution.py:507
  145.2 1.4 copy-done.15
  146.6 1.6 copy-done.1
  148.2 1.6 copy-done.3
  149.8 21.1 %expert_pair.1 = (bf16[1280,2048]{1,0:T(8,128)(2,1)}, bf16[64,2048]{1,0:T(8,128)(2,1)S(1)}, bf16[64,2048]{1,0:T(8,128)(2,1)S(1)}) custom-call(bf16[1024,2048]{1,0:T(8,128)(2,1)} %bitcast.2.refs_0_, bf16[768,2048]{1,0:T(8,128)(2,1)S(1)} %bitcast.72, bf16[3,176,2048]{2,1,0:T(8,128)(2,1)S(1)} %copy-done.3, bf16[3,176,2048]{2,1,0:T(8,128)(2,1)S(1)} %copy-done.1, ...), custom_call_target="tpu_custom_call" | custom-call | flops 9965666304 | bytes 18087936 | tf_op jit(solution)/shard_map/expert_pair/pallas_call | solution.py:292
  170.9 20.2 %collective-permute-done.refs_3_.refs_5_ = bf16[3,176,2048]{2,1,0:T(8,128)(2,1)} collective-permute-done((bf16[3,176,2048]{2,1,0:T(8,128)(2,1)}, bf16[3,176,2048]{2,1,0:T(8,128)(2,1)}, u32[]{:S(2)}, u32[]{:S(2)}) %collective-permute-start) | collective-permute-done | bytes 2162720 | tf_op jit(solution)/shard_map/ppermute | solution.py:507
  191.1 0.6 collective-permute-done.1.refs_4_.refs_6_
  191.7 10.8 %expert_ninth.1 = bf16[1280,2048]{1,0:T(8,128)(2,1)} custom-call(bf16[768,2048]{1,0:T(8,128)(2,1)S(1)} %bitcast.73, bf16[64,2048]{1,0:T(8,128)(2,1)S(1)} %get-tuple-element.19.refs_1_, bf16[64,2048]{1,0:T(8,128)(2,1)S(1)} %get-tuple-element.20.refs_2_, bf16[3,176,2048]{2,1,0:T(8,128)(2,1)} %pad_maximum_fusion.refs_1_.refs_3_, ...), custom_call_target="tpu_custom_call", output_to_operand_aliasing={{}: (7, {})} | custom-call | flops 1107296256 | bytes 9699328 | tf_op jit(solution)/shard_map/expert_ninth/pallas_call | solution.py:309
  202.5 7.5 %all-to-all-start.3 = ((bf16[32,40,2048]{2,1,0:T(8,128)(2,1)}), bf16[32,40,2048]{2,1,0:T(8,128)(2,1)}, u32[]{:S(2)}, u32[]{:S(2)}) async-start(bf16[32,40,2048]{2,1,0:T(8,128)(2,1)} %bitcast.75), calls=%async_computation.3 | async-start | bytes 10485760 | tf_op jit(solution)/shard_map/all_to_all | solution.py:510
  210.0 3.8 %collective-permute-start.3 = (bf16[3,176,2048]{2,1,0:T(8,128)(2,1)}, bf16[3,176,2048]{2,1,0:T(8,128)(2,1)S(1)}, u32[]{:S(2)}, u32[]{:S(2)}) collective-permute-start(bf16[3,176,2048]{2,1,0:T(8,128)(2,1)} %pad_maximum_fusion.1.refs_2_.refs_4_), channel_id=1, source_target_pairs={{0,3},{1,0},{2,1},{3,2},{4,7},{5,4},{6,5},{7,6},{8,11},{9,8},{10,9... | collective-permute-start | bytes 6488072 | tf_op jit(solution)/shard_map/ppermute | solution.py:507
  213.8 3.3 collective-permute-start.4
  217.1 44.5 %collective-permute-done.3.refs_6_ = bf16[3,176,2048]{2,1,0:T(8,128)(2,1)S(1)} collective-permute-done((bf16[3,176,2048]{2,1,0:T(8,128)(2,1)}, bf16[3,176,2048]{2,1,0:T(8,128)(2,1)S(1)}, u32[]{:S(2)}, u32[]{:S(2)}) %collective-permute-start.3) | collective-permute-done | bytes 2162720 | tf_op jit(solution)/shard_map/ppermute | solution.py:507
  261.5 3.6 collective-permute-done.2.refs_5_
  265.1 1.4 copy-done.17
  266.6 18.8 %expert_near.1 = (f32[256,2048]{1,0:T(8,128)S(1)}, f32[256,2048]{1,0:T(8,128)S(1)}, bf16[256,2048]{1,0:T(8,128)(2,1)S(1)}, bf16[256,2048]{1,0:T(8,128)(2,1)S(1)}) custom-call(bf16[1024,2048]{1,0:T(8,128)(2,1)} %bitcast.2.refs_0_, bf16[3,176,2048]{2,1,0:T(8,128)(2,1)} %pad_maximum_fusion.refs_1_.refs_3_, ...), custom_call_target="tpu_custom_call" | custom-call | flops 6643777536 | bytes 17170432 | tf_op jit(solution)/shard_map/expert_near/pallas_call | solution.py:325
  285.4 1.3 copy-done.4
  286.7 1.3 copy-done.5
  288.0 22.4 %collective-permute-done.5.refs_5_ = bf16[3,176,2048]{2,1,0:T(8,128)(2,1)} collective-permute-done((bf16[3,176,2048]{2,1,0:T(8,128)(2,1)}, bf16[3,176,2048]{2,1,0:T(8,128)(2,1)}, u32[]{:S(2)}, u32[]{:S(2)}) %collective-permute-start.5) | collective-permute-done | bytes 2162720 | tf_op jit(solution)/shard_map/ppermute | solution.py:507
  310.4 7.3 %expert_far.1 = bf16[512,2048]{1,0:T(8,128)(2,1)} custom-call(bf16[256,2048]{1,0:T(8,128)(2,1)S(1)} %get-tuple-element.15.refs_0_, bf16[256,2048]{1,0:T(8,128)(2,1)S(1)} %get-tuple-element.16.refs_1_, f32[256,2048]{1,0:T(8,128)} %copy-done.4, f32[256,2048]{1,0:T(8,128)} %copy-done.5, bf16[3,176,2048]{2,1,0:T(8,128)(2,1)} %collective-permute-done.4.refs_4_, ...), custom_call_target="tpu_custom_call" | custom-call | flops 2214592512 | bytes 8519680 | tf_op jit(solution)/shard_map/expert_far/pallas_call | solution.py:342
  317.8 0.0 copy-start.12
  317.8 7.4 %all-to-all-start.1 = ((bf16[32,16,2048]{2,1,0:T(8,128)(2,1)}), bf16[32,16,2048]{2,1,0:T(8,128)(2,1)S(1)}, u32[]{:S(2)}, u32[]{:S(2)}) async-start(bf16[32,16,2048]{2,1,0:T(8,128)(2,1)} %bitcast.78), calls=%async_computation.1 | async-start | bytes 4194304 | tf_op jit(solution)/shard_map/all_to_all | solution.py:510
  325.3 0.2 select_reduce_fusion.3
  325.5 0.8 copy.43.places
  326.3 0.8 copy.45.values
  327.1 5.9 %combine_other.1 = bf16[256,2048]{1,0:T(8,128)(2,1)} custom-call(bf16[1280,2048]{1,0:T(8,128)(2,1)} %bitcast.21.home, s32[256,4]{1,0:T(8,128)} %copy.43.places, f32[256,4]{1,0:T(8,128)} %copy.45.values), custom_call_target="tpu_custom_call" | custom-call | flops 1342177280 | bytes 6291456 | tf_op jit(solution)/shard_map/combine_other/pallas_call | solution.py:436
  333.0 0.2 select_reduce_fusion.7
  333.2 0.8 copy.41.places
  334.0 0.8 copy.47.values
  334.8 0.8 copy.46.places
  335.6 5.5 %grads_other.1 = f32[8,128]{1,0:T(8,128)} custom-call(bf16[1280,2048]{1,0:T(8,128)(2,1)} %bitcast.21.home, s32[256,4]{1,0:T(8,128)} %copy.43.places, bf16[128,2048]{1,0:T(8,128)(2,1)} %copy-done.8), custom_call_target="tpu_custom_call" | custom-call | flops 671088640 | bytes 6291456 | tf_op jit(solution)/shard_map/grads_other/pallas_call | solution.py:448
  341.1 3.5 collective-permute-start.11
  344.6 8.3 %shard_map.96 = (f32[256,2048]{1,0:T(8,128)}, f32[8,128]{1,0:T(8,128)}) custom-call(bf16[1280,2048]{1,0:T(8,128)(2,1)} %bitcast.21.home, s32[256,4]{1,0:T(8,128)} %copy.41.places, f32[256,4]{1,0:T(8,128)} %copy.47.values, bf16[128,2048]{1,0:T(8,128)(2,1)} %grads_at.1), custom_call_target="tpu_custom_call" | custom-call | flops 2013265920 | bytes 8388608 | tf_op jit(solution)/shard_map/pallas_call | solution.py:461
  352.9 7.0 %collective-permute-done.11.dw_back = f32[8,128]{1,0:T(8,128)S(1)} collective-permute-done((f32[8,128]{1,0:T(8,128)}, f32[8,128]{1,0:T(8,128)S(1)}, u32[]{:S(2)}, u32[]{:S(2)}) %collective-permute-start.11) | collective-permute-done | bytes 4128 | tf_op jit(solution)/shard_map/ppermute | solution.py:507
  360.0 0.6 copy-done.14
  360.5 0.4 copy-done.9
  361.0 5.7 %combine_full.1 = (bf16[128,2048]{1,0:T(8,128)(2,1)}, bf16[128,2048]{1,0:T(8,128)(2,1)}, f32[4,128]{1,0:T(4,128)}) custom-call(bf16[512,2048]{1,0:T(8,128)(2,1)S(1)} %bitcast.74, s32[256,4]{1,0:T(8,128)} %copy.46.places, f32[256,4]{1,0:T(8,128)} %copy.47.values, f32[8,128]{1,0:T(8,128)} %get-tuple-element.22.dw_own, f32[8,128]{1,0:T(8,128)} %copy-done.14, ...), custom_call_target="tpu_custom_call" | custom-call | flops 805306368 | bytes 8388608 | tf_op jit(solution)/shard_map/combine_full/pallas_call | solution.py:474
  (41 shorter events, 0.1 us)
Async XLA Ops:
  0.6 28.0 %collective-permute-start.8 = (bf16[128,2048]{1,0:T(8,128)(2,1)}, bf16[128,2048]{1,0:T(8,128)(2,1)S(1)}, u32[]{:S(2)}, u32[]{:S(2)}) collective-permute-start(bf16[128,2048]{1,0:T(8,128)(2,1)} %grads_at.1), channel_id=1, source_target_pairs={{0,2},{1,3},{2,0},{3,1},{4,6},{5,7},{6,4},{7,5},{8,10},{9,11},{10,... | collective-permute-start | bytes 1572872 | tf_op jit(solution)/shard_map/ppermute | solution.py:507
  4.6 24.1 %collective-permute-start.7 = (bf16[128,2048]{1,0:T(8,128)(2,1)}, bf16[128,2048]{1,0:T(8,128)(2,1)S(1)}, u32[]{:S(2)}, u32[]{:S(2)}) collective-permute-start(bf16[128,2048]{1,0:T(8,128)(2,1)} %tokens.3), channel_id=1, source_target_pairs={{0,2},{1,3},{2,0},{3,1},{4,6},{5,7},{6,4},{7,5},{8,10},{9,11},{10,... | collective-permute-start | bytes 1572872 | tf_op jit(solution)/shard_map/ppermute | solution.py:507
  6.1 22.0 %collective-permute-start.6 = (f32[8,128]{1,0:T(8,128)S(1)}, f32[8,128]{1,0:T(8,128)S(1)}, u32[]{:S(2)}, u32[]{:S(2)}) collective-permute-start(f32[8,128]{1,0:T(8,128)S(1)} %pad_maximum_fusion.5), channel_id=1, source_target_pairs={{0,2},{1,3},{2,0},{3,1},{4,6},{5,7},{6,4},{7,5},{8,10},{9,11},{10,... | collective-permute-start | bytes 12296 | tf_op jit(solution)/shard_map/ppermute | solution.py:507
  28.6 0.8 copy-start.8
  28.6 1.0 copy-start.10
  36.5 44.7 %all-to-all-start.2 = ((bf16[32,24,2048]{2,1,0:T(8,128)(2,1)}), bf16[32,24,2048]{2,1,0:T(8,128)(2,1)S(1)}, u32[]{:S(2)}, u32[]{:S(2)}) async-start(bf16[32,24,2048]{2,1,0:T(8,128)(2,1)} %bitcast.77), calls=%async_computation.2 | async-start | bytes 6291456 | tf_op jit(solution)/shard_map/all_to_all | solution.py:510
  81.2 65.3 %all-to-all-start = ((bf16[32,32,2048]{2,1,0:T(8,128)(2,1)}), bf16[32,32,2048]{2,1,0:T(8,128)(2,1)}, u32[]{:S(2)}, u32[]{:S(2)}) async-start(bf16[32,32,2048]{2,1,0:T(8,128)(2,1)} %bitcast.76), calls=%async_computation | async-start | bytes 8388608 | tf_op jit(solution)/shard_map/all_to_all | solution.py:510
  89.1 2.7 copy-start.6
  89.1 3.5 copy-start.7
  93.8 1.6 copy-start
  93.9 51.4 %collective-permute-start.10 = (bf16[3,176,2048]{2,1,0:T(8,128)(2,1)S(1)}, bf16[3,176,2048]{2,1,0:T(8,128)(2,1)S(1)}, u32[]{:S(2)}, u32[]{:S(2)}) collective-permute-start(bf16[3,176,2048]{2,1,0:T(8,128)(2,1)S(1)} %pad_maximum_fusion.3.refs_3_), channel_id=1, source_target_pairs={{0,1},{1,2},{2,3},{3,0},{4,5},{5,6},{6,7},{7,4},{8,9},{9,10},{10,1... | collective-permute-start | bytes 6488072 | tf_op jit(solution)/shard_map/ppermute | solution.py:507
  95.5 4.8 %copy-start.2 = (bf16[3,176,2048]{2,1,0:T(8,128)(2,1)}, bf16[3,176,2048]{2,1,0:T(8,128)(2,1)S(1)}, u32[]{:S(2)}) copy-start(bf16[3,176,2048]{2,1,0:T(8,128)(2,1)S(1)} %pad_maximum_fusion.2.refs_2_) | copy-start | bytes 6488068
  95.5 51.1 %collective-permute-start.9 = (bf16[3,176,2048]{2,1,0:T(8,128)(2,1)S(1)}, bf16[3,176,2048]{2,1,0:T(8,128)(2,1)}, u32[]{:S(2)}, u32[]{:S(2)}) collective-permute-start(bf16[3,176,2048]{2,1,0:T(8,128)(2,1)S(1)} %pad_maximum_fusion.2.refs_2_), channel_id=1, source_target_pairs={{0,3},{1,0},{2,1},{3,2},{4,7},{5,4},{6,5},{7,6},{8,11},{9,8},{10,9... | collective-permute-start | bytes 6488072 | tf_op jit(solution)/shard_map/ppermute | solution.py:507
  100.3 90.8 %collective-permute-start = (bf16[3,176,2048]{2,1,0:T(8,128)(2,1)}, bf16[3,176,2048]{2,1,0:T(8,128)(2,1)}, u32[]{:S(2)}, u32[]{:S(2)}) collective-permute-start(bf16[3,176,2048]{2,1,0:T(8,128)(2,1)} %pad_maximum_fusion.1.refs_2_.refs_4_), channel_id=1, source_target_pairs={{0,1},{1,2},{2,3},{3,0},{4,5},{5,6},{6,7},{7,4},{8,9},{9,10},{10,1... | collective-permute-start | bytes 6488072 | tf_op jit(solution)/shard_map/ppermute | solution.py:507
  101.9 89.8 %collective-permute-start.1 = (bf16[3,176,2048]{2,1,0:T(8,128)(2,1)}, bf16[3,176,2048]{2,1,0:T(8,128)(2,1)}, u32[]{:S(2)}, u32[]{:S(2)}) collective-permute-start(bf16[3,176,2048]{2,1,0:T(8,128)(2,1)} %pad_maximum_fusion.refs_1_.refs_3_), channel_id=1, source_target_pairs={{0,3},{1,0},{2,1},{3,2},{4,7},{5,4},{6,5},{7,6},{8,11},{9,8},{10,9... | collective-permute-start | bytes 6488072 | tf_op jit(solution)/shard_map/ppermute | solution.py:507
  145.2 1.4 copy-start.15
  146.6 1.6 copy-start.1
  148.2 1.6 copy-start.3
  202.5 115.3 %all-to-all-start.3 = ((bf16[32,40,2048]{2,1,0:T(8,128)(2,1)}), bf16[32,40,2048]{2,1,0:T(8,128)(2,1)}, u32[]{:S(2)}, u32[]{:S(2)}) async-start(bf16[32,40,2048]{2,1,0:T(8,128)(2,1)} %bitcast.75), calls=%async_computation.3 | async-start | bytes 10485760 | tf_op jit(solution)/shard_map/all_to_all | solution.py:510
  210.0 51.5 %collective-permute-start.3 = (bf16[3,176,2048]{2,1,0:T(8,128)(2,1)}, bf16[3,176,2048]{2,1,0:T(8,128)(2,1)S(1)}, u32[]{:S(2)}, u32[]{:S(2)}) collective-permute-start(bf16[3,176,2048]{2,1,0:T(8,128)(2,1)} %pad_maximum_fusion.1.refs_2_.refs_4_), channel_id=1, source_target_pairs={{0,3},{1,0},{2,1},{3,2},{4,7},{5,4},{6,5},{7,6},{8,11},{9,8},{10,9... | collective-permute-start | bytes 6488072 | tf_op jit(solution)/shard_map/ppermute | solution.py:507
  213.8 51.3 %collective-permute-start.2 = (bf16[3,176,2048]{2,1,0:T(8,128)(2,1)}, bf16[3,176,2048]{2,1,0:T(8,128)(2,1)S(1)}, u32[]{:S(2)}, u32[]{:S(2)}) collective-permute-start(bf16[3,176,2048]{2,1,0:T(8,128)(2,1)} %pad_maximum_fusion.refs_1_.refs_3_), channel_id=1, source_target_pairs={{0,1},{1,2},{2,3},{3,0},{4,5},{5,6},{6,7},{7,4},{8,9},{9,10},{10,1... | collective-permute-start | bytes 6488072 | tf_op jit(solution)/shard_map/ppermute | solution.py:507
  213.8 96.6 %collective-permute-start.5 = (bf16[3,176,2048]{2,1,0:T(8,128)(2,1)}, bf16[3,176,2048]{2,1,0:T(8,128)(2,1)}, u32[]{:S(2)}, u32[]{:S(2)}) collective-permute-start(bf16[3,176,2048]{2,1,0:T(8,128)(2,1)} %collective-permute-done.refs_3_.refs_5_), channel_id=1, source_target_pairs={{0,1},{1,2},{2,3},{3,0},{4,5},{5,6},{6,7},{7,4},{8,9},{9,10},{10,1... | collective-permute-start | bytes 6488072 | tf_op jit(solution)/shard_map/ppermute | solution.py:507
  213.8 96.6 %collective-permute-start.4 = (bf16[3,176,2048]{2,1,0:T(8,128)(2,1)}, bf16[3,176,2048]{2,1,0:T(8,128)(2,1)}, u32[]{:S(2)}, u32[]{:S(2)}) collective-permute-start(bf16[3,176,2048]{2,1,0:T(8,128)(2,1)} %collective-permute-done.1.refs_4_.refs_6_), channel_id=1, source_target_pairs={{0,3},{1,0},{2,1},{3,2},{4,7},{5,4},{6,5},{7,6},{8,11},{9,8},{10,9... | collective-permute-start | bytes 6488072 | tf_op jit(solution)/shard_map/ppermute | solution.py:507
  261.5 3.6 copy-start.16
  265.1 1.4 copy-start.17
  285.4 1.3 copy-start.4
  286.7 1.3 copy-start.5
  317.8 7.4 %copy-start.12 = (s32[4,128]{1,0:T(4,128)S(1)}, s32[4,128]{1,0:T(4,128)}, u32[]{:S(2)}) copy-start(s32[4,128]{1,0:T(4,128)} %get-tuple-element.50.route_other_ref) | copy-start | bytes 6148
  317.8 35.1 %all-to-all-start.1 = ((bf16[32,16,2048]{2,1,0:T(8,128)(2,1)}), bf16[32,16,2048]{2,1,0:T(8,128)(2,1)S(1)}, u32[]{:S(2)}, u32[]{:S(2)}) async-start(bf16[32,16,2048]{2,1,0:T(8,128)(2,1)} %bitcast.78), calls=%async_computation.1 | async-start | bytes 4194304 | tf_op jit(solution)/shard_map/all_to_all | solution.py:510
  327.1 5.9 %copy-start.11 = (s32[128,4]{0,1:T(4,128)S(1)}, s32[128,4]{0,1:T(4,128)}, u32[]{:S(2)}) copy-start(s32[128,4]{0,1:T(4,128)} %param.8) | copy-start | bytes 6148
  327.1 6.9 %copy-start.13 = (f32[128,4]{0,1:T(4,128)S(1)}, f32[128,4]{0,1:T(4,128)}, u32[]{:S(2)}) copy-start(f32[128,4]{0,1:T(4,128)} %param.9) | copy-start | bytes 6148
  333.0 27.0 %collective-permute-start.12 = (bf16[256,2048]{1,0:T(8,128)(2,1)}, bf16[256,2048]{1,0:T(8,128)(2,1)S(1)}, u32[]{:S(2)}, u32[]{:S(2)}) collective-permute-start(bf16[256,2048]{1,0:T(8,128)(2,1)} %combine_other.1), channel_id=1, source_target_pairs={{0,2},{1,3},{2,0},{3,1},{4,6},{5,7},{6,4},{7,5},{8,10},{9,11},{10,... | collective-permute-start | bytes 3145736 | tf_op jit(solution)/shard_map/ppermute | solution.py:507
  341.1 18.8 %collective-permute-start.11 = (f32[8,128]{1,0:T(8,128)}, f32[8,128]{1,0:T(8,128)S(1)}, u32[]{:S(2)}, u32[]{:S(2)}) collective-permute-start(f32[8,128]{1,0:T(8,128)} %grads_other.1), channel_id=1, source_target_pairs={{0,2},{1,3},{2,0},{3,1},{4,6},{5,7},{6,4},{7,5},{8,10},{9,11},{10,... | collective-permute-start | bytes 12296 | tf_op jit(solution)/shard_map/ppermute | solution.py:507
  360.0 0.6 copy-start.14
  360.0 1.0 copy-start.9
